TPU v7x, 32 devices: a whole 2x2x4 slice. The times are simulated.
32 devices in a mesh: expert: 8 (over z, core), shard: 4 (over y, x).
Axes of the slice: x: 2, y: 2, z: 4, core: 2. Of those that a mesh axis runs over, the one named last changes fastest.
Arguments:
- inputs: float32 [16384, 768], P(('expert', 'shard')), may hold values from -6 to 6
- cotangent: float32 [16384, 768], P(('expert', 'shard')), may hold values from -6 to 6
- norm_one: bfloat16 [768], P('shard'), may hold values from 0.5 to 1.5
- qkv_weight: bfloat16 [768, 2304], P('shard'), may hold values from -0.21875 to 0.21875
- out_weight: bfloat16 [768, 768], P('shard'), may hold values from -3.5 to 3.5
- norm_two: bfloat16 [768], P('shard'), may hold values from 0.5 to 1.5
- shared_gate: bfloat16 [768, 2048], P(None, 'shard'), may hold values from -0.21875 to 0.21875
- shared_up: bfloat16 [768, 2048], P(None, 'shard'), may hold values from -0.21875 to 0.21875
- shared_down: bfloat16 [2048, 768], P('shard'), may hold values from -0.125 to 0.125
- expert_gate: bfloat16 [8, 768, 2048], P('expert'), may hold values from -0.21875 to 0.21875
- expert_up: bfloat16 [8, 768, 2048], P('expert'), may hold values from -0.21875 to 0.21875
- expert_down: bfloat16 [8, 2048, 768], P('expert'), may hold values from -0.125 to 0.125
- gate_weights: float32 [16384, 2], P(('expert', 'shard')), may hold values from 0.25 to 1
- routes: int32 [16384, 2], P(('expert', 'shard')), may hold values from 0 to 7, all different within a row; in each aligned block of 512 rows (0 to 511, 512 to 1023, ...) at most 256 rows name the same one
- prefix: int32 [32], P(('expert', 'shard')), may hold values from 51 to 256
Outputs:
- output: float32 [16384, 768], P(('expert', 'shard'))
- input_grad: float32 [16384, 768], P(('expert', 'shard'))
- norm_one_grad: float32 [768], P('shard')
- qkv_grad: float32 [768, 2304], P('shard')
- out_grad: float32 [768, 768], P('shard')
- norm_two_grad: float32 [768], P('shard')
- shared_gate_grad: float32 [768, 2048], P(None, 'shard')
- shared_up_grad: float32 [768, 2048], P(None, 'shard')
- shared_down_grad: float32 [2048, 768], P('shard')
- expert_gate_grad: float32 [8, 768, 2048], P('expert', None, 'shard')
- expert_up_grad: float32 [8, 768, 2048], P('expert', None, 'shard')
- expert_down_grad: float32 [8, 2048, 768], P('expert', 'shard')
- gate_weights_grad: float32 [16384, 2], P(('expert', 'shard'))
Inputs may be any that keep to these rules, and one draw needn't show every extreme that they name: `routes`: each row names 2 different experts. Among the 512 rows of one device no expert is named more than 256 times, and some device names some expert exactly 256 times. `prefix`: leading tokens of a sequence that all its tokens attend to.
All inputs are finite; a program needn't handle non-finite values.
Results may differ from a plain program's by a relative error of at most 0.02.
Values may be sent and summed in bfloat16 or wider, within the bound.
A program may use at most 256 MiB of HBM per device.

v0:
```python
import jax
import jax.numpy as jnp
from jax import lax
from jax.sharding import PartitionSpec as P

HEADS = 12
HEAD_DIM = 64
TOP = 2


EPS = 1e-06


def rope_tables(length):
    half_dim = HEAD_DIM // 2
    frequency = 10000.0 ** (-jnp.arange(half_dim, dtype=jnp.float32) * 2.0 / HEAD_DIM)
    angles = jnp.arange(length, dtype=jnp.float32)[:, None] * frequency[None, :]
    return (jnp.cos(angles)[:, None, :], jnp.sin(angles)[:, None, :])


def rotate(vectors, cosine_table, sine_table):
    half_dim = vectors.shape[-1] // 2
    first_half = vectors[..., :half_dim]
    second = vectors[..., half_dim:]
    return jnp.concatenate(
        [
            first_half * cosine_table - second * sine_table,
            second * cosine_table + first_half * sine_table,
        ],
        axis=-1,
    )


def gated_unit(pre_gate):
    sigmoid_value = jax.nn.sigmoid(pre_gate)
    activated = pre_gate * sigmoid_value
    derivative = sigmoid_value * (1.0 + pre_gate * (1.0 - sigmoid_value))
    return (activated, derivative)


def norm_back(source, inverse, gain, grad_in):
    scaled = grad_in * gain
    gain_grad = jnp.sum(grad_in * source * inverse, axis=0)
    input_part = inverse * scaled - source * inverse**3 * jnp.mean(
        scaled * source, axis=-1, keepdims=True
    )
    return (gain_grad, input_part)


def matmul(left, right):
    return jnp.dot(left, right, preferred_element_type=jnp.float32)


def on_device(
    inputs,
    cotangent,
    norm_one,
    qkv_weight,
    out_weight,
    norm_two,
    shared_gate,
    shared_up,
    shared_down,
    expert_gate,
    expert_up,
    expert_down,
    gate_weights,
    routes,
    prefix,
):
    length, model_width = inputs.shape
    qkv_full, out_full, gain_one = (
        lax.all_gather(qkv_weight, "shard", axis=0, tiled=True),
        lax.all_gather(out_weight, "shard", axis=0, tiled=True),
        lax.all_gather(norm_one, "shard", axis=0, tiled=True),
    )
    gate_full, up_full, down_full, gain_two = (
        lax.all_gather(shared_gate, "shard", axis=1, tiled=True),
        lax.all_gather(shared_up, "shard", axis=1, tiled=True),
        lax.all_gather(shared_down, "shard", axis=0, tiled=True),
        lax.all_gather(norm_two, "shard", axis=0, tiled=True),
    )
    gain_one = gain_one.astype(jnp.float32)
    gain_two = gain_two.astype(jnp.float32)
    inverse_one = lax.rsqrt(jnp.mean(inputs * inputs, axis=-1, keepdims=True) + EPS)
    normed_one = (inputs * inverse_one * gain_one).astype(jnp.bfloat16)
    projected = matmul(normed_one, qkv_full)
    cosine_table, sine_table = rope_tables(length)
    head_shape = (length, HEADS, HEAD_DIM)
    queries = rotate(
        projected[:, :model_width].reshape(head_shape), cosine_table, sine_table
    ).astype(jnp.bfloat16)
    key_rows = rotate(
        projected[:, model_width : 2 * model_width].reshape(head_shape), cosine_table, sine_table
    ).astype(jnp.bfloat16)
    value_rows = projected[:, 2 * model_width :].reshape(head_shape).astype(jnp.bfloat16)
    score_scale = HEAD_DIM ** (-0.5)
    row_pos = lax.broadcasted_iota(jnp.int32, (length, length), 0)
    col_pos = lax.broadcasted_iota(jnp.int32, (length, length), 1)
    visible = (col_pos < prefix[0]) | (col_pos <= row_pos)

    def masked_scores():
        raw_scores = (
            jnp.einsum("qhd,khd->hqk", queries, key_rows, preferred_element_type=jnp.float32)
            * score_scale
        )
        return jnp.where(visible[None], raw_scores, -1e30)

    scores = masked_scores()
    row_peak = jnp.max(scores, axis=-1, keepdims=True)
    exponent = jnp.exp(scores - row_peak)
    expsum = jnp.sum(exponent, axis=-1, keepdims=True)
    logsum = row_peak + jnp.log(expsum)
    probs_low = (exponent / expsum).astype(jnp.bfloat16)
    attended = (
        jnp.einsum("hqk,khd->qhd", probs_low, value_rows, preferred_element_type=jnp.float32)
        .reshape(length, model_width)
        .astype(jnp.bfloat16)
    )
    resid = inputs + matmul(attended, out_full)
    inverse_two = lax.rsqrt(jnp.mean(resid * resid, axis=-1, keepdims=True) + EPS)
    normed_two = (resid * inverse_two * gain_two).astype(jnp.bfloat16)
    shared_pre = matmul(normed_two, gate_full)
    shared_lift = matmul(normed_two, up_full)
    shared_act, shared_slope = gated_unit(shared_pre)
    shared_hidden = (shared_act * shared_lift).astype(jnp.bfloat16)
    shared_out = matmul(shared_hidden, down_full)
    experts = lax.axis_size("expert") * expert_gate.shape[0]
    capacity = 4 * length // experts
    copies = length * TOP
    flat_route = routes.reshape(copies)
    onehot = (flat_route[:, None] == jnp.arange(experts, dtype=jnp.int32)[None, :]).astype(
        jnp.int32
    )
    slot_index = jnp.sum((jnp.cumsum(onehot, axis=0) - onehot) * onehot, axis=1)
    position = flat_route * capacity + slot_index
    source = (
        jnp.full((experts * capacity,), copies, jnp.int32)
        .at[position]
        .set(jnp.arange(copies, dtype=jnp.int32))
    )
    token_index = jnp.where(source < copies, source // TOP, length)
    copy_index = jnp.where(source < copies, source, copies)

    def place_rows(row_block, index):
        padded = jnp.concatenate([row_block, jnp.zeros((1, model_width), row_block.dtype)], axis=0)
        return padded[index].reshape(experts, capacity, model_width)

    dispatched = place_rows(normed_two, token_index)
    gate_local = expert_gate[0]
    up_local = expert_up[0]
    down_local = expert_down[0]
    received = lax.all_to_all(dispatched, "expert", split_axis=0, concat_axis=0, tiled=True)
    row_count = received.shape[0] * received.shape[1]
    row_block = received.reshape(row_count, model_width)
    pre_gate = matmul(row_block, gate_local)
    pre_up = matmul(row_block, up_local)
    activated, unused_slope = gated_unit(pre_gate)
    hidden = (activated * pre_up).astype(jnp.bfloat16)
    result = matmul(hidden, down_local).astype(jnp.bfloat16).reshape(received.shape)
    returned = lax.all_to_all(result, "expert", split_axis=0, concat_axis=0, tiled=True)
    hidden_shape = (received.shape[0], received.shape[1], pre_gate.shape[1])
    outcome = (returned, received, pre_gate.reshape(hidden_shape), pre_up.reshape(hidden_shape))
    returned, kept_rows, kept_gate, kept_up = outcome
    picked = (
        returned.reshape(experts * capacity, model_width)[position]
        .astype(jnp.float32)
        .reshape(length, TOP, model_width)
    )
    mixture = jnp.sum(gate_weights[:, :, None] * picked, axis=1)
    output = resid + mixture + shared_out
    gate_weights_grad = jnp.sum(cotangent[:, None, :] * picked, axis=2)
    copy_grad = (
        (gate_weights[:, :, None] * cotangent[:, None, :])
        .astype(jnp.bfloat16)
        .reshape(copies, model_width)
    )
    grad_send = place_rows(copy_grad, copy_index)
    grad_recv = lax.all_to_all(grad_send, "expert", split_axis=0, concat_axis=0, tiled=True)
    row_count = kept_rows.shape[0] * kept_rows.shape[1]
    rows_flat = kept_rows.reshape(row_count, model_width)
    pre_gate = kept_gate.reshape(row_count, -1)
    pre_up = kept_up.reshape(row_count, -1)
    grad_flat = grad_recv.reshape(row_count, model_width)
    activated, derivative = gated_unit(pre_gate)
    hidden_grad = matmul(grad_flat, down_local.T)
    gate_pre_grad = (hidden_grad * pre_up * derivative).astype(jnp.bfloat16)
    up_pre_grad = (hidden_grad * activated).astype(jnp.bfloat16)
    row_grad = (
        (matmul(gate_pre_grad, gate_local.T) + matmul(up_pre_grad, up_local.T))
        .astype(jnp.bfloat16)
        .reshape(kept_rows.shape)
    )
    row_returned = lax.all_to_all(row_grad, "expert", split_axis=0, concat_axis=0, tiled=True)
    hidden = (activated * pre_up).astype(jnp.bfloat16)
    gate_term = matmul(rows_flat.T, gate_pre_grad)
    up_term = matmul(rows_flat.T, up_pre_grad)
    down_term = matmul(hidden.T, grad_flat)
    expert_gate_grad, expert_up_grad, expert_down_grad = (
        lax.psum_scatter(
            gate_term[None].astype(jnp.bfloat16), "shard", scatter_dimension=2, tiled=True
        ).astype(jnp.float32),
        lax.psum_scatter(
            up_term[None].astype(jnp.bfloat16), "shard", scatter_dimension=2, tiled=True
        ).astype(jnp.float32),
        lax.psum_scatter(
            down_term[None].astype(jnp.bfloat16), "shard", scatter_dimension=1, tiled=True
        ).astype(jnp.float32),
    )
    copy_back = (
        row_returned.reshape(experts * capacity, model_width)[position]
        .astype(jnp.float32)
        .reshape(length, TOP, model_width)
    )
    out_low = cotangent.astype(jnp.bfloat16)
    shared_down_grad = matmul(shared_hidden.T, out_low)
    shared_hgrad = matmul(out_low, down_full.T)
    shared_pre_grad = (shared_hgrad * shared_lift * shared_slope).astype(jnp.bfloat16)
    shared_lift_grad = (shared_hgrad * shared_act).astype(jnp.bfloat16)
    shared_gate_grad = matmul(normed_two.T, shared_pre_grad)
    shared_up_grad = matmul(normed_two.T, shared_lift_grad)
    normed_two_grad = (
        matmul(shared_pre_grad, gate_full.T)
        + matmul(shared_lift_grad, up_full.T)
        + jnp.sum(copy_back, axis=1)
    )
    gain_two_grad, resid_extra = norm_back(resid, inverse_two, gain_two, normed_two_grad)
    resid_grad = cotangent + resid_extra
    ffn_pieces = (
        lax.psum_scatter(
            shared_gate_grad.astype(jnp.bfloat16), "shard", scatter_dimension=1, tiled=True
        ).astype(jnp.float32),
        lax.psum_scatter(
            shared_up_grad.astype(jnp.bfloat16), "shard", scatter_dimension=1, tiled=True
        ).astype(jnp.float32),
        lax.psum_scatter(
            shared_down_grad.astype(jnp.bfloat16), "shard", scatter_dimension=0, tiled=True
        ).astype(jnp.float32),
        lax.psum_scatter(
            gain_two_grad.astype(jnp.bfloat16), "shard", scatter_dimension=0, tiled=True
        ).astype(jnp.float32),
    )
    attn_low = resid_grad.astype(jnp.bfloat16)
    out_weight_grad = matmul(attended.T, attn_low)
    attended_grad = matmul(attn_low, out_full.T).astype(jnp.bfloat16).reshape(head_shape)
    scores = masked_scores()
    probs_full = jnp.exp(scores - logsum)
    value_grad = jnp.einsum(
        "hqk,qhd->khd",
        probs_full.astype(jnp.bfloat16),
        attended_grad,
        preferred_element_type=jnp.float32,
    )
    probs_grad = jnp.einsum(
        "qhd,khd->hqk", attended_grad, value_rows, preferred_element_type=jnp.float32
    )
    score_grad = (
        probs_full * (probs_grad - jnp.sum(probs_full * probs_grad, axis=-1, keepdims=True))
    ).astype(jnp.bfloat16)
    query_grad = (
        jnp.einsum("hqk,khd->qhd", score_grad, key_rows, preferred_element_type=jnp.float32)
        * score_scale
    )
    key_grad = (
        jnp.einsum("hqk,qhd->khd", score_grad, queries, preferred_element_type=jnp.float32)
        * score_scale
    )
    projected_grad = jnp.concatenate(
        [
            rotate(query_grad, cosine_table, -sine_table).reshape(length, model_width),
            rotate(key_grad, cosine_table, -sine_table).reshape(length, model_width),
            value_grad.reshape(length, model_width),
        ],
        axis=1,
    ).astype(jnp.bfloat16)
    qkv_weight_grad = matmul(normed_one.T, projected_grad)
    normed_one_grad = matmul(projected_grad, qkv_full.T)
    gain_one_grad, input_extra = norm_back(inputs, inverse_one, gain_one, normed_one_grad)
    input_grad = resid_grad + input_extra
    attn_pieces = (
        lax.psum_scatter(
            qkv_weight_grad.astype(jnp.bfloat16), "shard", scatter_dimension=0, tiled=True
        ).astype(jnp.float32),
        lax.psum_scatter(
            out_weight_grad.astype(jnp.bfloat16), "shard", scatter_dimension=0, tiled=True
        ).astype(jnp.float32),
        lax.psum_scatter(
            gain_one_grad.astype(jnp.bfloat16), "shard", scatter_dimension=0, tiled=True
        ).astype(jnp.float32),
    )
    summed = (
        lax.psum(attn_pieces[0].astype(jnp.bfloat16), "expert").astype(jnp.float32),
        lax.psum(attn_pieces[1].astype(jnp.bfloat16), "expert").astype(jnp.float32),
        lax.psum(attn_pieces[2].astype(jnp.bfloat16), "expert").astype(jnp.float32),
        lax.psum(ffn_pieces[0].astype(jnp.bfloat16), "expert").astype(jnp.float32),
        lax.psum(ffn_pieces[1].astype(jnp.bfloat16), "expert").astype(jnp.float32),
        lax.psum(ffn_pieces[2].astype(jnp.bfloat16), "expert").astype(jnp.float32),
        lax.psum(ffn_pieces[3].astype(jnp.bfloat16), "expert").astype(jnp.float32),
    )
    return (
        output,
        input_grad,
        summed[2],
        summed[0],
        summed[1],
        summed[6],
        summed[3],
        summed[4],
        summed[5],
        expert_gate_grad,
        expert_up_grad,
        expert_down_grad,
        gate_weights_grad,
    )


def solution(mesh):
    in_specs = (
        P(("expert", "shard"), None),
        P(("expert", "shard"), None),
        P("shard"),
        P("shard", None),
        P("shard", None),
        P("shard"),
        P(None, "shard"),
        P(None, "shard"),
        P("shard", None),
        P("expert", None, None),
        P("expert", None, None),
        P("expert", None, None),
        P(("expert", "shard"), None),
        P(("expert", "shard"), None),
        P(("expert", "shard")),
    )
    out_specs = (
        P(("expert", "shard"), None),
        P(("expert", "shard"), None),
        P("shard"),
        P("shard", None),
        P("shard", None),
        P("shard"),
        P(None, "shard"),
        P(None, "shard"),
        P("shard", None),
        P("expert", None, "shard"),
        P("expert", None, "shard"),
        P("expert", "shard", None),
        P(("expert", "shard"), None),
    )
    return jax.shard_map(
        on_device, mesh=mesh, in_specs=in_specs, out_specs=out_specs, check_vma=False
    )
```

profile of v0, /device:TPU:0, one launch (start us, length us, event | category | flops | bytes accessed | tf_op | source)
XLA Modules:
  0.0 837.4 jit_solution(5135879969428653697)
XLA Ops:
  11.2 4.1 mul.524
  15.3 5.3 mul.525
  29.8 4.3 scatter_custom_fusion
  34.1 11.7 %gather_fusion.2 = bf16[2048,768]{1,0:T(8,128)(2,1)} fusion(bf16[1025,768]{1,0:T(8,128)(2,1)} %concatenate.29, s32[2048]{0:T(1024)S(1)} %get-tuple-element.63), kind=kCustom, calls=%fused_computation.2 | custom fusion | bytes 6299648 | tf_op jit(solution)/shard_map/gather | solution.py:147
  45.8 6.6 all-to-all-start.2
  54.9 10.7 %all-reduce.9 = (bf16[768]{0:T(1024)(128)(2,1)S(1)}, bf16[768]{0:T(1024)(128)(2,1)}) all-reduce(bf16[768]{0:T(1024)(128)(2,1)S(1)} %dynamic-update-slice, bf16[768]{0:T(1024)(128)(2,1)S(1)} %dynamic-update-slice.1), channel_id=1, replica_groups=mesh['expert'=8,'shard'=4] {'shard'}, use_global_device_ids=true, to_apply=%add.2 | all-reduce | flops 1536 | bytes 6144
  70.2 4.5 fusion.59
  86.4 5.8 fusion.7
  96.9 8.0 fusion.1
  105.8 5.9 fusion.28
  116.9 18.3 %all-gather.10.cloned.1.call-done = bf16[768,2048]{1,0:T(8,128)(2,1)} async-done(((bf16[768,512]{1,0:T(8,128)(2,1)}), bf16[768,2048]{1,0:T(8,128)(2,1)}) %all-gather.10.cloned.1.call-update) | async-done | bytes 3145744 | tf_op jit(solution)/shard_map/all_gather | solution.py:78
  135.2 5.9 fusion.62
  141.1 39.6 %all-gather.12.cloned.1.call-done = bf16[768,2048]{1,0:T(8,128)(2,1)} async-done(((bf16[768,512]{1,0:T(8,128)(2,1)}), bf16[768,2048]{1,0:T(8,128)(2,1)}) %all-gather.12.cloned.1.call-update) | async-done | bytes 3145744 | tf_op jit(solution)/shard_map/all_gather | solution.py:79
  180.7 5.9 fusion.63
  186.7 39.8 %all-gather.14.cloned.1.call-done = bf16[2048,768]{1,0:T(8,128)(2,1)} async-done(((bf16[512,768]{1,0:T(8,128)(2,1)}), bf16[2048,768]{1,0:T(8,128)(2,1)}) %all-gather.14.cloned.1.call-update) | async-done | bytes 3145744 | tf_op jit(solution)/shard_map/all_gather | solution.py:80
  226.4 10.0 %multiply_convert_fusion.4 = (bf16[512,2048]{1,0:T(8,128)(2,1)}, bf16[512,2048]{1,0:T(8,128)(2,1)S(1)}, bf16[512,2048]{1,0:T(8,128)(2,1)}) fusion(f32[512,2048]{1,0:T(8,128)} %fusion.62, f32[512,2048]{1,0:T(8,128)} %fusion.63, bf16[2048,768]{1,0:T(8,128)(2,1)} %all-gather.14.cloned.1.call-done, f32[512,768]{1,0:T(8,128)} %param.16), kind=kOutput, calls=%fused_computation.24 | convolution fusion | flops 1626734592 | bytes 19398656 | tf_op jit(solution)/shard_map/dot_general | solution.py:51
  243.3 11.4 %gather_fusion = bf16[2048,768]{1,0:T(8,128)(2,1)} fusion(bf16[513,768]{1,0:T(8,128)(2,1)} %concatenate.28, s32[2048]{0:T(1024)S(1)} %get-tuple-element.64), kind=kCustom, calls=%fused_computation | custom fusion | bytes 6299648 | tf_op jit(solution)/shard_map/gather | solution.py:147
  254.7 4.6 all-to-all-start
  259.3 5.5 convolution_convert_fusion.5
  264.8 12.8 %fusion.9 = f32[2048,2048]{1,0:T(8,128)} fusion(bf16[2048,768]{1,0:T(8,128)(2,1)} %bitcast.18, bf16[1,2048,768]{2,1,0:T(8,128)(2,1)} %param.26), kind=kOutput, calls=%fused_computation.36 | convolution fusion | flops 6442450944 | bytes 23068672 | tf_op jit(solution)/shard_map/dot_general | solution.py:51
  277.6 53.3 %all-to-all-done = bf16[8,256,768]{2,1,0:T(8,128)(2,1)} async-done(((bf16[8,256,768]{2,1,0:T(8,128)(2,1)}), bf16[8,256,768]{2,1,0:T(8,128)(2,1)}, u32[]{:S(2)}, u32[]{:S(2)}) %all-to-all-start) | async-done | bytes 3145760 | tf_op jit(solution)/shard_map/all_to_all | solution.py:153
  330.9 12.6 %fusion.14 = f32[2048,2048]{1,0:T(8,128)} fusion(bf16[2048,768]{1,0:T(8,128)(2,1)} %bitcast.11, bf16[1,768,2048]{2,1,0:T(8,128)(2,1)} %param.25), kind=kOutput, calls=%fused_computation.41 | convolution fusion | flops 6442450944 | bytes 23068672 | tf_op jit(solution)/shard_map/dot_general | solution.py:51
  343.5 26.2 %multiply_convert_fusion.1 = (bf16[2048,2048]{1,0:T(8,128)(2,1)}, bf16[2048,2048]{1,0:T(8,128)(2,1)}, bf16[2048,2048]{1,0:T(8,128)(2,1)}) fusion(f32[2048,2048]{1,0:T(8,128)} %fusion.9, f32[2048,2048]{1,0:T(8,128)} %fusion.14, bf16[2048,768]{1,0:T(8,128)(2,1)} %bitcast.11, bf16[1,768,2048]{2,1,0:T(8,128)(2,1)S(1)} %copy-done), kind=kOutput, calls=%fused_computation.6 | convolution fusion | flops 6505365504 | bytes 65011712 | tf_op jit(solution)/shard_map/dot_general | solution.py:51
  369.7 10.4 %fusion.12 = f32[2048,768]{1,0:T(8,128)S(1)} fusion(bf16[2048,2048]{1,0:T(8,128)(2,1)} %get-tuple-element.44, bf16[1,768,2048]{2,1,0:T(8,128)(2,1)} %param.25), kind=kOutput, calls=%fused_computation.39 | convolution fusion | flops 6442450944 | bytes 17825792 | tf_op jit(solution)/shard_map/dot_general | solution.py:51
  380.2 8.2 add_convert_fusion
  392.0 5.6 convolution_convert_fusion.4
  398.4 5.5 fusion.64
  403.9 59.5 %all-to-all-done.3 = bf16[8,256,768]{2,1,0:T(8,128)(2,1)S(1)} async-done(((bf16[8,256,768]{2,1,0:T(8,128)(2,1)}), bf16[8,256,768]{2,1,0:T(8,128)(2,1)S(1)}, u32[]{:S(2)}, u32[]{:S(2)}) %all-to-all-start.3) | async-done | bytes 3145760 | tf_op jit(solution)/shard_map/all_to_all | solution.py:194
  463.4 5.6 gather_fusion.3
  469.0 4.9 reshape.294
  473.9 5.7 reduce_sum.116
  479.7 5.2 multiply_reduce_fusion.3
  493.2 11.4 %multiply_reduce_fusion = (f32[12,512]{1,0:T(8,128)S(1)}, f32[12,512,512]{1,2,0:T(8,128)}) fusion(f32[12,512]{1,0:T(8,128)S(1)} %log_add_fusion, f32[12,512,512]{1,2,0:T(8,128)} %get-tuple-element.75, pred[512,512]{0,1:T(8,128)(4,1)S(1)} %copy-done.13, bf16[512,12,64]{0,2,1:T(8,128)(2,1)} %bitcast.126, bf16[512,12,64]{0,2,1:T(8,128)(2,1)S(1)} %bitcast.125), kind=kOutput, calls=%fused_computation.11 | convolution fusion | flops 418375680 | bytes 27049984 | tf_op jit(solution)/shard_map/qhd,khd->hqk/dot_general | solution.py:254
  506.0 10.1 %multiply_convert_fusion.3 = bf16[12,512,512]{1,2,0:T(8,128)(2,1)} fusion(f32[12,512,512]{1,2,0:T(8,128)} %get-tuple-element.80, f32[12,512]{1,0:T(8,128)S(1)} %get-tuple-element.79, f32[12,512]{1,0:T(8,128)S(1)} %log_add_fusion, f32[12,512,512]{1,2,0:T(8,128)S(1)} %bitcast.115, pred[512,512]{0,1:T(8,128)(4,1)S(1)} %copy-done.13), kind=kLoop, calls=%fused_computation.10 | loop fusion | flops 18874368 | bytes 31768576 | tf_op jit(solution)/shard_map/convert_element_type | solution.py:259
  533.1 12.2 %fusion.21 = bf16[1,768,2048]{2,1,0:T(8,128)(2,1)} fusion(bf16[2048,768]{1,0:T(8,128)(2,1)} %bitcast.11, bf16[2048,2048]{1,0:T(8,128)(2,1)} %get-tuple-element.43), kind=kOutput, calls=%fused_computation.51 | convolution fusion | flops 6444023808 | bytes 14680064 | tf_op jit(solution)/shard_map/dot_general | solution.py:51
  545.4 12.2 %fusion.22 = bf16[1,768,2048]{2,1,0:T(8,128)(2,1)} fusion(bf16[2048,768]{1,0:T(8,128)(2,1)} %bitcast.11, bf16[2048,2048]{1,0:T(8,128)(2,1)} %get-tuple-element.44), kind=kOutput, calls=%fused_computation.52 | convolution fusion | flops 6444023808 | bytes 14680064 | tf_op jit(solution)/shard_map/dot_general | solution.py:51
  557.7 11.6 %fusion.20 = bf16[1,2048,768]{2,1,0:T(8,128)(2,1)} fusion(bf16[2048,2048]{1,0:T(8,128)(2,1)} %get-tuple-element.45, bf16[2048,768]{1,0:T(8,128)(2,1)} %bitcast.18), kind=kOutput, calls=%fused_computation.50 | convolution fusion | flops 6444023808 | bytes 14680064 | tf_op jit(solution)/shard_map/dot_general | solution.py:51
  571.2 10.2 %convolution_convert_fusion.3 = bf16[2048,768]{1,0:T(8,128)(2,1)} fusion(bf16[2048,2048]{1,0:T(8,128)(2,1)} %get-tuple-element.45, bf16[1,2048,768]{2,1,0:T(8,128)(2,1)S(1)} %copy-done.58), kind=kOutput, calls=%fused_computation.31 | convolution fusion | flops 6444023808 | bytes 14680064 | tf_op jit(solution)/shard_map/dot_general | solution.py:51
  585.8 70.8 %all-to-all-done.1 = bf16[8,256,768]{2,1,0:T(8,128)(2,1)S(1)} async-done(((bf16[8,256,768]{2,1,0:T(8,128)(2,1)}), bf16[8,256,768]{2,1,0:T(8,128)(2,1)S(1)}, u32[]{:S(2)}, u32[]{:S(2)}) %all-to-all-start.1) | async-done | bytes 3145760 | tf_op jit(solution)/shard_map/all_to_all | solution.py:161
  656.6 5.4 gather_fusion.1
  662.0 5.0 reshape.293
  667.1 5.6 multiply_reduce_fusion.4
  672.7 9.1 %all-reduce.8 = (bf16[768]{0:T(1024)(128)(2,1)S(1)}, bf16[768]{0:T(1024)(128)(2,1)S(1)}) all-reduce(bf16[768]{0:T(1024)(128)(2,1)S(1)} %get-tuple-element.30, bf16[768]{0:T(1024)(128)(2,1)S(1)} %get-tuple-element.28), channel_id=2, replica_groups=mesh['expert'=8,'shard'=4] {'shard'}, use_global_device_ids=true, to_apply=%region_14.15.clone | all-reduce | flops 1536 | bytes 6144
  682.0 13.6 %all-reduce.6 = (bf16[192]{0:T(256)(128)(2,1)S(1)}, bf16[192]{0:T(256)(128)(2,1)S(1)}) all-reduce(bf16[192]{0:T(256)(128)(2,1)S(1)} %dynamic-slice.3, bf16[192]{0:T(256)(128)(2,1)S(1)} %dynamic-slice.5), channel_id=1, replica_groups=mesh['expert'=8,'shard'=4] {'expert'}, use_global_device_ids=true, to_apply=%region_15.16 | all-reduce | flops 384 | bytes 1536 | tf_op jit(solution)/shard_map/psum | solution.py:294
  696.8 9.7 %multiply_reduce_fusion.1 = (f32[512,2]{1,0:T(8,128)}, f32[512,768]{1,0:T(8,128)}) fusion(f32[512,2,768]{2,1,0:T(2,128)} %reshape.293, f32[512,768]{1,0:T(8,128)} %param.16, f32[512,2]{1,0:T(8,128)S(1)} %copy-done.19), kind=kLoop, calls=%fused_computation.47 | loop fusion | flops 2751488 | bytes 6299648 | tf_op jit(solution)/shard_map/reduce_sum | solution.py:172
  712.2 4.6 add_add_fusion.1
  721.8 11.9 %reduce-scatter.23.cloned.1.call-done = bf16[1,512,768]{2,1,0:T(8,128)(2,1)} async-done(((bf16[1,2048,768]{2,1,0:T(8,128)(2,1)}), bf16[1,512,768]{2,1,0:T(8,128)(2,1)}) %reduce-scatter.23.cloned.1.call-update) | async-done | bytes 786448 | tf_op jit(solution)/shard_map/reduce_scatter | solution.py:206
  736.1 85.9 %all-reduce.12.cloned.1.call-done = (bf16[192,2304]{1,0:T(8,128)(2,1)}, bf16[192,768]{1,0:T(8,128)(2,1)}, bf16[768,512]{1,0:T(8,128)(2,1)}, bf16[768,512]{1,0:T(8,128)(2,1)}, bf16[512,768]{1,0:T(8,128)(2,1)}) async-done(((bf16[192,2304]{1,0:T(8,128)(2,1)}, bf16[192,768]{1,0:T(8,128)(2,1)}, bf16[768,512]{1,0:T(8,128)(2,1)}, bf16[768,512]{1,0:T(8,128)(2,1)}, bf16[512,768]{1,0:T(8,128)(2,1)}), ...) | async-done | bytes 3538960 | tf_op jit(solution)/shard_map/psum | solution.py:292
  (255 shorter events, 107.5 us)
Async XLA Ops:
  7.2 336.3 %copy-start = (bf16[1,768,2048]{2,1,0:T(8,128)(2,1)S(1)}, bf16[1,768,2048]{2,1,0:T(8,128)(2,1)}, u32[]{:S(2)}) copy-start(bf16[1,768,2048]{2,1,0:T(8,128)(2,1)} %param.24) | copy-start | bytes 9437188
  7.2 63.0 %all-gather.6.cloned.1.call-start = ((), (), s32[]{:S(2)}) async-start(), calls=%async_computation.12 | async-start | bytes 4423680 | tf_op jit(solution)/shard_map/all_gather | solution.py:73
  7.9 103.7 %all-gather.8.cloned.1.call-start = ((), (), s32[]{:S(2)}) async-start(), calls=%async_computation.13 | async-start | bytes 1474560 | tf_op jit(solution)/shard_map/all_gather | solution.py:74
  8.7 126.5 %all-gather.10.cloned.1.call-start = ((), (), s32[]{:S(2)}) async-start(), calls=%async_computation.14 | async-start | bytes 3932160 | tf_op jit(solution)/shard_map/all_gather | solution.py:78
  9.4 171.3 %all-gather.12.cloned.1.call-start = ((), (), s32[]{:S(2)}) async-start(), calls=%async_computation.15 | async-start | bytes 3932160 | tf_op jit(solution)/shard_map/all_gather | solution.py:79
  20.7 8.3 copy-start.18
  45.8 7.3 copy-start.57
  45.8 8.6 %copy-start.60 = (bf16[192]{0:T(256)(128)(2,1)S(1)}, bf16[192]{0:T(256)(128)(2,1)}, u32[]{:S(2)}) copy-start(bf16[192]{0:T(256)(128)(2,1)} %param.17) | copy-start | bytes 1156
  45.8 8.8 %copy-start.61 = (bf16[192]{0:T(256)(128)(2,1)S(1)}, bf16[192]{0:T(256)(128)(2,1)}, u32[]{:S(2)}) copy-start(bf16[192]{0:T(256)(128)(2,1)} %param.20) | copy-start | bytes 1156
  45.8 208.9 %all-to-all-start.2 = ((bf16[8,256,768]{2,1,0:T(8,128)(2,1)}), bf16[8,256,768]{2,1,0:T(8,128)(2,1)}, u32[]{:S(2)}, u32[]{:S(2)}) async-start(bf16[8,256,768]{2,1,0:T(8,128)(2,1)} %bitcast.120), calls=%async_computation.2 | async-start | bytes 6291456 | tf_op jit(solution)/shard_map/all_to_all | solution.py:179
  52.4 174.0 %all-gather.14.cloned.1.call-start = ((), (), s32[]{:S(2)}) async-start(), calls=%async_computation.16 | async-start | bytes 3932160 | tf_op jit(solution)/shard_map/all_gather | solution.py:80
  53.0 643.7 %reduce-scatter.13.cloned.1.call-start = ((), (), s32[]{:S(2)}) async-start(), calls=%async_computation.19 | async-start | bytes 3932160 | tf_op jit(solution)/shard_map/reduce_scatter | solution.py:230
  65.5 9.2 %copy-start.51 = (f32[768]{0:T(1024)}, f32[768]{0:T(1024)S(1)}, u32[]{:S(2)}) copy-start(f32[768]{0:T(1024)S(1)} %convert_element_type.183) | copy-start | bytes 9220
  68.6 36.3 %copy-start.12 = (pred[512,512]{0,1:T(8,128)(4,1)}, pred[512,512]{0,1:T(8,128)(4,1)S(1)}, u32[]{:S(2)}) copy-start(pred[512,512]{0,1:T(8,128)(4,1)S(1)} %fusion.29) | copy-start | bytes 786436
  69.5 14.5 %copy-start.37 = (f32[512,32]{0,1:T(8,128)}, f32[512,32]{0,1:T(8,128)S(1)}, u32[]{:S(2)}) copy-start(f32[512,32]{0,1:T(8,128)S(1)} %get-tuple-element.73) | copy-start | bytes 196612
  70.2 45.1 %copy-start.44 = (f32[768]{0:T(1024)}, f32[768]{0:T(1024)S(1)}, u32[]{:S(2)}) copy-start(f32[768]{0:T(1024)S(1)} %convert_element_type.190) | copy-start | bytes 9220
  86.3 5.8 copy-start.20
  86.3 5.8 copy-start.22
  86.3 5.8 copy-start.25
  86.4 5.8 copy-start.27
  92.2 12.7 %copy-start.40 = (f32[12,512]{1,0:T(8,128)}, f32[12,512]{1,0:T(8,128)S(1)}, u32[]{:S(2)}) copy-start(f32[12,512]{1,0:T(8,128)S(1)} %get-tuple-element.74) | copy-start | bytes 73732
  96.9 8.9 %copy-start.2 = (f32[12,512,512]{1,2,0:T(8,128)S(1)}, f32[12,512,512]{1,2,0:T(8,128)}, u32[]{:S(2)}) copy-start(f32[12,512,512]{1,2,0:T(8,128)} %get-tuple-element.75) | copy-start | bytes 37748740
  226.4 11.3 %copy-start.17 = (bf16[512,768]{1,0:T(8,128)(2,1)S(1)}, bf16[512,768]{1,0:T(8,128)(2,1)}, u32[]{:S(2)}) copy-start(bf16[512,768]{1,0:T(8,128)(2,1)} %multiply_convert_fusion.8) | copy-start | bytes 2359300
  254.7 76.2 %all-to-all-start = ((bf16[8,256,768]{2,1,0:T(8,128)(2,1)}), bf16[8,256,768]{2,1,0:T(8,128)(2,1)}, u32[]{:S(2)}, u32[]{:S(2)}) async-start(bf16[8,256,768]{2,1,0:T(8,128)(2,1)} %bitcast.121), calls=%async_computation | async-start | bytes 6291456 | tf_op jit(solution)/shard_map/all_to_all | solution.py:153
  259.3 437.4 %reduce-scatter.15.cloned.1.call-start = ((), (), s32[]{:S(2)}) async-start(), calls=%async_computation.20 | async-start | bytes 3932160 | tf_op jit(solution)/shard_map/reduce_scatter | solution.py:233
  369.7 10.4 %copy-start.64 = (bf16[2048,2048]{1,0:T(8,128)(2,1)S(1)}, bf16[2048,2048]{1,0:T(8,128)(2,1)}, u32[]{:S(2)}) copy-start(bf16[2048,2048]{1,0:T(8,128)(2,1)} %get-tuple-element.43) | copy-start | bytes 25165828
  388.3 75.1 %all-to-all-start.3 = ((bf16[8,256,768]{2,1,0:T(8,128)(2,1)}), bf16[8,256,768]{2,1,0:T(8,128)(2,1)S(1)}, u32[]{:S(2)}, u32[]{:S(2)}) async-start(bf16[8,256,768]{2,1,0:T(8,128)(2,1)} %bitcast.130), calls=%async_computation.3 | async-start | bytes 6291456 | tf_op jit(solution)/shard_map/all_to_all | solution.py:194
  392.0 304.7 %reduce-scatter.17.cloned.1.call-start = ((), (), s32[]{:S(2)}) async-start(), calls=%async_computation.21 | async-start | bytes 3932160 | tf_op jit(solution)/shard_map/reduce_scatter | solution.py:236
  397.6 299.1 %reduce-scatter.11.cloned.1.call-start = ((), (), s32[]{:S(2)}) async-start(), calls=%async_computation.18 | async-start | bytes 1474560 | tf_op jit(solution)/shard_map/reduce_scatter | solution.py:284
  473.9 5.8 copy-start.47
  486.2 7.0 copy-start.4
  493.2 11.4 %slice-start = ((s8[12582912]{0:T(1024)(128)(4,1)}), s8[4194304]{0:T(1024)(128)(4,1)S(1)}, s32[]{:S(2)}) async-start(s8[12582912]{0:T(1024)(128)(4,1)} %bitcast.114), calls=%async_computation.26 | async-start | bytes 8388608
  493.2 11.4 %slice-start.1 = ((s8[12582912]{0:T(1024)(128)(4,1)}), s8[4194304]{0:T(1024)(128)(4,1)S(1)}, s32[]{:S(2)}) async-start(s8[12582912]{0:T(1024)(128)(4,1)} %bitcast.114), calls=%async_computation.27 | async-start | bytes 8388608
  493.2 12.8 %slice-start.2 = ((s8[12582912]{0:T(1024)(128)(4,1)}), s8[4194304]{0:T(1024)(128)(4,1)S(1)}, s32[]{:S(2)}) async-start(s8[12582912]{0:T(1024)(128)(4,1)} %bitcast.114), calls=%async_computation.28 | async-start | bytes 8388608
  506.0 10.2 %copy-start.26 = (bf16[512,12,32]{0,2,1:T(8,128)(2,1)S(1)}, bf16[512,12,32]{0,2,1:T(8,128)(2,1)}, u32[]{:S(2)}) copy-start(bf16[512,12,32]{0,2,1:T(8,128)(2,1)} %copy-done.25) | copy-start | bytes 1179652
  506.0 10.2 %copy-start.28 = (bf16[512,12,32]{0,2,1:T(8,128)(2,1)S(1)}, bf16[512,12,32]{0,2,1:T(8,128)(2,1)}, u32[]{:S(2)}) copy-start(bf16[512,12,32]{0,2,1:T(8,128)(2,1)} %copy-done.27) | copy-start | bytes 1179652
  516.1 180.6 %reduce-scatter.9.cloned.1.call-start = ((), (), s32[]{:S(2)}) async-start(), calls=%async_computation.17 | async-start | bytes 4423680 | tf_op jit(solution)/shard_map/reduce_scatter | solution.py:281
  516.2 7.5 slice-start.3
  516.2 7.5 slice-start.4
  533.1 183.7 %reduce-scatter.19.cloned.1.call-start = ((), (), s32[]{:S(2)}) async-start(), calls=%async_computation.22 | async-start | bytes 3932160 | tf_op jit(solution)/shard_map/reduce_scatter | solution.py:200
  545.3 174.0 %reduce-scatter.21.cloned.1.call-start = ((), (), s32[]{:S(2)}) async-start(), calls=%async_computation.23 | async-start | bytes 3932160 | tf_op jit(solution)/shard_map/reduce_scatter | solution.py:203
  557.6 176.1 %reduce-scatter.23.cloned.1.call-start = ((), (), s32[]{:S(2)}) async-start(), calls=%async_computation.24 | async-start | bytes 3932160 | tf_op jit(solution)/shard_map/reduce_scatter | solution.py:206
  581.5 75.1 %all-to-all-start.1 = ((bf16[8,256,768]{2,1,0:T(8,128)(2,1)}), bf16[8,256,768]{2,1,0:T(8,128)(2,1)S(1)}, u32[]{:S(2)}, u32[]{:S(2)}) async-start(bf16[8,256,768]{2,1,0:T(8,128)(2,1)} %bitcast.131), calls=%async_computation.1 | async-start | bytes 6291456 | tf_op jit(solution)/shard_map/all_to_all | solution.py:161
  585.1 236.8 %all-reduce.12.cloned.1.call-start = ((), (), s32[]{:S(2)}) async-start(), calls=%async_computation.25 | async-start | bytes 7077888 | tf_op jit(solution)/shard_map/psum | solution.py:292
  672.7 24.1 %copy-start.19 = (f32[512,2]{1,0:T(8,128)S(1)}, f32[512,2]{1,0:T(8,128)}, u32[]{:S(2)}) copy-start(f32[512,2]{1,0:T(8,128)} %copy-done.18) | copy-start | bytes 12292
  696.8 11.4 %copy-start.5 = (f32[512,768]{1,0:T(8,128)S(1)}, f32[512,768]{1,0:T(8,128)}, u32[]{:S(2)}) copy-start(f32[512,768]{1,0:T(8,128)} %copy-done.4) | copy-start | bytes 4718596
  696.8 11.4 %copy-start.53 = (f32[512]{0:T(512)S(1)}, f32[512]{0:T(512)}, u32[]{:S(2)}) copy-start(f32[512]{0:T(512)} %get-tuple-element.65) | copy-start | bytes 6148
  821.9 5.9 copy-start.35
  (41 other events, 136.9 us)
Sparse Core Ops, SparseCore 0:
  9.9 49.9 all-gather.5
  61.7 27.7 all-gather.7
  91.3 43.8 all-gather.9
  136.8 43.8 all-gather.11
  182.4 43.9 all-gather.13
  241.4 43.9 reduce-scatter.12
  288.3 43.9 reduce-scatter.14
  397.7 44.3 reduce-scatter.16
  516.3 26.4 reduce-scatter.10
  545.7 47.2 reduce-scatter.8
  595.9 43.9 reduce-scatter.18
  642.7 44.1 reduce-scatter.20
  689.9 43.7 reduce-scatter.22
  736.3 85.5 all-reduce.11
where the time goes:
time: 845 us; the launch traced here: 837 us
  waiting for transfers between devices  382 us (45%)
  matrix products  222 us (26%)
  local copies, waits for them, and re-layouts  96.1 us (11%)
  other arithmetic  67.4 us (8%)
  blocking collectives  33.4 us (4%)
  starting transfers between devices  19.1 us (2%)
  between operations  17.1 us (2%)
    dot_general x24, matrix products, matmul(): return jnp.dot(left, right, preferred_element_type=jnp.float32)  190 us
    psum x1, waiting for transfers between devices, on_device(): lax.psum(attn_pieces[0].astype(jnp.bfloat16), 'expert').astype(jnp.float32)  85.9 us
    all_to_all x1, waiting for transfers between devices, on_device(): lax.all_to_all(result, 'expert', split_axis=0, concat_axis=0, tiled=True)  70.8 us
    all_to_all x1, waiting for transfers between devices, on_device(): lax.all_to_all(row_grad, 'expert', split_axis=0, concat_axis=0, tiled=True)  59.5 us
    all_to_all x1, waiting for transfers between devices, on_device(): lax.all_to_all(dispatched, 'expert', split_axis=0, concat_axis=0, tiled=T...  53.3 us
    all_gather x1, waiting for transfers between devices, on_device(): lax.all_gather(shared_down, 'shard', axis=0, tiled=True)  39.8 us
    all_gather x1, waiting for transfers between devices, on_device(): lax.all_gather(shared_up, 'shard', axis=1, tiled=True)  39.6 us
    gather x2, local copies, waits for them, and re-layouts, place_rows(): return padded[index].reshape(experts, capacity, model_width)  23 us
  transfers between devices with their start and end apart: 18, of which 8 were waited for; matrix products, arithmetic and copies ran while one was open for 43% of the time, Pallas kernels for 0%

commit v1 on v0

v1 whole, which is shorter than its diff:
```python
import functools

import jax
import jax.numpy as jnp
from jax import lax
from jax.experimental import pallas as pl
from jax.experimental.pallas import tpu as pltpu
from jax.sharding import PartitionSpec as P

HEADS = 12
HEAD_DIM = 64
TOP = 2
EPS = 1e-06
MESH = pl.DeviceIdType.MESH
F32 = jnp.float32
BF16 = jnp.bfloat16


def rope_tables(length):
    half_dim = HEAD_DIM // 2
    frequency = 10000.0 ** (-jnp.arange(half_dim, dtype=jnp.float32) * 2.0 / HEAD_DIM)
    angles = jnp.arange(length, dtype=jnp.float32)[:, None] * frequency[None, :]
    return (jnp.cos(angles)[:, None, :], jnp.sin(angles)[:, None, :])


def rotate(vectors, cosine_table, sine_table):
    half_dim = vectors.shape[-1] // 2
    first_half = vectors[..., :half_dim]
    second = vectors[..., half_dim:]
    return jnp.concatenate(
        [
            first_half * cosine_table - second * sine_table,
            second * cosine_table + first_half * sine_table,
        ],
        axis=-1,
    )


def gated_unit(pre_gate):
    sigmoid_value = jax.nn.sigmoid(pre_gate)
    activated = pre_gate * sigmoid_value
    derivative = sigmoid_value * (1.0 + pre_gate * (1.0 - sigmoid_value))
    return (activated, derivative)


def norm_back(source, inverse, gain, grad_in):
    scaled = grad_in * gain
    gain_grad = jnp.sum(grad_in * source * inverse, axis=0)
    input_part = inverse * scaled - source * inverse**3 * jnp.mean(
        scaled * source, axis=-1, keepdims=True
    )
    return (gain_grad, input_part)


def matmul(left, right):
    return jnp.dot(left, right, preferred_element_type=jnp.float32)


def place():
    expert, shard = lax.axis_index("expert"), lax.axis_index("shard")
    core, x, y = expert % 2, shard % 2, shard // 2
    return dict(
        expert=expert,
        shard=shard,
        core=core,
        z=expert // 2,
        sx=2 * y + 1 - x,
        sy=2 * (1 - y) + x,
        sd=2 * (1 - y) + 1 - x,
        dev_x=(expert, 2 * y + 1 - x),
        dev_y=(expert, 2 * (1 - y) + x),
        dev_c=(expert + 1 - 2 * core, shard),
    )


def meet(devices):
    barrier = pltpu.get_barrier_semaphore()
    for device in devices:
        pl.semaphore_signal(barrier, inc=1, device_id=device, device_id_type=MESH)
    pl.semaphore_wait(barrier, len(devices))


def remote(src, dst, send, recv, device):
    return pltpu.make_async_remote_copy(
        src_ref=src, dst_ref=dst, send_sem=send, recv_sem=recv, device_id=device, device_id_type=MESH
    )


class PlaneGather:
    COPIES = 7

    def __init__(self, src, dst, axis, send, recv, local, at):
        self.src, self.dst, self.axis, self.at = src, dst, axis, at
        self.send, self.recv, self.local = send, recv, local
        self.rows, self.cols = src.shape
        self.copies = []

    def view(self, shard, start, count):
        if self.axis == 0:
            return self.dst.at[pl.ds(pl.multiple_of(shard * self.rows + start, 16), count), :]
        return self.dst.at[
            pl.ds(pl.multiple_of(start, 16), count),
            pl.ds(pl.multiple_of(shard * self.cols, 128), self.cols),
        ]

    def copy(self, src, dst, index, device):
        made = remote(src, dst, self.send.at[index], self.recv.at[index], device)
        made.start()
        self.copies.append(made)

    def first(self):
        at, half = self.at, self.rows // 2
        src = self.src.at[pl.ds(pl.multiple_of(at["core"] * half, 16), half), :]
        dst = self.view(at["shard"], at["core"] * half, half)
        self.copy(src, dst, 0, at["dev_x"])
        self.copy(src, dst, 1, at["dev_y"])
        self.own = pltpu.make_async_copy(self.src, self.view(at["shard"], 0, self.rows), self.local)
        self.own.start()

    def second(self):
        at, half, quarter = self.at, self.rows // 2, self.rows // 4
        start = at["core"] * half
        self.copies[0].wait_recv()
        part = self.view(at["sx"], start, quarter)
        self.copy(part, part, 2, at["dev_y"])
        part = self.view(at["sx"], start, half)
        self.copy(part, part, 3, at["dev_c"])
        self.copies[1].wait_recv()
        part = self.view(at["sy"], start + quarter, quarter)
        self.copy(part, part, 4, at["dev_x"])
        part = self.view(at["sy"], start, half)
        self.copy(part, part, 5, at["dev_c"])

    def third(self):
        at, half = self.at, self.rows // 2
        self.copies[2].wait_recv()
        self.copies[4].wait_recv()
        part = self.view(at["sd"], at["core"] * half, half)
        self.copy(part, part, 6, at["dev_c"])

    def finish(self):
        for index in (3, 5, 6):
            self.copies[index].wait_recv()
        for made in self.copies:
            made.wait_send()
        self.own.wait()


def plane_gather_kernel(*refs, axes):
    count = len(axes)
    send, recv, local = refs[2 * count :]
    at = place()
    meet([at["dev_x"], at["dev_y"], at["dev_c"]])
    gathers = [
        PlaneGather(refs[k], refs[count + k], axes[k], send.at[k], recv.at[k], local.at[k], at)
        for k in range(count)
    ]
    for step in ("first", "second", "third", "finish"):
        for gather in gathers:
            getattr(gather, step)()


def plane_gather(arrays, axes, ident):
    if lax.axis_size("shard") != 4:
        return [lax.all_gather(v, "shard", axis=a, tiled=True) for v, a in zip(arrays, axes)]
    count = len(arrays)
    shapes = []
    for array, axis in zip(arrays, axes):
        shape = list(array.shape)
        shape[axis] *= 4
        shapes.append(jax.ShapeDtypeStruct(tuple(shape), array.dtype))
    return pl.pallas_call(
        functools.partial(plane_gather_kernel, axes=axes),
        out_shape=shapes,
        in_specs=[pl.BlockSpec(memory_space=pl.ANY)] * count,
        out_specs=[pl.BlockSpec(memory_space=pl.ANY)] * count,
        scratch_shapes=[
            pltpu.SemaphoreType.DMA((count, PlaneGather.COPIES)),
            pltpu.SemaphoreType.DMA((count, PlaneGather.COPIES)),
            pltpu.SemaphoreType.DMA((count,)),
        ],
        compiler_params=pltpu.CompilerParams(
            collective_id=ident, has_side_effects=True, vmem_limit_bytes=32 << 20
        ),
    )(*arrays)


class PlaneReduce:
    COPIES = 4

    def __init__(self, src, dst, mine, got, hold, last, send, recv, local, at):
        self.src, self.dst, self.mine, self.got, self.hold, self.last = src, dst, mine, got, hold, last
        self.send, self.recv, self.local, self.at = send, recv, local, at
        self.half = src.shape[1] // 2

    @staticmethod
    def scratch(shape):
        half = shape[1] // 2
        return [
            pltpu.VMEM((4, half, shape[2]), BF16),
            pltpu.VMEM((4, half, shape[2]), BF16),
            pltpu.VMEM((2, half, shape[2]), BF16),
            pltpu.VMEM((2, half, shape[2]), BF16),
        ]

    def first(self):
        at, half = self.at, self.half
        upper, lower = pl.ds(0, half), pl.ds(half, half)
        plan = [
            (at["sx"], upper, at["dev_x"], 0),
            (at["sd"], upper, at["dev_x"], 1),
            (at["sy"], lower, at["dev_y"], 2),
            (at["sd"], lower, at["dev_y"], 3),
        ]
        self.out = []
        for shard, rows, device, slot in plan:
            made = remote(
                self.src.at[shard, rows, :], self.got.at[slot], self.send.at[slot], self.recv.at[slot], device
            )
            made.start()
            self.out.append(made)
        self.near = []
        for slot, (shard, rows) in enumerate(
            [(at["shard"], upper), (at["sy"], upper), (at["shard"], lower), (at["sx"], lower)]
        ):
            made = pltpu.make_async_copy(self.src.at[shard, rows, :], self.mine.at[slot], self.local.at[slot])
            made.start()
            self.near.append(made)

    def second(self):
        at = self.at
        for slot in (1, 3):
            self.near[slot].wait()
            self.out[slot].wait_recv()
            self.hold[slot // 2] = (
                self.mine[slot].astype(F32) + self.got[slot].astype(F32)
            ).astype(BF16)
            made = remote(
                self.hold.at[slot // 2],
                self.last.at[slot // 2],
                self.send.at[4 + slot // 2],
                self.recv.at[4 + slot // 2],
                at["dev_y"] if slot == 1 else at["dev_x"],
            )
            made.start()
            self.out.append(made)

    def third(self):
        half = self.half
        for slot in (0, 2):
            self.near[slot].wait()
            self.out[slot].wait_recv()
            self.out[4 + slot // 2].wait_recv()
            self.dst[pl.ds(slot // 2 * half, half), :] = (
                self.mine[slot].astype(F32) + self.got[slot].astype(F32)
            ) + self.last[slot // 2].astype(F32)

    def finish(self):
        for made in self.out:
            made.wait_send()


def plane_reduce_kernel(*refs, count):
    scratch = refs[2 * count :]
    send, recv, local = scratch[4 * count :]
    at = place()
    meet([at["dev_x"], at["dev_y"]])
    reduces = [
        PlaneReduce(
            refs[k], refs[count + k], *scratch[4 * k : 4 * k + 4], send.at[k], recv.at[k], local.at[k], at
        )
        for k in range(count)
    ]
    for step in ("first", "second", "third", "finish"):
        for reduce in reduces:
            getattr(reduce, step)()


def plane_reduce(arrays, ident):
    if lax.axis_size("shard") != 4:
        return [
            lax.psum_scatter(v, "shard", scatter_dimension=0, tiled=True)[0].astype(F32) for v in arrays
        ]
    count = len(arrays)
    scratch = []
    for array in arrays:
        scratch += PlaneReduce.scratch(array.shape)
    return pl.pallas_call(
        functools.partial(plane_reduce_kernel, count=count),
        out_shape=[jax.ShapeDtypeStruct(v.shape[1:], F32) for v in arrays],
        in_specs=[pl.BlockSpec(memory_space=pl.ANY)] * count,
        out_specs=[pl.BlockSpec(memory_space=pltpu.VMEM)] * count,
        scratch_shapes=scratch
        + [
            pltpu.SemaphoreType.DMA((count, 6)),
            pltpu.SemaphoreType.DMA((count, 6)),
            pltpu.SemaphoreType.DMA((count, 4)),
        ],
        compiler_params=pltpu.CompilerParams(
            collective_id=ident, has_side_effects=True, vmem_limit_bytes=48 << 20
        ),
    )(*arrays)


def on_device(
    inputs,
    cotangent,
    norm_one,
    qkv_weight,
    out_weight,
    norm_two,
    shared_gate,
    shared_up,
    shared_down,
    expert_gate,
    expert_up,
    expert_down,
    gate_weights,
    routes,
    prefix,
):
    length, model_width = inputs.shape
    experts = lax.axis_size("expert") * expert_gate.shape[0]
    shards = lax.axis_size("shard")
    me = lax.axis_index("expert")
    out_low = cotangent.astype(BF16)
    cot_all = lax.all_gather(out_low, "expert", axis=0)

    capacity = 4 * length // experts
    copies = length * TOP
    flat_route = routes.reshape(copies)
    onehot = (flat_route[:, None] == jnp.arange(experts, dtype=jnp.int32)[None, :]).astype(jnp.int32)
    before = (jnp.cumsum(onehot, axis=0) - onehot).reshape(length, TOP, experts)
    onehot = onehot.reshape(length, TOP, experts)
    slot = jnp.sum(onehot * (before + 1), axis=1) - 1
    weight = jnp.sum(onehot.astype(F32) * gate_weights[:, :, None], axis=1)
    table = jnp.stack([slot.astype(F32).T, weight.T], axis=0)
    table_all = lax.all_gather(table, "expert", axis=0)
    table_mine = lax.dynamic_index_in_dim(table_all, me, axis=2, keepdims=False)

    gains = jnp.concatenate(
        [jnp.broadcast_to(norm_one, (32, norm_one.shape[0])), jnp.broadcast_to(norm_two, (32, norm_two.shape[0]))],
        axis=0,
    )
    qkv_full, out_full, gains_full = plane_gather([qkv_weight, out_weight, gains], (0, 0, 0), 1)
    gate_full, up_full, down_full = plane_gather([shared_gate, shared_up, shared_down], (1, 1, 0), 2)
    gains_full = gains_full.reshape(shards, 64, -1).astype(F32)
    gain_one = gains_full[:, 0, :].reshape(model_width)
    gain_two = gains_full[:, 32, :].reshape(model_width)

    inverse_one = lax.rsqrt(jnp.mean(inputs * inputs, axis=-1, keepdims=True) + EPS)
    normed_one = (inputs * inverse_one * gain_one).astype(BF16)
    projected = matmul(normed_one, qkv_full)
    cosine_table, sine_table = rope_tables(length)
    head_shape = (length, HEADS, HEAD_DIM)
    queries = rotate(
        projected[:, :model_width].reshape(head_shape), cosine_table, sine_table
    ).astype(BF16)
    key_rows = rotate(
        projected[:, model_width : 2 * model_width].reshape(head_shape), cosine_table, sine_table
    ).astype(BF16)
    value_rows = projected[:, 2 * model_width :].reshape(head_shape).astype(BF16)
    score_scale = HEAD_DIM ** (-0.5)
    row_pos = lax.broadcasted_iota(jnp.int32, (length, length), 0)
    col_pos = lax.broadcasted_iota(jnp.int32, (length, length), 1)
    visible = (col_pos < prefix[0]) | (col_pos <= row_pos)

    def masked_scores():
        raw_scores = (
            jnp.einsum("qhd,khd->hqk", queries, key_rows, preferred_element_type=F32) * score_scale
        )
        return jnp.where(visible[None], raw_scores, -1e30)

    scores = masked_scores()
    row_peak = jnp.max(scores, axis=-1, keepdims=True)
    exponent = jnp.exp(scores - row_peak)
    expsum = jnp.sum(exponent, axis=-1, keepdims=True)
    logsum = row_peak + jnp.log(expsum)
    probs_low = (exponent / expsum).astype(BF16)
    attended = (
        jnp.einsum("hqk,khd->qhd", probs_low, value_rows, preferred_element_type=F32)
        .reshape(length, model_width)
        .astype(BF16)
    )
    resid = inputs + matmul(attended, out_full)
    inverse_two = lax.rsqrt(jnp.mean(resid * resid, axis=-1, keepdims=True) + EPS)
    normed_two = (resid * inverse_two * gain_two).astype(BF16)
    normed_all = lax.all_gather(normed_two, "expert", axis=0)

    shared_pre = matmul(normed_two, gate_full)
    shared_lift = matmul(normed_two, up_full)
    shared_act, shared_slope = gated_unit(shared_pre)
    shared_hidden = (shared_act * shared_lift).astype(BF16)
    shared_out = matmul(shared_hidden, down_full)
    shared_down_grad = matmul(shared_hidden.T, out_low)
    shared_hgrad = matmul(out_low, down_full.T)
    shared_pre_grad = (shared_hgrad * shared_lift * shared_slope).astype(BF16)
    shared_lift_grad = (shared_hgrad * shared_act).astype(BF16)
    shared_gate_grad = matmul(normed_two.T, shared_pre_grad)
    shared_up_grad = matmul(normed_two.T, shared_lift_grad)
    shared_back = matmul(shared_pre_grad, gate_full.T) + matmul(shared_lift_grad, up_full.T)

    pick = (
        jnp.arange(capacity, dtype=F32)[None, :, None] == table_mine[:, 0][:, None, :]
    ).astype(BF16)
    weight_rows = jnp.sum(pick.astype(F32) * table_mine[:, 1][:, None, :], axis=2)

    def to_rows(values):
        return jnp.einsum("ect,etd->ecd", pick, values, preferred_element_type=F32)

    def to_tokens(rows):
        return jnp.einsum("ect,ecd->etd", pick, rows, preferred_element_type=F32)

    gate_local, up_local, down_local = expert_gate[0], expert_up[0], expert_down[0]
    row_count = experts * capacity
    rows = to_rows(normed_all).astype(BF16).reshape(row_count, model_width)
    cot_rows = to_rows(cot_all)
    grad_rows = (cot_rows * weight_rows[:, :, None]).astype(BF16).reshape(row_count, model_width)
    pre_gate = matmul(rows, gate_local)
    pre_up = matmul(rows, up_local)
    activated, derivative = gated_unit(pre_gate)
    hidden = (activated * pre_up).astype(BF16)
    hidden_grad = matmul(grad_rows, down_local.T)
    gate_pre_grad = (hidden_grad * pre_up * derivative).astype(BF16)
    up_pre_grad = (hidden_grad * activated).astype(BF16)
    row_grad = (matmul(gate_pre_grad, gate_local.T) + matmul(up_pre_grad, up_local.T)).astype(BF16)
    back_part = to_tokens(row_grad.reshape(experts, capacity, model_width)).astype(BF16)
    back = lax.psum_scatter(back_part, "expert", scatter_dimension=0, tiled=False).astype(F32)

    result = matmul(hidden, down_local).astype(BF16).reshape(experts, capacity, model_width)
    weighted = (result.astype(F32) * weight_rows[:, :, None]).astype(BF16)
    mix_part = to_tokens(weighted).astype(BF16)
    mixture = lax.psum_scatter(mix_part, "expert", scatter_dimension=0, tiled=False).astype(F32)
    weight_dot = jnp.sum(result.astype(F32) * cot_rows, axis=2)
    weight_back = jnp.einsum("ect,ec->et", pick.astype(F32), weight_dot, precision=lax.Precision.HIGHEST)
    weight_got = lax.all_to_all(weight_back, "expert", split_axis=0, concat_axis=0, tiled=True)
    gate_weights_grad = jnp.sum(onehot.astype(F32) * weight_got.T[:, None, :], axis=2)

    def blocks_of_columns(value):
        width = value.shape[1] // shards
        return value.astype(BF16).reshape(value.shape[0], shards, width).transpose(1, 0, 2)

    def blocks_of_rows(value):
        return value.astype(BF16).reshape(shards, value.shape[0] // shards, value.shape[1])

    gate_term = matmul(rows.T, gate_pre_grad)
    up_term = matmul(rows.T, up_pre_grad)
    down_term = matmul(hidden.T, grad_rows)
    expert_gate_grad, expert_up_grad, expert_down_grad = plane_reduce(
        [blocks_of_columns(gate_term), blocks_of_columns(up_term), blocks_of_rows(down_term)], 3
    )

    output = resid + mixture + shared_out
    normed_two_grad = shared_back + back
    gain_two_grad, resid_extra = norm_back(resid, inverse_two, gain_two, normed_two_grad)
    resid_grad = cotangent + resid_extra
    attn_low = resid_grad.astype(BF16)
    out_weight_grad = matmul(attended.T, attn_low)
    attended_grad = matmul(attn_low, out_full.T).astype(BF16).reshape(head_shape)
    scores = masked_scores()
    probs_full = jnp.exp(scores - logsum)
    value_grad = jnp.einsum(
        "hqk,qhd->khd", probs_full.astype(BF16), attended_grad, preferred_element_type=F32
    )
    probs_grad = jnp.einsum("qhd,khd->hqk", attended_grad, value_rows, preferred_element_type=F32)
    score_grad = (
        probs_full * (probs_grad - jnp.sum(probs_full * probs_grad, axis=-1, keepdims=True))
    ).astype(BF16)
    query_grad = (
        jnp.einsum("hqk,khd->qhd", score_grad, key_rows, preferred_element_type=F32) * score_scale
    )
    key_grad = (
        jnp.einsum("hqk,qhd->khd", score_grad, queries, preferred_element_type=F32) * score_scale
    )
    projected_grad = jnp.concatenate(
        [
            rotate(query_grad, cosine_table, -sine_table).reshape(length, model_width),
            rotate(key_grad, cosine_table, -sine_table).reshape(length, model_width),
            value_grad.reshape(length, model_width),
        ],
        axis=1,
    ).astype(BF16)
    qkv_weight_grad = matmul(normed_one.T, projected_grad)
    normed_one_grad = matmul(projected_grad, qkv_full.T)
    gain_one_grad, input_extra = norm_back(inputs, inverse_one, gain_one, normed_one_grad)
    input_grad = resid_grad + input_extra

    gain_block = jnp.zeros((shards, 32, model_width // shards), BF16)
    gain_block = gain_block.at[:, 0, :].set(gain_one_grad.astype(BF16).reshape(shards, -1))
    gain_block = gain_block.at[:, 1, :].set(gain_two_grad.astype(BF16).reshape(shards, -1))
    pieces = plane_reduce(
        [
            blocks_of_rows(qkv_weight_grad),
            blocks_of_rows(out_weight_grad),
            gain_block,
            blocks_of_columns(shared_gate_grad),
            blocks_of_columns(shared_up_grad),
            blocks_of_rows(shared_down_grad),
        ],
        4,
    )
    summed = [lax.psum(v.astype(BF16), "expert").astype(F32) for v in pieces]
    return (
        output,
        input_grad,
        summed[2][0],
        summed[0],
        summed[1],
        summed[2][1],
        summed[3],
        summed[4],
        summed[5],
        expert_gate_grad[None],
        expert_up_grad[None],
        expert_down_grad[None],
        gate_weights_grad,
    )


def solution(mesh):
    tokens = P(("expert", "shard"), None)
    in_specs = (
        tokens,
        tokens,
        P("shard"),
        P("shard", None),
        P("shard", None),
        P("shard"),
        P(None, "shard"),
        P(None, "shard"),
        P("shard", None),
        P("expert", None, None),
        P("expert", None, None),
        P("expert", None, None),
        tokens,
        tokens,
        P(("expert", "shard")),
    )
    out_specs = (
        tokens,
        tokens,
        P("shard"),
        P("shard", None),
        P("shard", None),
        P("shard"),
        P(None, "shard"),
        P(None, "shard"),
        P("shard", None),
        P("expert", None, "shard"),
        P("expert", None, "shard"),
        P("expert", "shard", None),
        tokens,
    )
    return jax.shard_map(
        on_device, mesh=mesh, in_specs=in_specs, out_specs=out_specs, check_vma=False
    )
```

time: 845 us -> 788 us (0.933)
  waiting for transfers between devices: 382 us -> 80.1 us
  Pallas kernels: 0 us -> 268 us
  local copies, waits for them, and re-layouts: 96.1 us -> 79.3 us
  starting transfers between devices: 19.1 us -> 3.79 us
  blocking collectives: 33.4 us -> 42.6 us
    pallas_call x0 -> x4, Pallas kernels: none -> 268 us  [the longest x2 199 us: plane_reduce(): pl.pallas_call(functools.partial(plane_reduce_kernel, count=count), out_s...]
    all_to_all x4 -> x1, waiting for transfers between devices: 184 us -> 0.01 us  [on_device(): lax.all_to_all(weight_back, 'expert', split_axis=0, concat_axis=0, tiled=...]
    psum x1, waiting for transfers between devices: 85.9 us -> 0.01 us  [on_device(): summed = [lax.psum(v.astype(BF16), 'expert').astype(F32) for v in pieces]]
    gather x4 -> x0, local copies, waits for them, and re-layouts: 34.1 us -> none  [the longest x2 23 us: place_rows(): return padded[index].reshape(experts, capacity, model_width)]
    unnamed x2 -> x0, blocking collectives: 19.8 us -> none
    all_gather x5 -> x2, waiting for transfers between devices: 97.7 us -> 80 us  [the longest x1 49.1 us: on_device(): cot_all = lax.all_gather(out_low, 'expert', axis=0)]
    dot_general x4 -> x9, matrix products: 14.9 us -> 31.4 us  [the longest x2 13.5 us: to_rows(): return jnp.einsum('ect,etd->ecd', pick, values, preferred_element_type=F32)]
    all_gather x0 -> x1, blocking collectives: none -> 15.5 us  [on_device(): table_all = lax.all_gather(table, 'expert', axis=0)]
  transfers between devices with their start and end apart: 18 -> 6, of which waited for: 8 -> 2; matrix products, arithmetic and copies ran while one was open for 43% -> 28% of each run, Pallas kernels for 0% -> 31%
where the time goes in v1:
time: 788 us; the launch traced here: 778 us
  Pallas kernels  268 us (34%)
  matrix products  224 us (28%)
  waiting for transfers between devices  80.1 us (10%)
  local copies, waits for them, and re-layouts  79.3 us (10%)
  other arithmetic  63.9 us (8%)
  blocking collectives  42.6 us (5%)
  between operations  16 us (2%)
    pallas_call x2, Pallas kernels, plane_reduce(): pl.pallas_call(functools.partial(plane_reduce_kernel, count=count), out_s...  199 us
    dot_general x24, matrix products, matmul(): return jnp.dot(left, right, preferred_element_type=jnp.float32)  176 us
    pallas_call x2, Pallas kernels, plane_gather(): pl.pallas_call(functools.partial(plane_gather_kernel, axes=axes), out_sha...  69.1 us
    all_gather x1, waiting for transfers between devices, on_device(): cot_all = lax.all_gather(out_low, 'expert', axis=0)  49.1 us
    all_gather x1, waiting for transfers between devices, on_device(): normed_all = lax.all_gather(normed_two, 'expert', axis=0)  30.9 us
    unnamed x191, local copies, waits for them, and re-layouts  28.8 us
    psum x1, blocking collectives, on_device(): summed = [lax.psum(v.astype(BF16), 'expert').astype(F32) for v in pieces]  27.1 us
  transfers between devices with their start and end apart: 6, of which 2 were waited for; matrix products, arithmetic and copies ran while one was open for 28% of the time, Pallas kernels for 31%

profile of v1, /device:TPU:0, one launch (start us, length us, event | category | flops | bytes accessed | tf_op | source)
XLA Modules:
  0.0 777.8 jit_solution(4044730121689437696)
XLA Ops:
  10.9 25.7 %shard_map.246 = (bf16[768,2304]{1,0:T(8,128)(2,1)S(1)}, bf16[768,768]{1,0:T(8,128)(2,1)S(1)}, bf16[256,192]{1,0:T(8,128)(2,1)S(1)}) custom-call(bf16[192,2304]{1,0:T(8,128)(2,1)S(1)} %copy-done.11, bf16[192,768]{1,0:T(8,128)(2,1)S(1)} %copy-done.15, bf16[64,192]{1,0:T(8,128)(2,1)S(1)} %pad_maximum_fusion.11.refs_2_), custom_call_target="tpu_custom_call" | custom-call | tf_op jit(solution)/shard_map/pallas_call | solution.py:172
  41.9 4.5 fusion.68
  49.3 3.0 copy.101
  52.3 3.0 copy.102
  68.6 4.9 fusion.47
  92.7 4.6 multiply_reduce_fusion.9
  98.3 15.5 %all-gather = f32[16,8,512]{2,1,0:T(8,128)S(1)} all-gather(f32[2,8,512]{2,1,0:T(8,128)S(1)} %pad_maximum_fusion.12), channel_id=2, replica_groups=mesh['expert'=8,'shard'=4] {'expert'}, dimensions={0}, use_global_device_ids=true | all-gather | bytes 294912 | tf_op jit(solution)/shard_map/all_gather | solution.py:338
  115.2 30.9 %all-gather.6.cloned.1.call-done = bf16[4096,768]{1,0:T(8,128)(2,1)} async-done(((bf16[512,768]{1,0:T(8,128)(2,1)}), bf16[4096,768]{1,0:T(8,128)(2,1)}) %all-gather.6.cloned.1.call-update) | async-done | bytes 6291472 | tf_op jit(solution)/shard_map/all_gather | solution.py:388
  146.0 5.4 fusion.37
  153.1 9.5 %fusion.28 = f32[2048,2048]{1,0:T(8,128)} fusion(bf16[2048,768]{1,0:T(8,128)(2,1)S(1)} %bitcast.210, bf16[1,768,2048]{2,1,0:T(8,128)(2,1)S(1)} %copy-done.80), kind=kOutput, calls=%fused_computation.54 | convolution fusion | flops 6442450944 | bytes 23068672 | tf_op jit(solution)/shard_map/dot_general | solution.py:56
  162.6 49.1 %all-gather.8.cloned.1.call-done = bf16[4096,768]{1,0:T(8,128)(2,1)} async-done(((bf16[512,768]{1,0:T(8,128)(2,1)}), bf16[4096,768]{1,0:T(8,128)(2,1)}) %all-gather.8.cloned.1.call-update) | async-done | bytes 6291472 | tf_op jit(solution)/shard_map/all_gather | solution.py:327
  211.7 8.1 %multiply_convert_fusion.4 = (bf16[8,256,768]{2,1,0:T(8,128)(2,1)S(1)}, f32[8,256,768]{2,1,0:T(8,128)}) fusion(f32[8,256]{1,0:T(8,128)S(1)} %multiply_reduce_fusion.1, bf16[8,512,768]{2,1,0:T(8,128)(2,1)} %bitcast.174, f32[8,512]{1,0:T(8,128)S(1)} %bitcast.191), kind=kOutput, calls=%fused_computation.20 | convolution fusion | flops 1614807040 | bytes 15753216 | tf_op jit(solution)/shard_map/ect,etd->ecd/dot_general | solution.py:409
  221.5 9.6 %fusion.23 = f32[2048,2048]{1,0:T(8,128)} fusion(bf16[2048,768]{1,0:T(8,128)(2,1)S(1)} %bitcast.186, bf16[1,2048,768]{2,1,0:T(8,128)(2,1)S(1)} %copy-done.81), kind=kOutput, calls=%fused_computation.49 | convolution fusion | flops 6442450944 | bytes 23068672 | tf_op jit(solution)/shard_map/dot_general | solution.py:56
  231.1 26.2 %multiply_convert_fusion.1 = (bf16[2048,2048]{1,0:T(8,128)(2,1)}, bf16[2048,2048]{1,0:T(8,128)(2,1)}, bf16[2048,2048]{1,0:T(8,128)(2,1)}) fusion(f32[2048,2048]{1,0:T(8,128)} %fusion.23, f32[2048,2048]{1,0:T(8,128)} %fusion.28, bf16[2048,768]{1,0:T(8,128)(2,1)} %bitcast.211, bf16[1,768,2048]{2,1,0:T(8,128)(2,1)S(1)} %copy-done), kind=kOutput, calls=%fused_computation.1 | convolution fusion | flops 6505365504 | bytes 65011712 | tf_op jit(solution)/shard_map/dot_general | solution.py:56
  257.3 22.1 %fusion.26 = f32[2048,768]{1,0:T(8,128)S(1)} fusion(bf16[2048,2048]{1,0:T(8,128)(2,1)} %get-tuple-element.105, bf16[1,768,2048]{2,1,0:T(8,128)(2,1)} %param.29), kind=kOutput, calls=%fused_computation.52 | convolution fusion | flops 6442450944 | bytes 17825792 | tf_op jit(solution)/shard_map/dot_general | solution.py:56
  279.5 6.9 add_convert_fusion
  286.4 3.8 fusion.21
  291.8 43.4 %shard_map.247 = (bf16[768,2048]{1,0:T(8,128)(2,1)S(1)}, bf16[768,2048]{1,0:T(8,128)(2,1)S(1)}, bf16[2048,768]{1,0:T(8,128)(2,1)S(1)}) custom-call(bf16[768,512]{1,0:T(8,128)(2,1)S(1)} %copy-done.12, bf16[768,512]{1,0:T(8,128)(2,1)S(1)} %copy-done.13, bf16[512,768]{1,0:T(8,128)(2,1)S(1)} %copy-done.14), custom_call_target="tpu_custom_call" | custom-call | tf_op jit(solution)/shard_map/pallas_call | solution.py:172
  339.8 4.9 fusion.12
  346.0 3.5 convolution_convert_fusion.6
  349.5 3.2 copy.120
  355.5 5.4 convolution_convert_fusion.5
  360.9 3.2 copy.122
  367.0 5.4 convolution_convert_fusion.4
  372.4 9.4 %convolution_convert_fusion.3 = bf16[2048,768]{1,0:T(8,128)(2,1)S(1)} fusion(bf16[2048,2048]{1,0:T(8,128)(2,1)} %get-tuple-element.106, bf16[1,2048,768]{2,1,0:T(8,128)(2,1)S(1)} %copy-done.82), kind=kOutput, calls=%fused_computation.44 | convolution fusion | flops 6444023808 | bytes 14680064 | tf_op jit(solution)/shard_map/dot_general | solution.py:56
  381.8 3.9 fusion.20
  387.6 4.7 fusion.74
  392.3 3.6 fusion.4
  398.4 3.3 all-to-all-start
  401.8 12.4 %convolution_convert_fusion.2 = bf16[768,2048]{1,0:T(8,128)(2,1)} fusion(bf16[2048,768]{1,0:T(8,128)(2,1)} %bitcast.212, bf16[2048,2048]{1,0:T(8,128)(2,1)} %get-tuple-element.104), kind=kOutput, calls=%fused_computation.43 | convolution fusion | flops 6444023808 | bytes 14680064 | tf_op jit(solution)/shard_map/dot_general | solution.py:56
  414.3 10.8 %convolution_convert_fusion.7 = bf16[2048,768]{1,0:T(8,128)(2,1)} fusion(bf16[2048,2048]{1,0:T(8,128)(2,1)} %get-tuple-element.106, bf16[2048,768]{1,0:T(8,128)(2,1)S(1)} %bitcast.187), kind=kOutput, calls=%fused_computation.48 | convolution fusion | flops 6444023808 | bytes 14680064 | tf_op jit(solution)/shard_map/dot_general | solution.py:56
  425.1 5.1 multiply_reduce_fusion.2
  434.8 11.4 %multiply_reduce_fusion = (f32[12,512]{1,0:T(8,128)S(1)}, f32[12,512,512]{1,2,0:T(8,128)}) fusion(f32[12,512]{1,0:T(8,128)S(1)} %log_add_fusion, f32[12,512,512]{1,2,0:T(8,128)} %copy-done.24, pred[512,512]{0,1:T(8,128)(4,1)S(1)} %copy-done.35, bf16[512,12,64]{0,2,1:T(8,128)(2,1)S(1)} %bitcast.180, bf16[512,12,64]{0,2,1:T(8,128)(2,1)} %bitcast.179), kind=kOutput, calls=%fused_computation.6 | convolution fusion | flops 418375680 | bytes 27049984 | tf_op jit(solution)/shard_map/qhd,khd->hqk/dot_general | solution.py:465
  448.1 7.3 multiply_convert_fusion.3
  459.8 3.2 fusion.44
  463.0 3.3 multiply_reduce_fusion.3
  469.0 5.4 convolution_convert_fusion
  474.4 120.3 %shard_map.248 = (f32[192,2304]{1,0:T(8,128)}, f32[192,768]{1,0:T(8,128)S(1)}, f32[32,192]{1,0:T(8,128)S(1)}, f32[768,512]{1,0:T(8,128)S(1)}, f32[768,512]{1,0:T(8,128)S(1)}, /*index=5*/f32[512,768]{1,0:T(8,128)}) custom-call(bf16[4,192,2304]{2,1,0:T(8,128)(2,1)} %bitcast.177, bf16[4,192,768]{2,1,0:T(8,128)(2,1)S(1)} %bitcast.157, ...), custom_call_target="tpu_custom_call" | custom-call | tf_op jit(solution)/shard_map/pallas_call | solution.py:288
  601.0 12.0 %convolution_convert_fusion.1 = bf16[768,2048]{1,0:T(8,128)(2,1)} fusion(bf16[2048,768]{1,0:T(8,128)(2,1)} %bitcast.213, bf16[2048,2048]{1,0:T(8,128)(2,1)} %get-tuple-element.105), kind=kOutput, calls=%fused_computation.42 | convolution fusion | flops 6444023808 | bytes 14680064 | tf_op jit(solution)/shard_map/dot_general | solution.py:56
  613.0 4.7 copy.124
  617.7 4.7 copy.125
  622.4 4.7 copy.126
  627.0 4.7 copy.127
  631.7 78.9 %shard_map.249 = (f32[768,512]{1,0:T(8,128)S(1)}, f32[768,512]{1,0:T(8,128)S(1)}, f32[512,768]{1,0:T(8,128)S(1)}) custom-call(bf16[4,768,512]{2,1,0:T(8,128)(2,1)} %bitcast.171, bf16[4,768,512]{2,1,0:T(8,128)(2,1)} %bitcast.172, bf16[4,512,768]{2,1,0:T(8,128)(2,1)} %bitcast.185), custom_call_target="tpu_custom_call" | custom-call | tf_op jit(solution)/shard_map/pallas_call | solution.py:288
  714.3 7.3 multiply_reduce_fusion.8
  722.3 27.1 %psum.42 = bf16[32,192]{1,0:T(8,128)(2,1)S(1)} all-reduce(bf16[32,192]{1,0:T(8,128)(2,1)S(1)} %convert_element_type.269), channel_id=1, replica_groups=mesh['expert'=8,'shard'=4] {'expert'}, use_global_device_ids=true, to_apply=%region_16.17 | all-reduce | flops 6144 | bytes 24576 | tf_op jit(solution)/shard_map/psum | solution.py:502
  750.0 4.0 subtract_add_fusion
  754.1 5.2 fusion.43
  (281 shorter events, 102.7 us)
Async XLA Ops:
  7.2 223.9 %copy-start = (bf16[1,768,2048]{2,1,0:T(8,128)(2,1)S(1)}, bf16[1,768,2048]{2,1,0:T(8,128)(2,1)}, u32[]{:S(2)}) copy-start(bf16[1,768,2048]{2,1,0:T(8,128)(2,1)} %param.28) | copy-start | bytes 9437188
  7.2 138.8 %all-gather.6.cloned.1.call-start = ((), (), s32[]{:S(2)}) async-start(), calls=%async_computation.5 | async-start | bytes 7077888 | tf_op jit(solution)/shard_map/all_gather | solution.py:388
  39.7 6.7 copy-start.72
  41.9 4.5 copy-start.75
  56.3 5.6 copy-start.60
  57.1 9.6 %copy-start.34 = (pred[512,512]{0,1:T(8,128)(4,1)}, pred[512,512]{0,1:T(8,128)(4,1)S(1)}, u32[]{:S(2)}) copy-start(pred[512,512]{0,1:T(8,128)(4,1)S(1)} %fusion.48) | copy-start | bytes 786436
  64.1 4.5 copy-start.24
  64.1 4.6 copy-start.64
  66.7 6.9 copy-start.66
  68.6 4.9 copy-start.9
  68.6 4.9 copy-start.28
  76.1 5.3 copy-start.70
  76.2 5.2 copy-start.68
  76.2 5.3 copy-start.78
  78.8 133.0 %all-gather.8.cloned.1.call-start = ((), (), s32[]{:S(2)}) async-start(), calls=%async_computation.6 | async-start | bytes 7077888 | tf_op jit(solution)/shard_map/all_gather | solution.py:327
  81.4 10.4 %copy-start.79 = (f32[512,2]{0,1:T(2,128)S(1)}, f32[512,2]{0,1:T(2,128)}, u32[]{:S(2)}) copy-start(f32[512,2]{0,1:T(2,128)} %param.31) | copy-start | bytes 12292
  81.5 343.6 %reduce-scatter.5.cloned.1.call-start = ((), (), s32[]{:S(2)}) async-start(), calls=%async_computation.4 | async-start | bytes 7077888 | tf_op jit(solution)/shard_map/reduce_scatter | solution.py:428
  81.7 69.7 %copy-start.31 = (s32[512,2]{1,0:T(8,128)}, s32[512,2]{1,0:T(8,128)S(1)}, u32[]{:S(2)}) copy-start(s32[512,2]{1,0:T(8,128)S(1)} %copy.104) | copy-start | bytes 12292
  146.0 7.0 copy-start.80
  211.7 9.8 %copy-start.81 = (bf16[1,2048,768]{2,1,0:T(8,128)(2,1)S(1)}, bf16[1,2048,768]{2,1,0:T(8,128)(2,1)}, u32[]{:S(2)}) copy-start(bf16[1,2048,768]{2,1,0:T(8,128)(2,1)} %param.30) | copy-start | bytes 9437188
  257.3 22.1 %copy-start.87 = (bf16[2048,2048]{1,0:T(8,128)(2,1)S(1)}, bf16[2048,2048]{1,0:T(8,128)(2,1)}, u32[]{:S(2)}) copy-start(bf16[2048,2048]{1,0:T(8,128)(2,1)} %get-tuple-element.104) | copy-start | bytes 25165828
  290.2 45.1 %copy-start.40 = (bf16[512,768]{1,0:T(8,128)(2,1)S(1)}, bf16[512,768]{1,0:T(8,128)(2,1)}, u32[]{:S(2)}) copy-start(bf16[512,768]{1,0:T(8,128)(2,1)} %multiply_convert_fusion.6) | copy-start | bytes 2359300
  290.2 463.8 %reduce-scatter.3.cloned.1.call-start = ((), (), s32[]{:S(2)}) async-start(), calls=%async_computation.3 | async-start | bytes 7077888 | tf_op jit(solution)/shard_map/reduce_scatter | solution.py:433
  335.2 4.5 copy-start.18
  367.0 5.4 copy-start.82
  387.6 4.7 copy-start.26
  398.4 315.7 %all-to-all-start = ((f32[8,1,512]{2,1,0:T(1,128)}), f32[8,1,512]{2,1,0:T(1,128)S(1)}, u32[]{:S(2)}, u32[]{:S(2)}) async-start(f32[8,1,512]{2,1,0:T(1,128)} %all_to_all.8), calls=%async_computation.2 | async-start | bytes 32768 | tf_op jit(solution)/shard_map/all_to_all | solution.py:436
  401.8 357.5 %all-reduce.4.cloned.1.call-start = ((), (), s32[]{:S(2)}) async-start(), calls=%async_computation.7 | async-start | bytes 7077888 | tf_op jit(solution)/shard_map/psum | solution.py:502
  401.8 12.5 %copy-start.43 = (bf16[8,256,768]{2,1,0:T(8,128)(2,1)S(1)}, bf16[8,256,768]{2,1,0:T(8,128)(2,1)}, u32[]{:S(2)}) copy-start(bf16[8,256,768]{2,1,0:T(8,128)(2,1)} %copy-done.42) | copy-start | bytes 9437188
  414.3 10.8 %copy-start.21 = (bf16[768,2048]{1,0:T(8,128)(2,1)S(1)}, bf16[768,2048]{1,0:T(8,128)(2,1)}, u32[]{:S(2)}) copy-start(bf16[768,2048]{1,0:T(8,128)(2,1)} %copy-done.20) | copy-start | bytes 9437188
  414.3 10.8 %copy-start.69 = (f32[768]{0:T(1024)S(1)}, f32[768]{0:T(1024)}, u32[]{:S(2)}) copy-start(f32[768]{0:T(1024)} %copy-done.68) | copy-start | bytes 9220
  414.3 10.8 %copy-start.71 = (f32[512]{0:T(512)S(1)}, f32[512]{0:T(512)}, u32[]{:S(2)}) copy-start(f32[512]{0:T(512)} %copy-done.70) | copy-start | bytes 6148
  425.1 5.2 copy-start.77
  425.1 5.2 copy-start.30
  425.1 5.2 copy-start.33
  431.6 14.5 %copy-start.27 = (f32[512,768]{1,0:T(8,128)}, f32[512,768]{1,0:T(8,128)S(1)}, u32[]{:S(2)}) copy-start(f32[512,768]{1,0:T(8,128)S(1)} %subtract_add_fusion.1) | copy-start | bytes 4718596
  434.7 11.4 %copy-start.36 = (bf16[512,768]{0,1:T(8,128)(2,1)}, bf16[512,768]{0,1:T(8,128)(2,1)S(1)}, u32[]{:S(2)}) copy-start(bf16[512,768]{0,1:T(8,128)(2,1)S(1)} %copy.114) | copy-start | bytes 2359300
  434.7 11.4 %slice-start = ((s8[12582912]{0:T(1024)(128)(4,1)}), s8[4194304]{0:T(1024)(128)(4,1)S(1)}, s32[]{:S(2)}) async-start(s8[12582912]{0:T(1024)(128)(4,1)} %bitcast.161), calls=%async_computation.8 | async-start | bytes 8388608
  434.7 11.4 %slice-start.1 = ((s8[12582912]{0:T(1024)(128)(4,1)}), s8[4194304]{0:T(1024)(128)(4,1)S(1)}, s32[]{:S(2)}) async-start(s8[12582912]{0:T(1024)(128)(4,1)} %bitcast.161), calls=%async_computation.9 | async-start | bytes 8388608
  434.7 13.3 %slice-start.2 = ((s8[12582912]{0:T(1024)(128)(4,1)}), s8[4194304]{0:T(1024)(128)(4,1)S(1)}, s32[]{:S(2)}) async-start(s8[12582912]{0:T(1024)(128)(4,1)} %bitcast.161), calls=%async_computation.10 | async-start | bytes 8388608
  448.1 7.3 copy-start.45
  448.1 7.3 copy-start.47
  594.7 4.6 copy-start.48
  631.7 82.6 %copy-start.32 = (s32[512,2]{1,0:T(8,128)S(1)}, s32[512,2]{1,0:T(8,128)}, u32[]{:S(2)}) copy-start(s32[512,2]{1,0:T(8,128)} %copy-done.31) | copy-start | bytes 12292
  631.7 118.3 %copy-start.74 = (f32[512]{0:T(512)S(1)}, f32[512]{0:T(512)}, u32[]{:S(2)}) copy-start(f32[512]{0:T(512)} %get-tuple-element.128) | copy-start | bytes 6148
  750.0 4.0 copy-start.19
  759.2 5.4 copy-start.53
  766.7 4.1 copy-start.1
  (49 other events, 107.0 us)
Sparse Core Ops, SparseCore 0:
  78.9 67.1 all-gather.5
  148.2 63.4 all-gather.7
  290.3 68.4 reduce-scatter.4
  385.8 67.8 reduce-scatter.2
  601.1 85.6 all-reduce.3

commit v2 on v1

--- a/solution.py
+++ b/solution.py
@@ -70,6 +70,8 @@
         dev_x=(expert, 2 * y + 1 - x),
         dev_y=(expert, 2 * (1 - y) + x),
         dev_c=(expert + 1 - 2 * core, shard),
+        dev_left=(expert - 2, shard),
+        dev_right=(expert + 2, shard),
     )
 
 
@@ -302,6 +304,314 @@
     )(*arrays)
 
 
+class ChainGather:
+    @staticmethod
+    def copies(chips):
+        return 4 * chips
+
+    def __init__(self, src, dst, send, recv, local, at, chips):
+        self.src, self.dst, self.send, self.recv, self.local = src, dst, send, recv, local
+        self.at, self.chips = at, chips
+
+    def copy(self, block, index, device, first=False):
+        part = self.dst.at[block]
+        return remote(
+            self.src if first else part, part, self.send.at[index], self.recv.at[index], self.at[device]
+        )
+
+    def right(self, step):
+        at = self.at
+        return self.copy((at["z"] - step + 1) * 2 + at["core"], step - 1, "dev_right", step == 1)
+
+    def left(self, step):
+        at = self.at
+        return self.copy(
+            (at["z"] + step - 1) * 2 + at["core"], self.chips + step - 1, "dev_left", step == 1
+        )
+
+    def over(self, step):
+        at = self.at
+        return self.copy(
+            (at["z"] - step) * 2 + at["core"], (2 if step >= 0 else 3) * self.chips + abs(step), "dev_c", step == 0
+        )
+
+    def arrived(self, step, side):
+        at = self.at
+        if side == "left":
+            return self.copy((at["z"] - step) * 2 + at["core"], step - 1, "dev_right")
+        return self.copy((at["z"] + step) * 2 + at["core"], self.chips + step - 1, "dev_left")
+
+    def start(self):
+        at = self.at
+        pl.when(at["z"] < self.chips - 1)(lambda: self.right(1).start())
+        pl.when(at["z"] > 0)(lambda: self.left(1).start())
+        self.over(0).start()
+        self.own = pltpu.make_async_copy(self.src, self.dst.at[at["expert"]], self.local)
+        self.own.start()
+
+    def step(self, step):
+        at, chips = self.at, self.chips
+
+        @pl.when(at["z"] - step >= 0)
+        def _():
+            self.arrived(step, "left").wait_recv()
+            if step < chips - 1:
+                pl.when(at["z"] < chips - 1)(lambda: self.right(step + 1).start())
+            self.over(step).start()
+
+        @pl.when(at["z"] + step < chips)
+        def _():
+            self.arrived(step, "right").wait_recv()
+            if step < chips - 1:
+                pl.when(at["z"] > 0)(lambda: self.left(step + 1).start())
+            self.over(-step).start()
+
+    def finish(self, step):
+        at = self.at
+        if step == 0:
+            self.over(0).wait()
+            self.own.wait()
+            return
+        pl.when(at["z"] - step >= 0)(lambda: self.over(step).wait())
+        pl.when(at["z"] + step < self.chips)(lambda: self.over(-step).wait())
+
+    def sent(self):
+        at, chips = self.at, self.chips
+        for step in range(1, chips):
+            pl.when((at["z"] - step + 1 >= 0) & (at["z"] < chips - 1))(lambda: self.right(step).wait_send())
+            pl.when((at["z"] + step - 1 < chips) & (at["z"] > 0))(lambda: self.left(step).wait_send())
+
+
+def chain_meet(at, chips, others):
+    barrier = pltpu.get_barrier_semaphore()
+    for device in others:
+        pl.semaphore_signal(barrier, inc=1, device_id=device, device_id_type=MESH)
+
+    @pl.when(at["z"] > 0)
+    def _():
+        pl.semaphore_signal(barrier, inc=1, device_id=at["dev_left"], device_id_type=MESH)
+
+    @pl.when(at["z"] < chips - 1)
+    def _():
+        pl.semaphore_signal(barrier, inc=1, device_id=at["dev_right"], device_id_type=MESH)
+
+    ends = jnp.where(at["z"] == 0, 1, 0) + jnp.where(at["z"] == chips - 1, 1, 0)
+    pl.semaphore_wait(barrier, len(others) + 2 - ends)
+
+
+def dot_nn(left, right):
+    return lax.dot_general(left, right, (((1,), (0,)), ((), ())), preferred_element_type=F32)
+
+
+def dot_nt(left, right):
+    return lax.dot_general(left, right, (((1,), (1,)), ((), ())), preferred_element_type=F32)
+
+
+def dot_tn(left, right):
+    return lax.dot_general(left, right, (((0,), (0,)), ((), ())), preferred_element_type=F32)
+
+
+def columns(start, count):
+    return pl.ds(pl.multiple_of(start, 128), count)
+
+
+def rope_lanes(length):
+    half = HEAD_DIM // 2
+    frequency = 10000.0 ** (-jnp.arange(half, dtype=F32) * 2.0 / HEAD_DIM)
+    angles = jnp.arange(length, dtype=F32)[:, None] * frequency[None, :]
+    cosine, sine = jnp.cos(angles), jnp.sin(angles)
+    return jnp.concatenate([cosine] * 4, axis=1), jnp.concatenate([-sine, sine] * 2, axis=1)
+
+
+def partner(values):
+    lane = lax.broadcasted_iota(jnp.int32, values.shape, 1)
+    half = HEAD_DIM // 2
+    ahead = pltpu.roll(values, 128 - half, 1)
+    behind = pltpu.roll(values, half, 1)
+    return jnp.where(lane % HEAD_DIM < half, ahead, behind)
+
+
+def front_kernel(*refs, plane, chips):
+    (prefix, x_ref, cot_ref, route_ref, weight_ref, cos_ref, sin_ref), refs = refs[:7], refs[7:]
+    if plane:
+        (qkv_part, out_part, gains_part, sg, su, sd), refs = refs[:6], refs[6:]
+    else:
+        (qkv_full, out_full, gains_full), refs = refs[:3], refs[3:]
+    (cot_all, table_all, h1_ref, rot_ref, att_ref, lse_ref, resid_ref, h2_ref, cot_low), refs = refs[:9], refs[9:]
+    if plane:
+        (qkv_full, out_full, gains_full, sg_full, su_full, sd_full), refs = refs[:6], refs[6:]
+    bias_ref, table_ref, chain_send, chain_recv, chain_local = refs[:5]
+    length, width = x_ref.shape
+    experts = table_ref.shape[0] // 2
+    at = place()
+    chain_meet(at, chips, [at["dev_x"], at["dev_y"], at["dev_c"]] if plane else [at["dev_c"]])
+    if plane:
+        send, recv, local = refs[5:8]
+        parts = [(qkv_part, qkv_full), (out_part, out_full), (gains_part, gains_full)]
+        shared = [(sg, sg_full), (su, su_full), (sd, sd_full)]
+        gathers = [
+            PlaneGather(a, b, 0, send.at[k], recv.at[k], local.at[k], at) for k, (a, b) in enumerate(parts + shared)
+        ]
+        first, later = gathers[2::-1], gathers[3:]
+        for gather in first:
+            gather.first()
+    cot_low[...] = cot_ref[...].astype(BF16)
+    names = lax.broadcasted_iota(jnp.int32, (experts, length), 0)
+    chosen = [route_ref[pl.ds(k, 1), :] == names for k in range(TOP)]
+    member = (chosen[0] | chosen[1]).astype(F32)
+    earlier = (
+        lax.broadcasted_iota(jnp.int32, (length, length), 0)
+        < lax.broadcasted_iota(jnp.int32, (length, length), 1)
+    ).astype(F32)
+    slot = dot_nn(member.astype(BF16), earlier.astype(BF16))
+    table_ref[:experts, :] = jnp.where(member > 0, slot, -1.0)
+    table_ref[experts:, :] = sum(
+        jnp.where(chosen[k], weight_ref[pl.ds(k, 1), :], 0.0) for k in range(TOP)
+    )
+    chains = [
+        ChainGather(a, b, chain_send.at[k], chain_recv.at[k], chain_local.at[k], at, chips)
+        for k, (a, b) in enumerate([(table_ref, table_all), (cot_low, cot_all)])
+    ]
+    for chain in chains:
+        chain.start()
+    row = lax.broadcasted_iota(jnp.int32, (length, length), 0)
+    col = lax.broadcasted_iota(jnp.int32, (length, length), 1)
+    bias_ref[...] = jnp.where((col < prefix[0]) | (col <= row), 0.0, -1e30)
+    if plane:
+        for step in ("second", "third", "finish"):
+            for gather in first:
+                getattr(gather, step)()
+        for gather in later:
+            gather.first()
+    blocks = gains_full.shape[0] // 64
+    gain_one = sum(gains_full[pl.ds(64 * k, 1), :].astype(F32) for k in range(blocks))
+    gain_two = sum(gains_full[pl.ds(64 * k + 32, 1), :].astype(F32) for k in range(blocks))
+    x = x_ref[...]
+    inverse = lax.rsqrt(jnp.mean(x * x, axis=-1, keepdims=True) + EPS)
+    h1_ref[...] = (x * inverse * gain_one).astype(BF16)
+
+    def project(block, turned):
+        cols = columns(block * 256, 256)
+        part = dot_nn(h1_ref[...], qkv_full[:, cols])
+        if turned:
+            part = jnp.concatenate(
+                [v * cos_ref[...] + partner(v) * sin_ref[...] for v in (part[:, :128], part[:, 128:])], axis=1
+            )
+        rot_ref[:, cols] = part.astype(BF16)
+
+    pl.loop(0, 2 * width // 256)(lambda block: project(block, True))
+    pl.loop(2 * width // 256, 3 * width // 256)(lambda block: project(block, False))
+    for chain in chains:
+        chain.step(1)
+    lse_ref[...] = jnp.zeros_like(lse_ref)
+    rows_at_once = min(256, length)
+
+    def pair(j):
+        queries, keys, values = (
+            rot_ref[:, columns(part * width + j * 128, 128)] for part in range(3)
+        )
+        low_lanes = lax.broadcasted_iota(jnp.int32, (rows_at_once, 128), 1) < HEAD_DIM
+        for start in range(0, length, rows_at_once):
+            rows = pl.ds(start, rows_at_once)
+            outs = []
+            for head in range(2):
+                mine = low_lanes if head == 0 else ~low_lanes
+                query = jnp.where(mine, queries[start : start + rows_at_once], 0.0) * HEAD_DIM**-0.5
+                scores = dot_nt(query.astype(BF16), keys) + bias_ref[rows, :]
+                peak = jnp.max(scores, axis=-1, keepdims=True)
+                exponent = jnp.exp(scores - peak)
+                total = jnp.sum(exponent, axis=-1, keepdims=True)
+                outs.append(dot_nn((exponent / total).astype(BF16), values))
+                lanes = lax.broadcasted_iota(jnp.int32, (rows_at_once, 128), 1)
+                lse_ref[rows, :] = jnp.where(lanes == 2 * j + head, peak + jnp.log(total), lse_ref[rows, :])
+            att_ref[rows, columns(j * 128, 128)] = jnp.where(low_lanes, *outs).astype(BF16)
+
+    pairs = width // 128
+    pl.loop(0, pairs // 2)(pair)
+    for step in range(2, chips - 1):
+        for chain in chains:
+            chain.step(step)
+    if plane:
+        for gather in later:
+            gather.second()
+    pl.loop(pairs // 2, pairs)(pair)
+    resid = x_ref[...] + dot_nn(att_ref[...], out_full[...])
+    resid_ref[...] = resid
+    inverse = lax.rsqrt(jnp.mean(resid * resid, axis=-1, keepdims=True) + EPS)
+    h2_ref[...] = (resid * inverse * gain_two).astype(BF16)
+    for chain in chains:
+        chain.step(chips - 1)
+    if plane:
+        for step in ("third", "finish"):
+            for gather in later:
+                getattr(gather, step)()
+    for chain in chains:
+        for step in range(chips):
+            chain.finish(step)
+        chain.sent()
+
+
+def front(prefix, inputs, cotangent, route_rows, weight_rows, qkv_weight, out_weight, gains, shared, ident):
+    length, width = inputs.shape
+    group = lax.axis_size("expert")
+    chips, plane = group // 2, lax.axis_size("shard") == 4
+    shards = lax.axis_size("shard")
+    cosine, sine = rope_lanes(length)
+    operands = [prefix, inputs, cotangent, route_rows, weight_rows, cosine, sine]
+    vmem, anywhere = pl.BlockSpec(memory_space=pltpu.VMEM), pl.BlockSpec(memory_space=pl.ANY)
+    in_specs = [pl.BlockSpec(memory_space=pltpu.SMEM)] + [vmem] * 6
+    weights = [qkv_weight, out_weight, gains]
+    if plane:
+        operands += weights + shared
+        in_specs += [anywhere] * 6
+    else:
+        weights = [lax.all_gather(v, "shard", axis=0, tiled=True) for v in weights]
+        shared = [lax.all_gather(v, "shard", axis=0, tiled=True) for v in shared]
+        operands += weights
+        in_specs += [vmem] * 3
+    shape = jax.ShapeDtypeStruct
+    out_shape = [
+        shape((group, length, width), BF16),
+        shape((group, 2 * group, length), F32),
+        shape((length, width), BF16),
+        shape((length, 3 * width), BF16),
+        shape((length, width), BF16),
+        shape((length, 128), F32),
+        shape((length, width), F32),
+        shape((length, width), BF16),
+        shape((length, width), BF16),
+    ]
+    out_specs = [anywhere] * 2 + [vmem] * 7
+    scratch = [
+        pltpu.VMEM((length, length), F32),
+        pltpu.VMEM((2 * group, length), F32),
+        pltpu.SemaphoreType.DMA((2, ChainGather.copies(chips))),
+        pltpu.SemaphoreType.DMA((2, ChainGather.copies(chips))),
+        pltpu.SemaphoreType.DMA((2,)),
+    ]
+    if plane:
+        out_shape += [shape((shards * v.shape[0], v.shape[1]), BF16) for v in weights + shared]
+        out_specs += [vmem] * 3 + [anywhere] * 3
+        scratch += [
+            pltpu.SemaphoreType.DMA((6, PlaneGather.COPIES)),
+            pltpu.SemaphoreType.DMA((6, PlaneGather.COPIES)),
+            pltpu.SemaphoreType.DMA((6,)),
+        ]
+    outs = pl.pallas_call(
+        functools.partial(front_kernel, plane=plane, chips=chips),
+        out_shape=out_shape,
+        in_specs=in_specs,
+        out_specs=out_specs,
+        scratch_shapes=scratch,
+        compiler_params=pltpu.CompilerParams(
+            collective_id=ident, has_side_effects=True, vmem_limit_bytes=48 << 20
+        ),
+    )(*operands)
+    if not plane:
+        outs = list(outs) + weights + shared
+    return outs
+
+
 def on_device(
     inputs,
     cotangent,
@@ -323,43 +633,58 @@
     experts = lax.axis_size("expert") * expert_gate.shape[0]
     shards = lax.axis_size("shard")
     me = lax.axis_index("expert")
-    out_low = cotangent.astype(BF16)
-    cot_all = lax.all_gather(out_low, "expert", axis=0)
-
+    shards_at = lax.axis_index("shard")
     capacity = 4 * length // experts
-    copies = length * TOP
-    flat_route = routes.reshape(copies)
-    onehot = (flat_route[:, None] == jnp.arange(experts, dtype=jnp.int32)[None, :]).astype(jnp.int32)
-    before = (jnp.cumsum(onehot, axis=0) - onehot).reshape(length, TOP, experts)
-    onehot = onehot.reshape(length, TOP, experts)
-    slot = jnp.sum(onehot * (before + 1), axis=1) - 1
-    weight = jnp.sum(onehot.astype(F32) * gate_weights[:, :, None], axis=1)
-    table = jnp.stack([slot.astype(F32).T, weight.T], axis=0)
-    table_all = lax.all_gather(table, "expert", axis=0)
-    table_mine = lax.dynamic_index_in_dim(table_all, me, axis=2, keepdims=False)
-
     gains = jnp.concatenate(
-        [jnp.broadcast_to(norm_one, (32, norm_one.shape[0])), jnp.broadcast_to(norm_two, (32, norm_two.shape[0]))],
-        axis=0,
-    )
-    qkv_full, out_full, gains_full = plane_gather([qkv_weight, out_weight, gains], (0, 0, 0), 1)
-    gate_full, up_full, down_full = plane_gather([shared_gate, shared_up, shared_down], (1, 1, 0), 2)
-    gains_full = gains_full.reshape(shards, 64, -1).astype(F32)
-    gain_one = gains_full[:, 0, :].reshape(model_width)
-    gain_two = gains_full[:, 32, :].reshape(model_width)
-
+        [jnp.broadcast_to(v, (32, v.shape[0])) for v in (norm_one, norm_two)], axis=0
+    )
+    gains = lax.dynamic_update_slice(
+        jnp.zeros((64, model_width), BF16), gains, (0, shards_at * norm_one.shape[0])
+    )
+    (
+        cot_all,
+        table_all,
+        normed_one,
+        turned,
+        attended,
+        logsum,
+        resid,
+        normed_two,
+        out_low,
+        qkv_full,
+        out_full,
+        gains_full,
+        gate_blocks,
+        up_blocks,
+        down_full,
+    ) = front(
+        prefix,
+        inputs,
+        cotangent,
+        routes.T,
+        gate_weights.T,
+        qkv_weight,
+        out_weight,
+        gains,
+        [shared_gate, shared_up, shared_down],
+        1,
+    )
+    table_mine = jnp.stack(
+        [lax.dynamic_index_in_dim(table_all, me + k * experts, axis=1, keepdims=False) for k in range(2)], axis=1
+    )
+    gain_rows = jnp.sum(gains_full.reshape(shards, 64, model_width).astype(F32), axis=0)
+    gain_one, gain_two = gain_rows[0], gain_rows[32]
     inverse_one = lax.rsqrt(jnp.mean(inputs * inputs, axis=-1, keepdims=True) + EPS)
-    normed_one = (inputs * inverse_one * gain_one).astype(BF16)
-    projected = matmul(normed_one, qkv_full)
+    inverse_two = lax.rsqrt(jnp.mean(resid * resid, axis=-1, keepdims=True) + EPS)
+    normed_all = lax.all_gather(normed_two, "expert", axis=0)
+    gate_full = gate_blocks.reshape(shards, model_width, -1).transpose(1, 0, 2).reshape(model_width, -1)
+    up_full = up_blocks.reshape(shards, model_width, -1).transpose(1, 0, 2).reshape(model_width, -1)
     cosine_table, sine_table = rope_tables(length)
     head_shape = (length, HEADS, HEAD_DIM)
-    queries = rotate(
-        projected[:, :model_width].reshape(head_shape), cosine_table, sine_table
-    ).astype(BF16)
-    key_rows = rotate(
-        projected[:, model_width : 2 * model_width].reshape(head_shape), cosine_table, sine_table
-    ).astype(BF16)
-    value_rows = projected[:, 2 * model_width :].reshape(head_shape).astype(BF16)
+    queries, key_rows, value_rows = (
+        turned[:, k * model_width : (k + 1) * model_width].reshape(head_shape) for k in range(3)
+    )
+    logsum = logsum[:, :HEADS].T[:, :, None]
     score_scale = HEAD_DIM ** (-0.5)
     row_pos = lax.broadcasted_iota(jnp.int32, (length, length), 0)
     col_pos = lax.broadcasted_iota(jnp.int32, (length, length), 1)
@@ -370,22 +695,6 @@
             jnp.einsum("qhd,khd->hqk", queries, key_rows, preferred_element_type=F32) * score_scale
         )
         return jnp.where(visible[None], raw_scores, -1e30)
-
-    scores = masked_scores()
-    row_peak = jnp.max(scores, axis=-1, keepdims=True)
-    exponent = jnp.exp(scores - row_peak)
-    expsum = jnp.sum(exponent, axis=-1, keepdims=True)
-    logsum = row_peak + jnp.log(expsum)
-    probs_low = (exponent / expsum).astype(BF16)
-    attended = (
-        jnp.einsum("hqk,khd->qhd", probs_low, value_rows, preferred_element_type=F32)
-        .reshape(length, model_width)
-        .astype(BF16)
-    )
-    resid = inputs + matmul(attended, out_full)
-    inverse_two = lax.rsqrt(jnp.mean(resid * resid, axis=-1, keepdims=True) + EPS)
-    normed_two = (resid * inverse_two * gain_two).astype(BF16)
-    normed_all = lax.all_gather(normed_two, "expert", axis=0)
 
     shared_pre = matmul(normed_two, gate_full)
     shared_lift = matmul(normed_two, up_full)
@@ -434,7 +743,8 @@
     weight_dot = jnp.sum(result.astype(F32) * cot_rows, axis=2)
     weight_back = jnp.einsum("ect,ec->et", pick.astype(F32), weight_dot, precision=lax.Precision.HIGHEST)
     weight_got = lax.all_to_all(weight_back, "expert", split_axis=0, concat_axis=0, tiled=True)
-    gate_weights_grad = jnp.sum(onehot.astype(F32) * weight_got.T[:, None, :], axis=2)
+    onehot = routes[:, :, None] == jnp.arange(experts, dtype=jnp.int32)[None, None, :]
+    gate_weights_grad = jnp.sum(jnp.where(onehot, weight_got.T[:, None, :], 0.0), axis=2)
 
     def blocks_of_columns(value):
         width = value.shape[1] // shards

time: 788 us -> 707 us (0.90)
  waiting for transfers between devices: 80.1 us -> 42.9 us
  other arithmetic: 63.9 us -> 38 us
  matrix products: 224 us -> 199 us
  blocking collectives: 42.6 us -> 26.8 us
  Pallas kernels: 268 us -> 283 us
  local copies, waits for them, and re-layouts: 79.3 us -> 90.5 us
    all_gather x1 -> x0, waiting for transfers between devices: 49.1 us -> none  [on_device(): cot_all = lax.all_gather(out_low, 'expert', axis=0)]
    dot_general x24 -> x22, matrix products: 176 us -> 153 us  [matmul(): return jnp.dot(left, right, preferred_element_type=jnp.float32)]
    reduce_sum x4 -> x3, other arithmetic: 17.3 us -> 1.52 us  [the longest x1 0.73 us: on_device(): jnp.sum(gains_full.reshape(shards, 64, model_width).astype(F32), axis=0)]
    all_gather x1 -> x0, blocking collectives: 15.5 us -> none  [on_device(): table_all = lax.all_gather(table, 'expert', axis=0)]
    pallas_call x2 -> x1, Pallas kernels: 69.1 us -> 82.5 us  [front(): pl.pallas_call(functools.partial(front_kernel, plane=plane, chips=chips),...]
    all_gather x1, waiting for transfers between devices: 30.9 us -> 42.8 us  [on_device(): normed_all = lax.all_gather(normed_two, 'expert', axis=0)]
    unnamed x191 -> x158, local copies, waits for them, and re-layouts: 28.8 us -> 25.1 us
  transfers between devices with their start and end apart: 6 -> 5, of which waited for: 2 -> 1; matrix products, arithmetic and copies ran while one was open for 28% -> 32% of each run, Pallas kernels for 31% -> 29%
where the time goes in v2:
time: 707 us; the launch traced here: 700 us
  Pallas kernels  283 us (40%)
  matrix products  199 us (28%)
  local copies, waits for them, and re-layouts  90.5 us (13%)
  waiting for transfers between devices  42.9 us (6%)
  other arithmetic  38 us (5%)
  blocking collectives  26.8 us (4%)
  between operations  15.4 us (2%)
    pallas_call x2, Pallas kernels, plane_reduce(): pl.pallas_call(functools.partial(plane_reduce_kernel, count=count), out_s...  200 us
    dot_general x22, matrix products, matmul(): return jnp.dot(left, right, preferred_element_type=jnp.float32)  153 us
    pallas_call x1, Pallas kernels, front(): pl.pallas_call(functools.partial(front_kernel, plane=plane, chips=chips),...  82.5 us
    all_gather x1, waiting for transfers between devices, on_device(): normed_all = lax.all_gather(normed_two, 'expert', axis=0)  42.8 us
    psum x1, blocking collectives, on_device(): summed = [lax.psum(v.astype(BF16), 'expert').astype(F32) for v in pieces]  26.8 us
    unnamed x158, local copies, waits for them, and re-layouts  25.1 us
    reshape x4, local copies, waits for them, and re-layouts, blocks_of_columns(): value.astype(BF16).reshape(value.shape[0], shards, width).transpose(1, 0, 2)  19 us
    convert_element_type x4, local copies, waits for them, and re-layouts, blocks_of_columns(): value.astype(BF16).reshape(value.shape[0], shards, width).transpose(1, 0, 2)  18.9 us
  transfers between devices with their start and end apart: 5, of which 1 were waited for; matrix products, arithmetic and copies ran while one was open for 32% of the time, Pallas kernels for 29%

profile of v2, /device:TPU:0, one launch (start us, length us, event | category | flops | bytes accessed | tf_op | source)
XLA Modules:
  0.0 699.9 jit_solution(8660009832125069347)
XLA Ops:
  11.0 2.9 pad_maximum_fusion.5
  18.8 82.5 %shard_map.246 = (bf16[8,512,768]{2,1,0:T(8,128)(2,1)}, f32[8,16,512]{2,1,0:T(8,128)S(1)}, bf16[512,768]{1,0:T(8,128)(2,1)S(1)}, bf16[512,2304]{1,0:T(8,128)(2,1...) custom-call(s32[1]{0:T(128)} %copy.174.refs_0_, ...), custom_call_target="tpu_custom_call" | custom-call | tf_op jit(solution)/shard_map/pallas_call | solution.py:600
  109.9 8.2 %multiply_convert_fusion.4 = (bf16[8,256,768]{2,1,0:T(8,128)(2,1)S(1)}, f32[8,256,768]{2,1,0:T(8,128)}) fusion(f32[8,256]{1,0:T(8,128)S(1)} %multiply_reduce_fusion.1, bf16[8,512,768]{2,1,0:T(8,128)(2,1)} %get-tuple-element.68, f32[8,512]{1,0:T(8,128)S(1)} %bitcast.177), kind=kOutput, calls=%fused_computation.14 | convolution fusion | flops 1614807040 | bytes 15753216 | tf_op jit(solution)/shard_map/ect,etd->ecd/dot_general | solution.py:718
  119.7 9.6 %fusion.17 = f32[2048,2048]{1,0:T(8,128)} fusion(bf16[2048,768]{1,0:T(8,128)(2,1)S(1)} %bitcast.174, bf16[1,2048,768]{2,1,0:T(8,128)(2,1)S(1)} %copy-done.60), kind=kOutput, calls=%fused_computation.40 | convolution fusion | flops 6442450944 | bytes 23068672 | tf_op jit(solution)/shard_map/dot_general | solution.py:56
  129.2 42.8 %all-gather.3.cloned.1.call-done = bf16[4096,768]{1,0:T(8,128)(2,1)} async-done(((bf16[512,768]{1,0:T(8,128)(2,1)}), bf16[4096,768]{1,0:T(8,128)(2,1)}) %all-gather.3.cloned.1.call-update) | async-done | bytes 6291472 | tf_op jit(solution)/shard_map/all_gather | solution.py:679
  172.1 5.4 fusion.31
  179.1 9.5 %fusion.22 = f32[2048,2048]{1,0:T(8,128)} fusion(bf16[2048,768]{1,0:T(8,128)(2,1)S(1)} %bitcast.193, bf16[1,768,2048]{2,1,0:T(8,128)(2,1)S(1)} %copy-done.59), kind=kOutput, calls=%fused_computation.45 | convolution fusion | flops 6442450944 | bytes 23068672 | tf_op jit(solution)/shard_map/dot_general | solution.py:56
  188.6 26.2 %multiply_convert_fusion.1 = (bf16[2048,2048]{1,0:T(8,128)(2,1)}, bf16[2048,2048]{1,0:T(8,128)(2,1)}, bf16[2048,2048]{1,0:T(8,128)(2,1)}) fusion(f32[2048,2048]{1,0:T(8,128)} %fusion.17, f32[2048,2048]{1,0:T(8,128)} %fusion.22, bf16[2048,768]{1,0:T(8,128)(2,1)} %bitcast.194, bf16[1,768,2048]{2,1,0:T(8,128)(2,1)S(1)} %copy-done), kind=kOutput, calls=%fused_computation.1 | convolution fusion | flops 6505365504 | bytes 65011712 | tf_op jit(solution)/shard_map/dot_general | solution.py:56
  214.8 10.4 %fusion.20 = f32[2048,768]{1,0:T(8,128)S(1)} fusion(bf16[2048,2048]{1,0:T(8,128)(2,1)} %get-tuple-element.97, bf16[1,768,2048]{2,1,0:T(8,128)(2,1)} %param.29), kind=kOutput, calls=%fused_computation.43 | convolution fusion | flops 6442450944 | bytes 17825792 | tf_op jit(solution)/shard_map/dot_general | solution.py:56
  225.2 6.9 add_convert_fusion
  232.2 3.8 fusion.15
  236.0 4.8 copy.122
  240.8 2.9 copy.121
  243.7 3.0 fusion.53
  253.4 3.9 fusion.56
  259.6 3.8 multiply_convert_fusion.5
  263.4 3.6 convolution_convert_fusion.6
  266.9 3.5 convolution_convert_fusion.5
  270.4 3.6 convolution_convert_fusion.4
  274.1 6.5 fusion.58
  280.6 6.9 convolution_convert_fusion.3
  287.5 3.9 fusion.14
  298.3 4.7 copy.136
  303.0 4.7 copy.137
  307.7 4.7 copy.138
  312.4 4.8 copy.139
  317.2 5.5 fusion.57
  322.8 3.5 fusion.3
  328.8 3.3 all-to-all-start
  332.2 12.2 %convolution_convert_fusion.2 = bf16[768,2048]{1,0:T(8,128)(2,1)} fusion(bf16[2048,768]{1,0:T(8,128)(2,1)} %bitcast.195, bf16[2048,2048]{1,0:T(8,128)(2,1)} %get-tuple-element.96), kind=kOutput, calls=%fused_computation.34 | convolution fusion | flops 6444023808 | bytes 14680064 | tf_op jit(solution)/shard_map/dot_general | solution.py:56
  344.4 10.7 %convolution_convert_fusion.7 = bf16[2048,768]{1,0:T(8,128)(2,1)} fusion(bf16[2048,2048]{1,0:T(8,128)(2,1)} %get-tuple-element.98, bf16[2048,768]{1,0:T(8,128)(2,1)S(1)} %bitcast.175), kind=kOutput, calls=%fused_computation.39 | convolution fusion | flops 6444023808 | bytes 14680064 | tf_op jit(solution)/shard_map/dot_general | solution.py:56
  355.2 5.5 multiply_reduce_fusion.2
  365.1 11.1 %multiply_reduce_fusion = (f32[12,512]{1,0:T(8,128)S(1)}, f32[12,512,512]{1,2,0:T(8,128)}) fusion(f32[12,512,512]{1,2,0:T(8,128)} %fusion.58, f32[12,512]{1,0:T(8,128)S(1)} %copy.126, pred[512,512]{0,1:T(8,128)(4,1)S(1)} %fusion.41, bf16[512,12,64]{0,2,1:T(8,128)(2,1)S(1)} %bitcast.164, bf16[512,12,64]{0,2,1:T(8,128)(2,1)S(1)} %bitcast.163), kind=kOutput, calls=%fused_computation.6 | convolution fusion | flops 418375680 | bytes 27049984 | tf_op jit(solution)/shard_map/qhd,khd->hqk/dot_general | solution.py:775
  378.1 7.4 %multiply_convert_fusion.3 = bf16[12,512,512]{1,2,0:T(8,128)(2,1)S(1)} fusion(f32[12,512,512]{1,2,0:T(8,128)} %get-tuple-element.126, f32[12,512,512]{1,2,0:T(8,128)S(1)} %bitcast.146, f32[12,512]{1,0:T(8,128)S(1)} %get-tuple-element.125, f32[12,512]{1,0:T(8,128)S(1)} %copy.126, pred[512,512]{0,1:T(8,128)(4,1)S(1)} %fusion.41), kind=kLoop, calls=%fused_computation.5 | loop fusion | flops 18874368 | bytes 31768576 | tf_op jit(solution)/shard_map/convert_element_type | solution.py:778
  389.8 3.2 fusion.38
  393.0 3.3 multiply_reduce_fusion.3
  399.0 3.8 convolution_convert_fusion
  402.8 121.3 %shard_map.247 = (f32[192,2304]{1,0:T(8,128)}, f32[192,768]{1,0:T(8,128)S(1)}, f32[32,192]{1,0:T(8,128)S(1)}, f32[768,512]{1,0:T(8,128)S(1)}, f32[768,512]{1,0:T(8,128)S(1)}, /*index=5*/f32[512,768]{1,0:T(8,128)}) custom-call(bf16[4,192,2304]{2,1,0:T(8,128)(2,1)} %bitcast.162, bf16[4,192,768]{2,1,0:T(8,128)(2,1)S(1)} %bitcast.138, ...), custom_call_target="tpu_custom_call" | custom-call | tf_op jit(solution)/shard_map/pallas_call | solution.py:290
  530.4 12.0 %convolution_convert_fusion.1 = bf16[768,2048]{1,0:T(8,128)(2,1)} fusion(bf16[2048,768]{1,0:T(8,128)(2,1)} %bitcast.196, bf16[2048,2048]{1,0:T(8,128)(2,1)} %get-tuple-element.97), kind=kOutput, calls=%fused_computation.33 | convolution fusion | flops 6444023808 | bytes 14680064 | tf_op jit(solution)/shard_map/dot_general | solution.py:56
  542.4 4.8 copy.140
  547.2 4.7 copy.141
  551.9 4.8 copy.142
  556.7 4.7 copy.143
  561.4 79.0 %shard_map.248 = (f32[768,512]{1,0:T(8,128)S(1)}, f32[768,512]{1,0:T(8,128)S(1)}, f32[512,768]{1,0:T(8,128)S(1)}) custom-call(bf16[4,768,512]{2,1,0:T(8,128)(2,1)} %bitcast.155, bf16[4,768,512]{2,1,0:T(8,128)(2,1)} %bitcast.156, bf16[4,512,768]{2,1,0:T(8,128)(2,1)} %bitcast.173), custom_call_target="tpu_custom_call" | custom-call | tf_op jit(solution)/shard_map/pallas_call | solution.py:290
  644.5 26.8 %psum.42 = bf16[32,192]{1,0:T(8,128)(2,1)S(1)} all-reduce(bf16[32,192]{1,0:T(8,128)(2,1)S(1)} %convert_element_type.207), channel_id=1, replica_groups=mesh['expert'=8,'shard'=4] {'expert'}, use_global_device_ids=true, to_apply=%region_11.12 | all-reduce | flops 6144 | bytes 24576 | tf_op jit(solution)/shard_map/psum | solution.py:812
  671.9 4.0 subtract_add_fusion
  676.0 5.6 fusion.37
  681.6 2.6 convert_element_type.210
  (227 shorter events, 71.1 us)
Async XLA Ops:
  7.2 181.4 %copy-start = (bf16[1,768,2048]{2,1,0:T(8,128)(2,1)S(1)}, bf16[1,768,2048]{2,1,0:T(8,128)(2,1)}, u32[]{:S(2)}) copy-start(bf16[1,768,2048]{2,1,0:T(8,128)(2,1)} %param.28) | copy-start | bytes 9437188
  7.2 164.9 %all-gather.3.cloned.1.call-start = ((), (), s32[]{:S(2)}) async-start(), calls=%async_computation.5 | async-start | bytes 7077888 | tf_op jit(solution)/shard_map/all_gather | solution.py:679
  107.0 248.1 %reduce-scatter.5.cloned.1.call-start = ((), (), s32[]{:S(2)}) async-start(), calls=%async_computation.4 | async-start | bytes 7077888 | tf_op jit(solution)/shard_map/reduce_scatter | solution.py:737
  109.8 8.2 %copy-start.53 = (f32[8,256]{1,0:T(8,128)}, f32[8,256]{1,0:T(8,128)S(1)}, u32[]{:S(2)}) copy-start(f32[8,256]{1,0:T(8,128)S(1)} %multiply_reduce_fusion.1) | copy-start | bytes 24580
  109.8 9.8 %copy-start.60 = (bf16[1,2048,768]{2,1,0:T(8,128)(2,1)S(1)}, bf16[1,2048,768]{2,1,0:T(8,128)(2,1)}, u32[]{:S(2)}) copy-start(bf16[1,2048,768]{2,1,0:T(8,128)(2,1)} %param.30) | copy-start | bytes 9437188
  172.0 7.0 %copy-start.59 = (bf16[1,768,2048]{2,1,0:T(8,128)(2,1)S(1)}, bf16[1,768,2048]{2,1,0:T(8,128)(2,1)}, u32[]{:S(2)}) copy-start(bf16[1,768,2048]{2,1,0:T(8,128)(2,1)} %param.29) | copy-start | bytes 9437188
  214.8 10.4 %copy-start.70 = (bf16[2048,2048]{1,0:T(8,128)(2,1)S(1)}, bf16[2048,2048]{1,0:T(8,128)(2,1)}, u32[]{:S(2)}) copy-start(bf16[2048,2048]{1,0:T(8,128)(2,1)} %get-tuple-element.96) | copy-start | bytes 25165828
  235.9 440.0 %reduce-scatter.3.cloned.1.call-start = ((), (), s32[]{:S(2)}) async-start(), calls=%async_computation.3 | async-start | bytes 7077888 | tf_op jit(solution)/shard_map/reduce_scatter | solution.py:742
  236.0 4.9 copy-start.41
  243.7 6.6 copy-start.15
  243.7 7.3 %copy-start.28 = (f32[512,768]{1,0:T(8,128)S(1)}, f32[512,768]{1,0:T(8,128)}, u32[]{:S(2)}) copy-start(f32[512,768]{1,0:T(8,128)} %refs_1_.1) | copy-start | bytes 4718596
  247.9 4.8 copy-start.18
  247.9 5.5 copy-start.13
  253.4 3.9 copy-start.42
  263.3 3.6 copy-start.68
  263.3 3.6 copy-start.67
  263.4 7.1 %copy-start.69 = (bf16[512,2048]{1,0:T(8,128)(2,1)}, bf16[512,2048]{1,0:T(8,128)(2,1)S(1)}, u32[]{:S(2)}) copy-start(bf16[512,2048]{1,0:T(8,128)(2,1)S(1)} %get-tuple-element.101) | copy-start | bytes 6291460
  270.4 3.6 copy-start.30
  270.4 3.6 copy-start.32
  270.4 10.2 %slice-start.3 = ((s8[8388608]{0:T(1024)(128)(4,1)}), s8[4194304]{0:T(1024)(128)(4,1)S(1)}, s32[]{:S(2)}) async-start(s8[8388608]{0:T(1024)(128)(4,1)} %bitcast.199), calls=%async_computation.10 | async-start | bytes 8388608
  274.1 6.5 copy-start.61
  274.1 6.5 slice-start.4
  280.6 6.9 copy-start.54
  328.8 315.1 %all-to-all-start = ((f32[8,1,512]{2,1,0:T(1,128)}), f32[8,1,512]{2,1,0:T(1,128)S(1)}, u32[]{:S(2)}, u32[]{:S(2)}) async-start(f32[8,1,512]{2,1,0:T(1,128)} %all_to_all.8), calls=%async_computation.2 | async-start | bytes 32768 | tf_op jit(solution)/shard_map/all_to_all | solution.py:745
  332.1 349.5 %all-reduce.4.cloned.1.call-start = ((), (), s32[]{:S(2)}) async-start(), calls=%async_computation.6 | async-start | bytes 7077888 | tf_op jit(solution)/shard_map/psum | solution.py:812
  332.2 12.3 %copy-start.44 = (bf16[8,256,768]{2,1,0:T(8,128)(2,1)S(1)}, bf16[8,256,768]{2,1,0:T(8,128)(2,1)}, u32[]{:S(2)}) copy-start(bf16[8,256,768]{2,1,0:T(8,128)(2,1)} %copy-done.43) | copy-start | bytes 9437188
  344.4 10.7 %copy-start.35 = (f32[512,768]{1,0:T(8,128)S(1)}, f32[512,768]{1,0:T(8,128)}, u32[]{:S(2)}) copy-start(f32[512,768]{1,0:T(8,128)} %get-tuple-element.61) | copy-start | bytes 4718596
  355.1 5.5 copy-start.37
  361.1 15.2 %copy-start.27 = (f32[512,768]{1,0:T(8,128)}, f32[512,768]{1,0:T(8,128)S(1)}, u32[]{:S(2)}) copy-start(f32[512,768]{1,0:T(8,128)S(1)} %subtract_add_fusion.1) | copy-start | bytes 4718596
  361.1 4.0 copy-start.38
  365.1 11.2 %copy-start.39 = (bf16[512,768]{0,1:T(8,128)(2,1)}, bf16[512,768]{0,1:T(8,128)(2,1)S(1)}, u32[]{:S(2)}) copy-start(bf16[512,768]{0,1:T(8,128)(2,1)S(1)} %copy.127) | copy-start | bytes 2359300
  365.1 11.2 %slice-start = ((s8[12582912]{0:T(1024)(128)(4,1)}), s8[4194304]{0:T(1024)(128)(4,1)S(1)}, s32[]{:S(2)}) async-start(s8[12582912]{0:T(1024)(128)(4,1)} %bitcast.145), calls=%async_computation.7 | async-start | bytes 8388608
  365.1 11.2 %slice-start.1 = ((s8[12582912]{0:T(1024)(128)(4,1)}), s8[4194304]{0:T(1024)(128)(4,1)S(1)}, s32[]{:S(2)}) async-start(s8[12582912]{0:T(1024)(128)(4,1)} %bitcast.145), calls=%async_computation.8 | async-start | bytes 8388608
  365.1 13.0 %slice-start.2 = ((s8[12582912]{0:T(1024)(128)(4,1)}), s8[4194304]{0:T(1024)(128)(4,1)S(1)}, s32[]{:S(2)}) async-start(s8[12582912]{0:T(1024)(128)(4,1)} %bitcast.145), calls=%async_computation.9 | async-start | bytes 8388608
  378.1 7.4 %copy-start.33 = (bf16[512,768]{0,1:T(8,128)(2,1)S(1)}, bf16[512,768]{0,1:T(8,128)(2,1)}, u32[]{:S(2)}) copy-start(bf16[512,768]{0,1:T(8,128)(2,1)} %copy.125) | copy-start | bytes 2359300
  389.2 3.8 copy-start.46
  392.9 3.4 copy-start.65
  393.0 3.6 copy-start.11
  524.1 4.6 copy-start.45
  561.4 82.5 %copy-start.20 = (s32[512,2]{0,1:T(2,128)S(1)}, s32[512,2]{0,1:T(2,128)}, u32[]{:S(2)}) copy-start(s32[512,2]{0,1:T(2,128)} %param.32) | copy-start | bytes 12292
  561.4 110.5 %copy-start.57 = (f32[512]{0:T(512)S(1)}, f32[512]{0:T(512)}, u32[]{:S(2)}) copy-start(f32[512]{0:T(512)} %get-tuple-element.115) | copy-start | bytes 6148
  671.9 4.0 copy-start.36
  681.6 4.0 copy-start.51
  681.6 5.4 copy-start.50
  684.2 4.0 copy-start.55
  685.6 3.5 copy-start.7
  687.0 3.3 copy-start.5
  689.1 4.1 copy-start.1
  (33 other events, 52.5 us)
Sparse Core Ops, SparseCore 0:
  107.1 64.8 all-gather.2
  236.1 68.4 reduce-scatter.4
  306.9 68.4 reduce-scatter.2
  530.5 85.7 all-reduce.3

commit v3 on v2

--- a/solution.py
+++ b/solution.py
@@ -14,46 +14,6 @@
 MESH = pl.DeviceIdType.MESH
 F32 = jnp.float32
 BF16 = jnp.bfloat16
-
-
-def rope_tables(length):
-    half_dim = HEAD_DIM // 2
-    frequency = 10000.0 ** (-jnp.arange(half_dim, dtype=jnp.float32) * 2.0 / HEAD_DIM)
-    angles = jnp.arange(length, dtype=jnp.float32)[:, None] * frequency[None, :]
-    return (jnp.cos(angles)[:, None, :], jnp.sin(angles)[:, None, :])
-
-
-def rotate(vectors, cosine_table, sine_table):
-    half_dim = vectors.shape[-1] // 2
-    first_half = vectors[..., :half_dim]
-    second = vectors[..., half_dim:]
-    return jnp.concatenate(
-        [
-            first_half * cosine_table - second * sine_table,
-            second * cosine_table + first_half * sine_table,
-        ],
-        axis=-1,
-    )
-
-
-def gated_unit(pre_gate):
-    sigmoid_value = jax.nn.sigmoid(pre_gate)
-    activated = pre_gate * sigmoid_value
-    derivative = sigmoid_value * (1.0 + pre_gate * (1.0 - sigmoid_value))
-    return (activated, derivative)
-
-
-def norm_back(source, inverse, gain, grad_in):
-    scaled = grad_in * gain
-    gain_grad = jnp.sum(grad_in * source * inverse, axis=0)
-    input_part = inverse * scaled - source * inverse**3 * jnp.mean(
-        scaled * source, axis=-1, keepdims=True
-    )
-    return (gain_grad, input_part)
-
-
-def matmul(left, right):
-    return jnp.dot(left, right, preferred_element_type=jnp.float32)
 
 
 def place():
@@ -146,162 +106,6 @@
         for made in self.copies:
             made.wait_send()
         self.own.wait()
-
-
-def plane_gather_kernel(*refs, axes):
-    count = len(axes)
-    send, recv, local = refs[2 * count :]
-    at = place()
-    meet([at["dev_x"], at["dev_y"], at["dev_c"]])
-    gathers = [
-        PlaneGather(refs[k], refs[count + k], axes[k], send.at[k], recv.at[k], local.at[k], at)
-        for k in range(count)
-    ]
-    for step in ("first", "second", "third", "finish"):
-        for gather in gathers:
-            getattr(gather, step)()
-
-
-def plane_gather(arrays, axes, ident):
-    if lax.axis_size("shard") != 4:
-        return [lax.all_gather(v, "shard", axis=a, tiled=True) for v, a in zip(arrays, axes)]
-    count = len(arrays)
-    shapes = []
-    for array, axis in zip(arrays, axes):
-        shape = list(array.shape)
-        shape[axis] *= 4
-        shapes.append(jax.ShapeDtypeStruct(tuple(shape), array.dtype))
-    return pl.pallas_call(
-        functools.partial(plane_gather_kernel, axes=axes),
-        out_shape=shapes,
-        in_specs=[pl.BlockSpec(memory_space=pl.ANY)] * count,
-        out_specs=[pl.BlockSpec(memory_space=pl.ANY)] * count,
-        scratch_shapes=[
-            pltpu.SemaphoreType.DMA((count, PlaneGather.COPIES)),
-            pltpu.SemaphoreType.DMA((count, PlaneGather.COPIES)),
-            pltpu.SemaphoreType.DMA((count,)),
-        ],
-        compiler_params=pltpu.CompilerParams(
-            collective_id=ident, has_side_effects=True, vmem_limit_bytes=32 << 20
-        ),
-    )(*arrays)
-
-
-class PlaneReduce:
-    COPIES = 4
-
-    def __init__(self, src, dst, mine, got, hold, last, send, recv, local, at):
-        self.src, self.dst, self.mine, self.got, self.hold, self.last = src, dst, mine, got, hold, last
-        self.send, self.recv, self.local, self.at = send, recv, local, at
-        self.half = src.shape[1] // 2
-
-    @staticmethod
-    def scratch(shape):
-        half = shape[1] // 2
-        return [
-            pltpu.VMEM((4, half, shape[2]), BF16),
-            pltpu.VMEM((4, half, shape[2]), BF16),
-            pltpu.VMEM((2, half, shape[2]), BF16),
-            pltpu.VMEM((2, half, shape[2]), BF16),
-        ]
-
-    def first(self):
-        at, half = self.at, self.half
-        upper, lower = pl.ds(0, half), pl.ds(half, half)
-        plan = [
-            (at["sx"], upper, at["dev_x"], 0),
-            (at["sd"], upper, at["dev_x"], 1),
-            (at["sy"], lower, at["dev_y"], 2),
-            (at["sd"], lower, at["dev_y"], 3),
-        ]
-        self.out = []
-        for shard, rows, device, slot in plan:
-            made = remote(
-                self.src.at[shard, rows, :], self.got.at[slot], self.send.at[slot], self.recv.at[slot], device
-            )
-            made.start()
-            self.out.append(made)
-        self.near = []
-        for slot, (shard, rows) in enumerate(
-            [(at["shard"], upper), (at["sy"], upper), (at["shard"], lower), (at["sx"], lower)]
-        ):
-            made = pltpu.make_async_copy(self.src.at[shard, rows, :], self.mine.at[slot], self.local.at[slot])
-            made.start()
-            self.near.append(made)
-
-    def second(self):
-        at = self.at
-        for slot in (1, 3):
-            self.near[slot].wait()
-            self.out[slot].wait_recv()
-            self.hold[slot // 2] = (
-                self.mine[slot].astype(F32) + self.got[slot].astype(F32)
-            ).astype(BF16)
-            made = remote(
-                self.hold.at[slot // 2],
-                self.last.at[slot // 2],
-                self.send.at[4 + slot // 2],
-                self.recv.at[4 + slot // 2],
-                at["dev_y"] if slot == 1 else at["dev_x"],
-            )
-            made.start()
-            self.out.append(made)
-
-    def third(self):
-        half = self.half
-        for slot in (0, 2):
-            self.near[slot].wait()
-            self.out[slot].wait_recv()
-            self.out[4 + slot // 2].wait_recv()
-            self.dst[pl.ds(slot // 2 * half, half), :] = (
-                self.mine[slot].astype(F32) + self.got[slot].astype(F32)
-            ) + self.last[slot // 2].astype(F32)
-
-    def finish(self):
-        for made in self.out:
-            made.wait_send()
-
-
-def plane_reduce_kernel(*refs, count):
-    scratch = refs[2 * count :]
-    send, recv, local = scratch[4 * count :]
-    at = place()
-    meet([at["dev_x"], at["dev_y"]])
-    reduces = [
-        PlaneReduce(
-            refs[k], refs[count + k], *scratch[4 * k : 4 * k + 4], send.at[k], recv.at[k], local.at[k], at
-        )
-        for k in range(count)
-    ]
-    for step in ("first", "second", "third", "finish"):
-        for reduce in reduces:
-            getattr(reduce, step)()
-
-
-def plane_reduce(arrays, ident):
-    if lax.axis_size("shard") != 4:
-        return [
-            lax.psum_scatter(v, "shard", scatter_dimension=0, tiled=True)[0].astype(F32) for v in arrays
-        ]
-    count = len(arrays)
-    scratch = []
-    for array in arrays:
-        scratch += PlaneReduce.scratch(array.shape)
-    return pl.pallas_call(
-        functools.partial(plane_reduce_kernel, count=count),
-        out_shape=[jax.ShapeDtypeStruct(v.shape[1:], F32) for v in arrays],
-        in_specs=[pl.BlockSpec(memory_space=pl.ANY)] * count,
-        out_specs=[pl.BlockSpec(memory_space=pltpu.VMEM)] * count,
-        scratch_shapes=scratch
-        + [
-            pltpu.SemaphoreType.DMA((count, 6)),
-            pltpu.SemaphoreType.DMA((count, 6)),
-            pltpu.SemaphoreType.DMA((count, 4)),
-        ],
-        compiler_params=pltpu.CompilerParams(
-            collective_id=ident, has_side_effects=True, vmem_limit_bytes=48 << 20
-        ),
-    )(*arrays)
 
 
 class ChainGather:
@@ -612,6 +416,910 @@
     return outs
 
 
+def near_order(chips):
+    table = []
+    for z in range(chips):
+        others = sorted(range(chips), key=lambda s: (abs(s - z), abs(2 * s - chips + 1) * -1))
+        table.append(others)
+    return table
+
+
+def pick_static(table, step, z):
+    return sum(jnp.where(z == k, row[step], 0) for k, row in enumerate(table))
+
+
+def gated_block(rows, grad, gate, up, down):
+    pre_gate = dot_nn(rows, gate)
+    pre_up = dot_nn(rows, up)
+    sigmoid = 1.0 / (1.0 + jnp.exp(-pre_gate))
+    active = pre_gate * sigmoid
+    hidden = (active * pre_up).astype(BF16)
+    hidden_grad = dot_nt(grad, down)
+    gate_grad = (hidden_grad * pre_up * (sigmoid * (1.0 + pre_gate * (1.0 - sigmoid)))).astype(BF16)
+    up_grad = (hidden_grad * active).astype(BF16)
+    result = dot_nn(hidden, down)
+    back = dot_nt(gate_grad, gate) + dot_nt(up_grad, up)
+    return hidden, gate_grad, up_grad, result, back
+
+
+def middle_kernel(*refs, chips, shards, capacity):
+    (h2_ref, cot_ref, table_ref, cot_all, gate_hbm, up_hbm, down_hbm, sg_hbm, su_hbm, sd_hbm), refs = refs[:10], refs[10:]
+    (rows_out, grad_out, hid_out, da_out, db_out, mix_out, back_out), refs = refs[:7], refs[7:]
+    sown, sgot, (dots_out, sy_ref, dh_ref), refs = refs[:3], refs[3:6], refs[6:9], refs[9:]
+    (sgg_s, sug_s, sdg_s, sg_sem, sg_send, sg_recv), refs = refs[:6], refs[6:]
+    (gate_w, up_w, down_w, sg_w, su_w, sd_w, h2_all, cot_buf, rows_ref, grad_ref, cotr_ref, scale_ref), refs = refs[:12], refs[12:]
+    (y_acc, r_acc, stage_f, stage_s, stage_t, got, total), refs = refs[:7], refs[7:]
+    w_sem, s_sem, cot_sem, row_sem, f_sem, tot_sem, core_send, core_recv, chain_send, chain_recv, chain_local = refs
+    length, width = h2_ref.shape
+    experts = 2 * chips
+    hidden_width = gate_w.shape[1]
+    unit = stage_f.shape[-1]
+    units = hidden_width // unit
+    block = sg_w.shape[-1]
+    at = place()
+    me, core, z = at["expert"], at["core"], at["z"]
+    order = near_order(chips)
+    chain_meet(at, chips, [at["dev_c"]])
+    chain = ChainGather(h2_ref, h2_all, chain_send, chain_recv, chain_local, at, chips)
+    chain.start()
+
+    def load_cot(step):
+        chip = pick_static(order, step, z)
+        return pltpu.make_async_copy(
+            cot_all.at[pl.ds(2 * chip, 2)], cot_buf.at[step % 2], cot_sem.at[step % 2]
+        )
+
+    load_cot(0).start()
+    loads = [
+        pltpu.make_async_copy(a, b, w_sem.at[k])
+        for k, (a, b) in enumerate([(gate_hbm.at[0], gate_w), (up_hbm.at[0], up_w), (down_hbm.at[0], down_w)])
+    ]
+    for load in loads:
+        load.start()
+
+    def load_shared(k, slot):
+        return [
+            pltpu.make_async_copy(sg_hbm.at[pl.ds(k * width, width), :], sg_w.at[slot], s_sem.at[slot, 0]),
+            pltpu.make_async_copy(su_hbm.at[pl.ds(k * width, width), :], su_w.at[slot], s_sem.at[slot, 1]),
+            pltpu.make_async_copy(sd_hbm.at[pl.ds(k * block, block), :], sd_w.at[slot], s_sem.at[slot, 2]),
+        ]
+
+    for load in load_shared(0, 0):
+        load.start()
+
+    def one_hot(source):
+        slots = table_ref[source, pl.ds(me, 1), :]
+        return lax.broadcasted_iota(jnp.int32, (capacity, length), 0).astype(F32) == slots
+
+    def row_copies(step):
+        return [
+            pltpu.make_async_copy(rows_ref.at[step % 2], rows_out.at[step], row_sem.at[step % 2, 0]),
+            pltpu.make_async_copy(grad_ref.at[step % 2], grad_out.at[step], row_sem.at[step % 2, 1]),
+        ]
+
+    def hidden_copies(step, k, slot):
+        return [
+            pltpu.make_async_copy(
+                stage_f.at[slot, n], out.at[step, :, columns(k * unit, unit)], f_sem.at[slot, n]
+            )
+            for n, out in enumerate([hid_out, da_out, db_out])
+        ]
+
+    def core_copies(step):
+        return [
+            remote(
+                stage.at[1 - core], got.at[n, step], core_send.at[n, step], core_recv.at[n, step], at["dev_c"]
+            )
+            for n, stage in enumerate([stage_s, stage_t])
+        ]
+
+    def total_copies(step):
+        chip = pick_static(order, step, z)
+        return [
+            pltpu.make_async_copy(total.at[n], out.at[chip], tot_sem.at[n])
+            for n, out in enumerate([mix_out, back_out])
+        ]
+
+    def join(step):
+        if step > 0:
+            for copy in total_copies(step - 1):
+                copy.wait()
+        for n, (copy, stage) in enumerate(zip(core_copies(step), [stage_s, stage_t])):
+            copy.wait()
+            total[n] = (stage[core].astype(F32) + got[n, step].astype(F32)).astype(BF16)
+        for copy in total_copies(step):
+            copy.start()
+
+    def expert_rows(step):
+        chip = pick_static(order, step, z)
+        slot = step % 2
+        load_cot(step).wait()
+        if step + 1 < chips:
+            load_cot(step + 1).start()
+        if step >= 2:
+            for copy in row_copies(step - 2):
+                copy.wait()
+        for d in range(2):
+            source, part = 2 * chip + d, pl.ds(d * capacity, capacity)
+            chosen = one_hot(source)
+            select = chosen.astype(F32).astype(BF16)
+            rows_ref[slot, part, :] = dot_nn(select, h2_all[source]).astype(BF16)
+            cot_rows = dot_nn(select, cot_buf[slot, d])
+            scale = jnp.sum(
+                jnp.where(chosen, table_ref[source, pl.ds(experts + me, 1), :], 0.0), axis=1, keepdims=True
+            )
+            grad_ref[slot, part, :] = (cot_rows * scale).astype(BF16)
+            cotr_ref[part, :] = cot_rows.astype(BF16)
+            scale_ref[part, :] = scale
+        for copy in row_copies(step):
+            copy.start()
+        y_acc[...] = jnp.zeros_like(y_acc)
+        r_acc[...] = jnp.zeros_like(r_acc)
+        if step == 0:
+            for load in loads:
+                load.wait()
+
+        @pl.loop(0, units)
+        def _(k):
+            cols = columns(k * unit, unit)
+            hidden, gate_grad, up_grad, result, back = gated_block(
+                rows_ref[slot], grad_ref[slot], gate_w[:, cols], up_w[:, cols],
+                down_w[pl.ds(pl.multiple_of(k * unit, unit), unit), :],
+            )
+            turn = k % 2
+
+            def settle():
+                for copy in hidden_copies(step, k, turn):
+                    copy.wait()
+
+            if step == 0:
+                pl.when(k >= 2)(settle)
+            else:
+                settle()
+            stage_f[turn, 0] = hidden
+            stage_f[turn, 1] = gate_grad
+            stage_f[turn, 2] = up_grad
+            for copy in hidden_copies(step, k, turn):
+                copy.start()
+            y_acc[...] += result
+            r_acc[...] += back
+
+        if step > 0:
+            join(step - 1)
+        result = y_acc[...].astype(BF16).astype(F32)
+        dots = jnp.sum(result * cotr_ref[...].astype(F32), axis=1, keepdims=True)
+        weighted = (result * scale_ref[...]).astype(BF16)
+        back = r_acc[...].astype(BF16)
+        for d in range(2):
+            source = 2 * chip + d
+            chosen = one_hot(source)
+            select = chosen.astype(F32).astype(BF16)
+            part = slice(d * capacity, (d + 1) * capacity)
+            stage_s[d] = dot_tn(select, weighted[part]).astype(BF16)
+            stage_t[d] = dot_tn(select, back[part]).astype(BF16)
+            dots_out[source] = jnp.sum(jnp.where(chosen, dots[part], 0.0), axis=0, keepdims=True)
+        for copy in core_copies(step):
+            copy.start()
+
+    sy_ref[...] = jnp.zeros_like(sy_ref)
+    dh_ref[...] = jnp.zeros_like(dh_ref)
+
+    def shared_copies(k, arrival=False):
+        copies = []
+        for n, held in enumerate((sgg_s, sug_s, sdg_s)):
+            half = held.shape[0] // 2
+            mine, other = (pl.ds(pl.multiple_of(c * half, 16), half) for c in (core, 1 - core))
+            over = remote(held.at[other, :], sgot[n].at[k], sg_send.at[n], sg_recv.at[n, k], at["dev_c"])
+            if arrival:
+                copies.append(over)
+            else:
+                copies += [pltpu.make_async_copy(held.at[mine, :], sown[n].at[k], sg_sem.at[n]), over]
+        return copies
+
+    def shared_settle(k):
+        for copy in shared_copies(k)[::2]:
+            copy.wait()
+        for copy in shared_copies(k, True):
+            copy.wait_send()
+
+    def shared_block(k):
+        slot = k % 2
+        for load in load_shared(k, slot):
+            load.wait()
+
+        @pl.when(k + 1 < shards)
+        def _():
+            for load in load_shared(k + 1, 1 - slot):
+                load.start()
+
+        hidden, gate_grad, up_grad, result, back = gated_block(
+            h2_ref[...], cot_ref[...], sg_w[slot], su_w[slot], sd_w[slot]
+        )
+        sy_ref[...] += result
+        dh_ref[...] += back
+        pl.when(k > 0)(lambda: shared_settle(k - 1))
+        sgg_s[...] = dot_tn(h2_ref[...], gate_grad).astype(BF16)
+        sug_s[...] = dot_tn(h2_ref[...], up_grad).astype(BF16)
+        sdg_s[...] = dot_tn(hidden, cot_ref[...]).astype(BF16)
+        for copy in shared_copies(k):
+            copy.start()
+
+    chain.finish(0)
+    expert_rows(0)
+    pl.loop(0, shards // 2)(shared_block)
+    chain.step(1)
+    pl.loop(shards // 2, shards)(shared_block)
+    for step in range(1, chips):
+        if step > 1:
+            chain.step(step)
+        chain.finish(step)
+        expert_rows(step)
+    join(chips - 1)
+    shared_settle(shards - 1)
+
+    @pl.loop(0, shards)
+    def _(k):
+        for copy in shared_copies(k, True):
+            copy.wait_recv()
+
+    for copy in total_copies(chips - 1):
+        copy.wait()
+    for step in range(max(0, chips - 2), chips):
+        for copy in row_copies(step):
+            copy.wait()
+    for k in range(max(0, units - 2), units):
+        for copy in hidden_copies(chips - 1, k, k % 2):
+            copy.wait()
+    chain.sent()
+
+
+def middle(h2, cot_low, table_all, cot_all, expert_weights, shared_full, ident):
+    length, width = h2.shape
+    group, shards = lax.axis_size("expert"), lax.axis_size("shard")
+    chips = group // 2
+    capacity = 4 * length // group
+    hidden_width = expert_weights[0].shape[2]
+    block = shared_full[0].shape[1]
+    unit = min(512, hidden_width)
+    vmem, anywhere = pl.BlockSpec(memory_space=pltpu.VMEM), pl.BlockSpec(memory_space=pl.ANY)
+    shape = jax.ShapeDtypeStruct
+    both = 2 * capacity
+    out_shape = [
+        shape((chips, both, width), BF16),
+        shape((chips, both, width), BF16),
+        shape((chips, both, hidden_width), BF16),
+        shape((chips, both, hidden_width), BF16),
+        shape((chips, both, hidden_width), BF16),
+        shape((chips, length, width), BF16),
+        shape((chips, length, width), BF16),
+        *[shape((shards, width // 2, block), BF16)] * 2,
+        shape((shards, block // 2, width), BF16),
+        *[shape((shards, width // 2, block), BF16)] * 2,
+        shape((shards, block // 2, width), BF16),
+        shape((group, 1, length), F32),
+        shape((length, width), F32),
+        shape((length, width), F32),
+    ]
+    dma = pltpu.SemaphoreType.DMA
+    scratch = [
+        pltpu.VMEM((width, block), BF16),
+        pltpu.VMEM((width, block), BF16),
+        pltpu.VMEM((block, width), BF16),
+        dma((3,)),
+        dma((3,)),
+        dma((3, shards)),
+        pltpu.VMEM((width, hidden_width), BF16),
+        pltpu.VMEM((width, hidden_width), BF16),
+        pltpu.VMEM((hidden_width, width), BF16),
+        pltpu.VMEM((2, width, block), BF16),
+        pltpu.VMEM((2, width, block), BF16),
+        pltpu.VMEM((2, block, width), BF16),
+        pltpu.VMEM((group, length, width), BF16),
+        pltpu.VMEM((2, 2, length, width), BF16),
+        pltpu.VMEM((2, both, width), BF16),
+        pltpu.VMEM((2, both, width), BF16),
+        pltpu.VMEM((both, width), BF16),
+        pltpu.VMEM((both, 1), F32),
+        pltpu.VMEM((both, width), F32),
+        pltpu.VMEM((both, width), F32),
+        pltpu.VMEM((2, 3, both, unit), BF16),
+        pltpu.VMEM((2, length, width), BF16),
+        pltpu.VMEM((2, length, width), BF16),
+        pltpu.VMEM((2, chips, length, width), BF16),
+        pltpu.VMEM((2, length, width), BF16),
+        dma((3,)),
+        dma((2, 3)),
+        dma((2,)),
+        dma((2, 2)),
+        dma((2, 3)),
+        dma((2,)),
+        dma((2, chips)),
+        dma((2, chips)),
+        dma((ChainGather.copies(chips),)),
+        dma((ChainGather.copies(chips),)),
+        dma,
+    ]
+    return pl.pallas_call(
+        functools.partial(middle_kernel, chips=chips, shards=shards, capacity=capacity),
+        out_shape=out_shape,
+        in_specs=[vmem] * 3 + [anywhere] * 7,
+        out_specs=[anywhere] * 13 + [vmem] * 3,
+        scratch_shapes=scratch,
+        compiler_params=pltpu.CompilerParams(
+            collective_id=ident, has_side_effects=True, vmem_limit_bytes=60 << 20
+        ),
+    )(h2, cot_low, table_all, cot_all, *expert_weights, *shared_full)
+
+
+class ChainReduce:
+    def __init__(self, own, from_left, from_right, send, recv, at, chips):
+        self.own, self.from_left, self.from_right = own, from_left, from_right
+        self.send, self.recv, self.at, self.chips = send, recv, at, chips
+
+    @staticmethod
+    def scratch(shape):
+        return [pltpu.VMEM(shape, BF16)] * 3
+
+    def copy(self, block, right):
+        index = block if right else self.chips + block
+        landing = self.from_left if right else self.from_right
+        return remote(
+            self.own.at[block],
+            landing.at[block],
+            self.send.at[index],
+            self.recv.at[index],
+            self.at["dev_right" if right else "dev_left"],
+        )
+
+    def move(self, step):
+        z, chips = self.at["z"], self.chips
+        far = chips - step
+
+        @pl.when(z < far)
+        def _():
+            @pl.when(z > 0)
+            def _():
+                self.copy(far, True).wait_recv()
+                self.own[far] = (self.own[far].astype(F32) + self.from_left[far].astype(F32)).astype(BF16)
+
+            self.copy(far, True).start()
+
+        near = step - 1
+
+        @pl.when(z > near)
+        def _():
+            @pl.when(z < chips - 1)
+            def _():
+                self.copy(near, False).wait_recv()
+                self.own[near] = (self.own[near].astype(F32) + self.from_right[near].astype(F32)).astype(BF16)
+
+            self.copy(near, False).start()
+
+    def result(self, dst):
+        z, chips = self.at["z"], self.chips
+        dst[...] += self.own[z].astype(F32)
+
+        @pl.when(z > 0)
+        def _():
+            self.copy(z, True).wait_recv()
+            dst[...] += self.from_left[z].astype(F32)
+
+        @pl.when(z < chips - 1)
+        def _():
+            self.copy(z, False).wait_recv()
+            dst[...] += self.from_right[z].astype(F32)
+
+    def sent(self):
+        for step in range(1, self.chips):
+            pl.when(self.at["z"] < self.chips - step)(lambda: self.copy(self.chips - step, True).wait_send())
+            pl.when(self.at["z"] > step - 1)(lambda: self.copy(step - 1, False).wait_send())
+
+
+class PlaneReduce:
+    COPIES = 6
+
+    def __init__(self, src, got, hold, last, send, recv, at):
+        self.src, self.got, self.hold, self.last = src, got, hold, last
+        self.send, self.recv, self.at = send, recv, at
+        self.half = src.shape[1] // 2
+
+    @staticmethod
+    def scratch(shape):
+        half = shape[1] // 2
+        return [
+            pltpu.VMEM((4, half, shape[2]), BF16),
+            pltpu.VMEM((2, half, shape[2]), BF16),
+            pltpu.VMEM((2, half, shape[2]), BF16),
+        ]
+
+    def send_to(self, src, dst, index, device):
+        made = remote(src, dst, self.send.at[index], self.recv.at[index], device)
+        made.start()
+        return made
+
+    def first(self):
+        at, half = self.at, self.half
+        upper, lower = pl.ds(0, half), pl.ds(half, half)
+        self.out = [
+            self.send_to(self.src.at[shard, rows, :], self.got.at[slot], slot, device)
+            for slot, (shard, rows, device) in enumerate(
+                [
+                    (at["sx"], upper, at["dev_x"]),
+                    (at["sd"], upper, at["dev_x"]),
+                    (at["sy"], lower, at["dev_y"]),
+                    (at["sd"], lower, at["dev_y"]),
+                ]
+            )
+        ]
+
+    def second(self):
+        at, half = self.at, self.half
+        for slot, shard, device in ((1, at["sy"], at["dev_y"]), (3, at["sx"], at["dev_x"])):
+            self.out[slot].wait_recv()
+            turn = slot // 2
+            mine = self.src[shard, pl.ds(turn * half, half), :]
+            self.hold[turn] = (mine.astype(F32) + self.got[slot].astype(F32)).astype(BF16)
+            self.out.append(self.send_to(self.hold.at[turn], self.last.at[turn], 4 + turn, device))
+
+    def value(self, turn):
+        half = self.half
+        self.out[2 * turn].wait_recv()
+        self.out[4 + turn].wait_recv()
+        mine = self.src[self.at["shard"], pl.ds(turn * half, half), :]
+        return (mine.astype(F32) + self.got[2 * turn].astype(F32)) + self.last[turn].astype(F32)
+
+    def sent(self):
+        for made in self.out:
+            made.wait_send()
+
+
+def plane_blocks(at, index, plane):
+    if not plane:
+        return index
+    order = [at["sd"], at["sx"], at["sy"], at["shard"]]
+    return sum(jnp.where(index == k, shard, 0) for k, shard in enumerate(order))
+
+
+def weights_kernel(*refs, plane, chips, shards):
+    (rows_ref, grad_ref, dh_ref, hid_hbm, da_hbm, db_hbm, back_hbm), refs = refs[:7], refs[7:]
+    (gate_out, up_out, down_out, sum_ref), refs = refs[:4], refs[4:]
+    (chunk, own, from_left, from_right), refs = refs[:4], refs[4:]
+    own_sem, chunk_sem, chain_send, chain_recv = refs[:4]
+    block = chunk.shape[-1]
+    at = place()
+    chain_meet(at, chips, [at["dev_x"], at["dev_y"]] if plane else [])
+    load = pltpu.make_async_copy(back_hbm, own, own_sem)
+    load.start()
+    if plane:
+        send, recv = refs[4:6]
+        work = refs[6:]
+        reduces = [
+            PlaneReduce(work[4 * k], *work[4 * k + 1 : 4 * k + 4], send.at[k], recv.at[k], at) for k in range(2)
+        ]
+        targets = [work[0], work[4], down_out]
+    else:
+        targets = [gate_out, up_out, down_out]
+    sources = [da_hbm, db_hbm, hid_hbm]
+
+    def fetch(array, index):
+        shard = plane_blocks(at, index, plane)
+        slot = index % 2
+        return pltpu.make_async_copy(
+            sources[array].at[:, columns(shard * block, block)], chunk.at[slot], chunk_sem.at[slot]
+        )
+
+    def make(array):
+        @pl.loop(0, shards)
+        def _(index):
+            fetch(array, index).wait()
+            pl.when(index + 1 < shards)(lambda: fetch(array, index + 1).start())
+            if array < 2:
+                pl.when(index + 1 == shards)(lambda: fetch(array + 1, 0).start())
+            shard = plane_blocks(at, index, plane)
+            held = chunk[index % 2]
+            if array < 2:
+                targets[array][shard] = dot_tn(rows_ref[...], held).astype(BF16)
+            else:
+                targets[array][shard] = dot_tn(held, grad_ref[...]).astype(BF16)
+
+    fetch(0, 0).start()
+    chain = ChainReduce(own, from_left, from_right, chain_send, chain_recv, at, chips)
+    load.wait()
+    chain.move(1)
+    for array in range(3):
+        make(array)
+        if plane and array < 2:
+            reduces[array].first()
+        if array == 1:
+            for step in range(2, chips - 1):
+                chain.move(step)
+    if plane:
+        reduces[0].second()
+    chain.move(chips - 1)
+    if plane:
+        reduces[1].second()
+    sum_ref[...] = dh_ref[...]
+    chain.result(sum_ref)
+    chain.sent()
+    if plane:
+        for reduce, out in zip(reduces, (gate_out, up_out)):
+            for turn in range(2):
+                out[pl.ds(turn * reduce.half, reduce.half), :] = reduce.value(turn)
+            reduce.sent()
+
+
+def weights(rows, grad_rows, shared_back, hidden, gate_grad, up_grad, back_part, ident):
+    chips, length, width = back_part.shape
+    shards = lax.axis_size("shard")
+    plane = shards == 4
+    count, hidden_width = hidden.shape
+    block = hidden_width // shards
+    vmem, anywhere = pl.BlockSpec(memory_space=pltpu.VMEM), pl.BlockSpec(memory_space=pl.ANY)
+    shape, dma = jax.ShapeDtypeStruct, pltpu.SemaphoreType.DMA
+    wide = (shards, width, block)
+    scratch = [pltpu.VMEM((2, count, block), BF16)] + ChainReduce.scratch((chips, length, width))
+    scratch += [dma, dma((2,)), dma((2 * chips,)), dma((2 * chips,))]
+    if plane:
+        out_shape = [shape((width, block), F32)] * 2
+        scratch += [dma((2, PlaneReduce.COPIES))] * 2
+        scratch += ([pltpu.VMEM(wide, BF16)] + PlaneReduce.scratch(wide)) * 2
+    else:
+        out_shape = [shape(wide, BF16)] * 2
+    out_shape += [shape((shards, block, width), BF16), shape((length, width), F32)]
+    return pl.pallas_call(
+        functools.partial(weights_kernel, plane=plane, chips=chips, shards=shards),
+        out_shape=out_shape,
+        in_specs=[vmem] * 3 + [anywhere] * 4,
+        out_specs=[vmem] * 4,
+        scratch_shapes=scratch,
+        compiler_params=pltpu.CompilerParams(
+            collective_id=ident, has_side_effects=True, vmem_limit_bytes=60 << 20
+        ),
+    )(rows, grad_rows, shared_back, hidden, gate_grad, up_grad, back_part)
+
+
+def norm_back(source, inverse, gain, grad_in):
+    scaled = grad_in * gain
+    gain_grad = jnp.sum(grad_in * source * inverse, axis=0, keepdims=True)
+    input_part = inverse * scaled - source * inverse**3 * jnp.mean(
+        scaled * source, axis=-1, keepdims=True
+    )
+    return (gain_grad, input_part)
+
+
+def rear_kernel(*refs, plane, chips, shards):
+    (prefix, x_ref, cot_ref, resid_ref, dh_ref, gains_ref, rot_ref, att_ref, h1_ref, lse_ref), refs = refs[:10], refs[10:]
+    (qkv_ref, out_ref, cos_ref, sin_ref, mix_hbm), refs = refs[:5], refs[5:]
+    if plane:
+        halves, refs = refs[:6], refs[6:]
+    (mix_out, input_grad_ref, qkv_grad_ref, out_grad_ref), refs = refs[:4], refs[4:]
+    if plane:
+        pieces, refs = refs[:3], refs[3:]
+    (bias_ref, dres_ref, datt_ref, dqkv_ref, own, from_left, from_right), refs = refs[:7], refs[7:]
+    own_sem, chain_send, chain_recv = refs[:3]
+    length, width = x_ref.shape
+    at = place()
+    chain_meet(at, chips, [at["dev_x"], at["dev_y"]] if plane else [])
+    load = pltpu.make_async_copy(mix_hbm, own, own_sem)
+    load.start()
+    if plane:
+        send, recv, half_sem = refs[3:6]
+        work = [refs[6 + 5 * k : 11 + 5 * k] for k in range(3)]
+        loads = [
+            [
+                pltpu.make_async_copy(halves[2 * k + n], work[k][n], half_sem.at[k, n])
+                for n in range(2)
+            ]
+            for k in range(3)
+        ]
+        for two in loads:
+            for made in two:
+                made.start()
+        reduces = [PlaneReduce(work[k][0], *work[k][2:], send.at[k], recv.at[k], at) for k in range(3)]
+    chain = ChainReduce(own, from_left, from_right, chain_send, chain_recv, at, chips)
+    load.wait()
+    chain.move(1)
+    if plane:
+        for k in range(3):
+            for made in loads[k]:
+                made.wait()
+
+            @pl.loop(0, shards)
+            def _(shard):
+                work[k][0][shard] = (
+                    work[k][0][shard].astype(F32) + work[k][1][shard].astype(F32)
+                ).astype(BF16)
+
+            reduces[k].first()
+    blocks = gains_ref.shape[0] // 64
+    gain_one = sum(gains_ref[pl.ds(64 * k, 1), :].astype(F32) for k in range(blocks))
+    gain_two = sum(gains_ref[pl.ds(64 * k + 32, 1), :].astype(F32) for k in range(blocks))
+    resid = resid_ref[...]
+    inverse = lax.rsqrt(jnp.mean(resid * resid, axis=-1, keepdims=True) + EPS)
+    gain_two_grad, extra = norm_back(resid, inverse, gain_two, dh_ref[...])
+    dres = cot_ref[...] + extra
+    dres_ref[...] = dres
+    low = dres.astype(BF16)
+    datt_ref[...] = dot_nt(low, out_ref[...]).astype(BF16)
+    out_grad = dot_tn(att_ref[...], low).astype(BF16)
+    rows = width // shards
+    for k in range(shards):
+        out_grad_ref[k, :rows, :] = out_grad[k * rows : (k + 1) * rows]
+    row = lax.broadcasted_iota(jnp.int32, (length, length), 0)
+    col = lax.broadcasted_iota(jnp.int32, (length, length), 1)
+    bias_ref[...] = jnp.where((col < prefix[0]) | (col <= row), 0.0, -1e30)
+    scale = HEAD_DIM**-0.5
+
+    def pair(j):
+        cols = columns(j * 128, 128)
+        queries, keys, values = (
+            rot_ref[:, columns(part * width + j * 128, 128)] for part in range(3)
+        )
+        grads = datt_ref[:, cols]
+        low_lanes = lax.broadcasted_iota(jnp.int32, (length, 128), 1) < HEAD_DIM
+        lanes = lax.broadcasted_iota(jnp.int32, (length, 128), 1)
+        parts = []
+        for head in range(2):
+            mine = low_lanes if head == 0 else ~low_lanes
+            query = jnp.where(mine, queries, 0.0) * scale
+            grad = jnp.where(mine, grads, 0.0).astype(BF16)
+            logsum = jnp.sum(jnp.where(lanes == 2 * j + head, lse_ref[...], 0.0), axis=1, keepdims=True)
+            probs = jnp.exp(dot_nt(query.astype(BF16), keys) + bias_ref[...] - logsum)
+            probs_grad = dot_nt(grad, values)
+            inner = jnp.sum(probs * probs_grad, axis=-1, keepdims=True)
+            score_grad = (probs * (probs_grad - inner)).astype(BF16)
+            parts.append(
+                (
+                    dot_nn(score_grad, keys) * scale,
+                    dot_tn(score_grad, queries) * scale,
+                    dot_tn(probs.astype(BF16), grads),
+                )
+            )
+        for part in range(3):
+            both = jnp.where(low_lanes, parts[0][part], parts[1][part])
+            if part < 2:
+                both = both * cos_ref[...] - partner(both) * sin_ref[...]
+            dqkv_ref[:, columns(part * width + j * 128, 128)] = both.astype(BF16)
+
+    pairs = width // 128
+    pl.loop(0, pairs // 2)(pair)
+    for step in range(2, chips - 1):
+        chain.move(step)
+    if plane:
+        reduces[0].second()
+    pl.loop(pairs // 2, pairs)(pair)
+    chain.move(chips - 1)
+    if plane:
+        reduces[1].second()
+        reduces[2].second()
+
+    @pl.loop(0, 3 * width // 256)
+    def _(k):
+        cols = columns(k * 256, 256)
+        qkv_grad_ref[:, cols] = dot_tn(h1_ref[...], dqkv_ref[:, cols]).astype(BF16)
+
+    dh1 = dot_nt(dqkv_ref[...], qkv_ref[...])
+    x = x_ref[...]
+    inverse = lax.rsqrt(jnp.mean(x * x, axis=-1, keepdims=True) + EPS)
+    gain_one_grad, extra = norm_back(x, inverse, gain_one, dh1)
+    input_grad_ref[...] = dres_ref[...] + extra
+    index = lax.broadcasted_iota(jnp.int32, (64, width), 0)
+    gain_rows = jnp.where(index == 0, gain_one_grad, jnp.where(index == 1, gain_two_grad, 0.0)).astype(BF16)
+    for k in range(shards):
+        out_grad_ref[k, rows:, :] = gain_rows
+    mix_out[...] = jnp.zeros_like(mix_out)
+    chain.result(mix_out)
+    chain.sent()
+    if plane:
+        for reduce, piece in zip(reduces, pieces):
+            count = piece.shape[1]
+            both = jnp.concatenate([reduce.value(0), reduce.value(1)], axis=0)
+            for k in range(chips):
+                piece[k] = both[k * count : (k + 1) * count].astype(BF16)
+            reduce.sent()
+
+
+def rear(prefix, inputs, cotangent, resid, dh2, gains_full, kept, full, mix_part, halves, ident):
+    length, width = inputs.shape
+    chips, shards = mix_part.shape[0], lax.axis_size("shard")
+    plane = shards == 4
+    cosine, sine = rope_lanes(length)
+    vmem, anywhere = pl.BlockSpec(memory_space=pltpu.VMEM), pl.BlockSpec(memory_space=pl.ANY)
+    shape, dma = jax.ShapeDtypeStruct, pltpu.SemaphoreType.DMA
+    operands = [prefix, inputs, cotangent, resid, dh2, gains_full, *kept, *full, cosine, sine, mix_part]
+    in_specs = [pl.BlockSpec(memory_space=pltpu.SMEM)] + [vmem] * 13 + [anywhere]
+    out_shape = [
+        shape((length, width), F32),
+        shape((length, width), F32),
+        shape((width, 3 * width), BF16),
+        shape((shards, width // shards + 64, width), BF16),
+    ]
+    scratch = [
+        pltpu.VMEM((length, length), F32),
+        pltpu.VMEM((length, width), F32),
+        pltpu.VMEM((length, width), BF16),
+        pltpu.VMEM((length, 3 * width), BF16),
+        *ChainReduce.scratch((chips, length, width)),
+        dma,
+        dma((2 * chips,)),
+        dma((2 * chips,)),
+    ]
+    if plane:
+        operands += halves
+        in_specs += [anywhere] * 6
+        scratch += [dma((3, PlaneReduce.COPIES))] * 2 + [dma((3, 2))]
+        for half in halves[::2]:
+            out_shape.append(shape((chips, half.shape[1] // chips, half.shape[2]), BF16))
+            scratch += [pltpu.VMEM(half.shape, BF16)] * 2 + PlaneReduce.scratch(half.shape)
+    return pl.pallas_call(
+        functools.partial(rear_kernel, plane=plane, chips=chips, shards=shards),
+        out_shape=out_shape,
+        in_specs=in_specs,
+        out_specs=[vmem] * len(out_shape),
+        scratch_shapes=scratch,
+        compiler_params=pltpu.CompilerParams(
+            collective_id=ident, has_side_effects=True, vmem_limit_bytes=60 << 20
+        ),
+    )(*operands)
+
+
+def last_kernel(*refs, chips, shards):
+    (resid_ref, mix_ref, sy_ref), refs = refs[:3], refs[3:]
+    attention, pieces, down_hbm, refs = refs[:2], refs[2:5], refs[5], refs[6:]
+    output_ref, grads, refs = refs[0], refs[1:7], refs[7:]
+    halves, refs = refs[:4], refs[4:]
+    plane_work, refs = refs[:10], refs[10:]
+    chain_work, refs = refs[:25], refs[25:]
+    load_sem, core_send, core_recv, plane_send, plane_recv, sums_send, sums_recv, all_send, all_recv, all_local = refs
+    at = place()
+    core = at["core"]
+    chain_meet(at, chips, [at["dev_x"], at["dev_y"], at["dev_c"]])
+    swaps, loads = [], []
+    for k in range(2):
+        rows = attention[k].shape[1] // 2
+        part = lambda c: attention[k].at[:, pl.ds(pl.multiple_of(c * rows, 16), rows), :]
+        swaps.append(
+            remote(part(1 - core), halves[2 * k + 1], core_send.at[k], core_recv.at[k], at["dev_c"])
+        )
+        loads.append(pltpu.make_async_copy(part(core), halves[2 * k], load_sem.at[k]))
+    chain_work = [chain_work[5 * k : 5 * k + 5] for k in range(5)]
+    loads += [pltpu.make_async_copy(pieces[k], chain_work[2 + k][0], load_sem.at[2 + k]) for k in range(3)]
+    loads.append(pltpu.make_async_copy(down_hbm, plane_work[0], load_sem.at[5]))
+    for made in swaps + loads:
+        made.start()
+    sums = [
+        ChainReduce(*chain_work[k][:3], sums_send.at[k], sums_recv.at[k], at, chips) for k in range(5)
+    ]
+    alls = [
+        ChainGather(chain_work[k][3], chain_work[k][4], all_send.at[k], all_recv.at[k], all_local.at[k], at, chips)
+        for k in range(5)
+    ]
+    planes = [
+        PlaneReduce(src, *plane_work[1 + 3 * k : 4 + 3 * k], plane_send.at[k], plane_recv.at[k], at)
+        for k, src in enumerate([plane_work[0], halves[0], halves[2]])
+    ]
+    ahead = (2, 3, 4)
+    for k in ahead:
+        loads[k].wait()
+        sums[k].move(1)
+    for k in range(2):
+        swaps[k].wait()
+        loads[k].wait()
+
+        @pl.loop(0, shards)
+        def _(shard):
+            halves[2 * k][shard] = (
+                halves[2 * k][shard].astype(F32) + halves[2 * k + 1][shard].astype(F32)
+            ).astype(BF16)
+
+        planes[1 + k].first()
+    loads[5].wait()
+    planes[0].first()
+    output_ref[...] = resid_ref[...] + mix_ref[...] + sy_ref[...]
+    for step in range(2, chips):
+        for k in ahead:
+            sums[k].move(step)
+        if step == 2:
+            planes[1].second()
+            planes[2].second()
+
+    def total(k):
+        total_ref = chain_work[k][3]
+        z = at["z"]
+        value = sums[k].own[z].astype(F32)
+        pl.when(z > 0)(lambda: sums[k].copy(z, True).wait_recv())
+        pl.when(z < chips - 1)(lambda: sums[k].copy(z, False).wait_recv())
+        value += jnp.where(z > 0, sums[k].from_left[z].astype(F32), 0.0)
+        value += jnp.where(z < chips - 1, sums[k].from_right[z].astype(F32), 0.0)
+        total_ref[...] = value.astype(BF16)
+        alls[k].start()
+
+    for k in ahead:
+        total(k)
+    for k in range(2):
+        count = chain_work[k][0].shape[1]
+        both = jnp.concatenate([planes[1 + k].value(0), planes[1 + k].value(1)], axis=0)
+        for n in range(chips):
+            sums[k].own[n] = both[n * count : (n + 1) * count].astype(BF16)
+        sums[k].move(1)
+    for step in range(2, chips):
+        for k in range(2):
+            sums[k].move(step)
+        for k in ahead:
+            alls[k].step(step - 1)
+    for k in range(2):
+        total(k)
+    for k in ahead:
+        alls[k].step(chips - 1)
+    planes[0].second()
+    for step in range(1, chips):
+        for k in range(2):
+            alls[k].step(step)
+
+    def spread(k):
+        for step in range(chips):
+            alls[k].finish(step)
+        alls[k].sent()
+        sums[k].sent()
+        count = chain_work[k][0].shape[1]
+        for n in range(chips):
+            for c in range(2):
+                grads[k][pl.ds((c * chips + n) * count, count), :] = chain_work[k][4][2 * n + c].astype(F32)
+
+    for k in ahead:
+        spread(k)
+    for turn in range(2):
+        grads[5][pl.ds(turn * planes[0].half, planes[0].half), :] = planes[0].value(turn)
+    for k in range(2):
+        spread(k)
+    for reduce in planes:
+        reduce.sent()
+
+
+def last(resid, mixture, shared_out, qkv_grad, out_grad, pieces, down_blocks, ident):
+    length, width = resid.shape
+    shards, chips = lax.axis_size("shard"), lax.axis_size("expert") // 2
+    vmem, anywhere = pl.BlockSpec(memory_space=pltpu.VMEM), pl.BlockSpec(memory_space=pl.ANY)
+    shape, dma = jax.ShapeDtypeStruct, pltpu.SemaphoreType.DMA
+    attention = [qkv_grad, out_grad]
+    half_shapes = [(shards, v.shape[1] // 2, v.shape[2]) for v in attention]
+    chain_shapes = [(chips, v.shape[1] // 2 // chips, v.shape[2]) for v in attention] + [v.shape for v in pieces]
+    out_shape = [shape((length, width), F32)]
+    out_shape += [shape((2 * s[0] * s[1], s[2]), F32) for s in chain_shapes]
+    out_shape.append(shape(down_blocks.shape[1:], F32))
+    scratch = []
+    for s in half_shapes:
+        scratch += [pltpu.VMEM(s, BF16)] * 2
+    scratch.append(pltpu.VMEM(down_blocks.shape, BF16))
+    for s in [down_blocks.shape] + half_shapes:
+        scratch += PlaneReduce.scratch(s)
+    for s in chain_shapes:
+        scratch += ChainReduce.scratch(s)
+        scratch += [pltpu.VMEM(s[1:], BF16), pltpu.VMEM((2 * chips,) + s[1:], BF16)]
+    scratch += [
+        dma((6,)),
+        dma((2,)),
+        dma((2,)),
+        dma((3, PlaneReduce.COPIES)),
+        dma((3, PlaneReduce.COPIES)),
+        dma((5, 2 * chips)),
+        dma((5, 2 * chips)),
+        dma((5, ChainGather.copies(chips))),
+        dma((5, ChainGather.copies(chips))),
+        dma((5,)),
+    ]
+    return pl.pallas_call(
+        functools.partial(last_kernel, chips=chips, shards=shards),
+        out_shape=out_shape,
+        in_specs=[vmem] * 3 + [anywhere] * 6,
+        out_specs=[vmem] * 7,
+        scratch_shapes=scratch,
+        compiler_params=pltpu.CompilerParams(
+            collective_id=ident, has_side_effects=True, vmem_limit_bytes=60 << 20
+        ),
+    )(resid, mixture, shared_out, qkv_grad, out_grad, *pieces, down_blocks)
+
+
 def on_device(
     inputs,
     cotangent,
@@ -629,17 +1337,14 @@
     routes,
     prefix,
 ):
-    length, model_width = inputs.shape
-    experts = lax.axis_size("expert") * expert_gate.shape[0]
-    shards = lax.axis_size("shard")
-    me = lax.axis_index("expert")
-    shards_at = lax.axis_index("shard")
-    capacity = 4 * length // experts
+    length, width = inputs.shape
+    experts, shards = lax.axis_size("expert"), lax.axis_size("shard")
+    me, shard = lax.axis_index("expert"), lax.axis_index("shard")
     gains = jnp.concatenate(
         [jnp.broadcast_to(v, (32, v.shape[0])) for v in (norm_one, norm_two)], axis=0
     )
     gains = lax.dynamic_update_slice(
-        jnp.zeros((64, model_width), BF16), gains, (0, shards_at * norm_one.shape[0])
+        jnp.zeros((64, width), BF16), gains, (0, shard * norm_one.shape[0])
     )
     (
         cot_all,
@@ -650,7 +1355,7 @@
         logsum,
         resid,
         normed_two,
-        out_low,
+        cot_low,
         qkv_full,
         out_full,
         gains_full,
@@ -669,160 +1374,88 @@
         [shared_gate, shared_up, shared_down],
         1,
     )
-    table_mine = jnp.stack(
-        [lax.dynamic_index_in_dim(table_all, me + k * experts, axis=1, keepdims=False) for k in range(2)], axis=1
-    )
-    gain_rows = jnp.sum(gains_full.reshape(shards, 64, model_width).astype(F32), axis=0)
-    gain_one, gain_two = gain_rows[0], gain_rows[32]
-    inverse_one = lax.rsqrt(jnp.mean(inputs * inputs, axis=-1, keepdims=True) + EPS)
-    inverse_two = lax.rsqrt(jnp.mean(resid * resid, axis=-1, keepdims=True) + EPS)
-    normed_all = lax.all_gather(normed_two, "expert", axis=0)
-    gate_full = gate_blocks.reshape(shards, model_width, -1).transpose(1, 0, 2).reshape(model_width, -1)
-    up_full = up_blocks.reshape(shards, model_width, -1).transpose(1, 0, 2).reshape(model_width, -1)
-    cosine_table, sine_table = rope_tables(length)
-    head_shape = (length, HEADS, HEAD_DIM)
-    queries, key_rows, value_rows = (
-        turned[:, k * model_width : (k + 1) * model_width].reshape(head_shape) for k in range(3)
-    )
-    logsum = logsum[:, :HEADS].T[:, :, None]
-    score_scale = HEAD_DIM ** (-0.5)
-    row_pos = lax.broadcasted_iota(jnp.int32, (length, length), 0)
-    col_pos = lax.broadcasted_iota(jnp.int32, (length, length), 1)
-    visible = (col_pos < prefix[0]) | (col_pos <= row_pos)
-
-    def masked_scores():
-        raw_scores = (
-            jnp.einsum("qhd,khd->hqk", queries, key_rows, preferred_element_type=F32) * score_scale
+    (
+        rows,
+        grad_rows,
+        hidden,
+        gate_pre_grad,
+        up_pre_grad,
+        mix_part,
+        back_part,
+        *shared_halves,
+        weight_back,
+        shared_out,
+        shared_back,
+    ) = middle(
+        normed_two,
+        cot_low,
+        table_all,
+        cot_all,
+        [expert_gate, expert_up, expert_down],
+        [gate_blocks, up_blocks, down_full],
+        2,
+    )
+    shared_halves = [shared_halves[k + n] for k in range(3) for n in (0, 3)]
+    weight_got = lax.all_to_all(
+        weight_back.reshape(experts, length), "expert", split_axis=0, concat_axis=0, tiled=True
+    )
+    chosen = routes[:, :, None] == jnp.arange(experts, dtype=jnp.int32)[None, None, :]
+    gate_weights_grad = jnp.sum(jnp.where(chosen, weight_got.T[:, None, :], 0.0), axis=2)
+    rows, grad_rows, hidden, gate_pre_grad, up_pre_grad = (
+        v.reshape(-1, v.shape[-1]) for v in (rows, grad_rows, hidden, gate_pre_grad, up_pre_grad)
+    )
+    gate_term, up_term, down_term, normed_two_grad = weights(
+        rows, grad_rows, shared_back, hidden, gate_pre_grad, up_pre_grad, back_part, 3
+    )
+    mixture, input_grad, qkv_grad, out_grad, *pieces = rear(
+        prefix,
+        inputs,
+        cotangent,
+        resid,
+        normed_two_grad,
+        gains_full,
+        [turned, attended, normed_one, logsum],
+        [qkv_full, out_full],
+        mix_part,
+        shared_halves,
+        4,
+    )
+    qkv_grad = qkv_grad.reshape(shards, width // shards, 3 * width)
+    if shards == 4:
+        output, qkv_sum, out_sum, *shared_sums, down_term = last(
+            resid, mixture, shared_out, qkv_grad, out_grad, pieces, down_term, 5
         )
-        return jnp.where(visible[None], raw_scores, -1e30)
-
-    shared_pre = matmul(normed_two, gate_full)
-    shared_lift = matmul(normed_two, up_full)
-    shared_act, shared_slope = gated_unit(shared_pre)
-    shared_hidden = (shared_act * shared_lift).astype(BF16)
-    shared_out = matmul(shared_hidden, down_full)
-    shared_down_grad = matmul(shared_hidden.T, out_low)
-    shared_hgrad = matmul(out_low, down_full.T)
-    shared_pre_grad = (shared_hgrad * shared_lift * shared_slope).astype(BF16)
-    shared_lift_grad = (shared_hgrad * shared_act).astype(BF16)
-    shared_gate_grad = matmul(normed_two.T, shared_pre_grad)
-    shared_up_grad = matmul(normed_two.T, shared_lift_grad)
-    shared_back = matmul(shared_pre_grad, gate_full.T) + matmul(shared_lift_grad, up_full.T)
-
-    pick = (
-        jnp.arange(capacity, dtype=F32)[None, :, None] == table_mine[:, 0][:, None, :]
-    ).astype(BF16)
-    weight_rows = jnp.sum(pick.astype(F32) * table_mine[:, 1][:, None, :], axis=2)
-
-    def to_rows(values):
-        return jnp.einsum("ect,etd->ecd", pick, values, preferred_element_type=F32)
-
-    def to_tokens(rows):
-        return jnp.einsum("ect,ecd->etd", pick, rows, preferred_element_type=F32)
-
-    gate_local, up_local, down_local = expert_gate[0], expert_up[0], expert_down[0]
-    row_count = experts * capacity
-    rows = to_rows(normed_all).astype(BF16).reshape(row_count, model_width)
-    cot_rows = to_rows(cot_all)
-    grad_rows = (cot_rows * weight_rows[:, :, None]).astype(BF16).reshape(row_count, model_width)
-    pre_gate = matmul(rows, gate_local)
-    pre_up = matmul(rows, up_local)
-    activated, derivative = gated_unit(pre_gate)
-    hidden = (activated * pre_up).astype(BF16)
-    hidden_grad = matmul(grad_rows, down_local.T)
-    gate_pre_grad = (hidden_grad * pre_up * derivative).astype(BF16)
-    up_pre_grad = (hidden_grad * activated).astype(BF16)
-    row_grad = (matmul(gate_pre_grad, gate_local.T) + matmul(up_pre_grad, up_local.T)).astype(BF16)
-    back_part = to_tokens(row_grad.reshape(experts, capacity, model_width)).astype(BF16)
-    back = lax.psum_scatter(back_part, "expert", scatter_dimension=0, tiled=False).astype(F32)
-
-    result = matmul(hidden, down_local).astype(BF16).reshape(experts, capacity, model_width)
-    weighted = (result.astype(F32) * weight_rows[:, :, None]).astype(BF16)
-    mix_part = to_tokens(weighted).astype(BF16)
-    mixture = lax.psum_scatter(mix_part, "expert", scatter_dimension=0, tiled=False).astype(F32)
-    weight_dot = jnp.sum(result.astype(F32) * cot_rows, axis=2)
-    weight_back = jnp.einsum("ect,ec->et", pick.astype(F32), weight_dot, precision=lax.Precision.HIGHEST)
-    weight_got = lax.all_to_all(weight_back, "expert", split_axis=0, concat_axis=0, tiled=True)
-    onehot = routes[:, :, None] == jnp.arange(experts, dtype=jnp.int32)[None, None, :]
-    gate_weights_grad = jnp.sum(jnp.where(onehot, weight_got.T[:, None, :], 0.0), axis=2)
-
-    def blocks_of_columns(value):
-        width = value.shape[1] // shards
-        return value.astype(BF16).reshape(value.shape[0], shards, width).transpose(1, 0, 2)
-
-    def blocks_of_rows(value):
-        return value.astype(BF16).reshape(shards, value.shape[0] // shards, value.shape[1])
-
-    gate_term = matmul(rows.T, gate_pre_grad)
-    up_term = matmul(rows.T, up_pre_grad)
-    down_term = matmul(hidden.T, grad_rows)
-    expert_gate_grad, expert_up_grad, expert_down_grad = plane_reduce(
-        [blocks_of_columns(gate_term), blocks_of_columns(up_term), blocks_of_rows(down_term)], 3
-    )
-
-    output = resid + mixture + shared_out
-    normed_two_grad = shared_back + back
-    gain_two_grad, resid_extra = norm_back(resid, inverse_two, gain_two, normed_two_grad)
-    resid_grad = cotangent + resid_extra
-    attn_low = resid_grad.astype(BF16)
-    out_weight_grad = matmul(attended.T, attn_low)
-    attended_grad = matmul(attn_low, out_full.T).astype(BF16).reshape(head_shape)
-    scores = masked_scores()
-    probs_full = jnp.exp(scores - logsum)
-    value_grad = jnp.einsum(
-        "hqk,qhd->khd", probs_full.astype(BF16), attended_grad, preferred_element_type=F32
-    )
-    probs_grad = jnp.einsum("qhd,khd->hqk", attended_grad, value_rows, preferred_element_type=F32)
-    score_grad = (
-        probs_full * (probs_grad - jnp.sum(probs_full * probs_grad, axis=-1, keepdims=True))
-    ).astype(BF16)
-    query_grad = (
-        jnp.einsum("hqk,khd->qhd", score_grad, key_rows, preferred_element_type=F32) * score_scale
-    )
-    key_grad = (
-        jnp.einsum("hqk,qhd->khd", score_grad, queries, preferred_element_type=F32) * score_scale
-    )
-    projected_grad = jnp.concatenate(
-        [
-            rotate(query_grad, cosine_table, -sine_table).reshape(length, model_width),
-            rotate(key_grad, cosine_table, -sine_table).reshape(length, model_width),
-            value_grad.reshape(length, model_width),
-        ],
-        axis=1,
-    ).astype(BF16)
-    qkv_weight_grad = matmul(normed_one.T, projected_grad)
-    normed_one_grad = matmul(projected_grad, qkv_full.T)
-    gain_one_grad, input_extra = norm_back(inputs, inverse_one, gain_one, normed_one_grad)
-    input_grad = resid_grad + input_extra
-
-    gain_block = jnp.zeros((shards, 32, model_width // shards), BF16)
-    gain_block = gain_block.at[:, 0, :].set(gain_one_grad.astype(BF16).reshape(shards, -1))
-    gain_block = gain_block.at[:, 1, :].set(gain_two_grad.astype(BF16).reshape(shards, -1))
-    pieces = plane_reduce(
-        [
-            blocks_of_rows(qkv_weight_grad),
-            blocks_of_rows(out_weight_grad),
-            gain_block,
-            blocks_of_columns(shared_gate_grad),
-            blocks_of_columns(shared_up_grad),
-            blocks_of_rows(shared_down_grad),
-        ],
-        4,
-    )
-    summed = [lax.psum(v.astype(BF16), "expert").astype(F32) for v in pieces]
+    else:
+
+        def over_plane(value):
+            return lax.psum_scatter(value, "shard", scatter_dimension=0, tiled=True)[0]
+
+        def over_all(value):
+            return lax.psum(over_plane(value), "expert").astype(F32)
+
+        output = resid + mixture + shared_out
+        gate_term, up_term, down_term = (
+            over_plane(v).astype(F32) for v in (gate_term, up_term, down_term)
+        )
+        qkv_sum, out_sum = over_all(qkv_grad), over_all(out_grad)
+        shared_sums = []
+        for own, got in zip(shared_halves[::2], shared_halves[1::2]):
+            half = (own.astype(F32) + got.astype(F32)).astype(BF16)
+            both = jnp.concatenate([jnp.where(me % 2 == c, half, 0) for c in range(2)], axis=1)
+            shared_sums.append(over_all(both))
+    part = width // shards
+    gain_grads = lax.dynamic_slice(out_sum[part : part + 2], (0, shard * part), (2, part))
     return (
         output,
         input_grad,
-        summed[2][0],
-        summed[0],
-        summed[1],
-        summed[2][1],
-        summed[3],
-        summed[4],
-        summed[5],
-        expert_gate_grad[None],
-        expert_up_grad[None],
-        expert_down_grad[None],
+        gain_grads[0],
+        qkv_sum,
+        out_sum[:part],
+        gain_grads[1],
+        *shared_sums,
+        gate_term[None],
+        up_term[None],
+        down_term[None],
         gate_weights_grad,
     )
 

time: 707 us -> 542 us (0.77)
  Pallas kernels: 283 us -> 499 us
  matrix products: 199 us -> 0 us
  local copies, waits for them, and re-layouts: 90.5 us -> 28.6 us
  waiting for transfers between devices: 42.9 us -> 0.01 us
  other arithmetic: 38 us -> 2.1 us
  blocking collectives: 26.8 us -> 0 us
  between operations: 15.4 us -> 1.94 us
    pallas_call x2 -> x4, Pallas kernels: 200 us -> 417 us  [the longest x1 117 us: last(): pl.pallas_call(functools.partial(last_kernel, chips=chips, shards=shards)...]
    dot_general x32 -> x0, matrix products: 199 us -> none  [the longest x22 153 us: matmul(): return jnp.dot(left, right, preferred_element_type=jnp.float32)]
    all_gather x1 -> x0, waiting for transfers between devices: 42.8 us -> none  [on_device(): normed_all = lax.all_gather(normed_two, 'expert', axis=0)]
    psum x1 -> x0, blocking collectives: 26.8 us -> none  [on_device(): summed = [lax.psum(v.astype(BF16), 'expert').astype(F32) for v in pieces]]
    reshape x6 -> x0, local copies, waits for them, and re-layouts: 26.7 us -> none  [the longest x4 19 us: blocks_of_columns(): value.astype(BF16).reshape(value.shape[0], shards, width).transpose(1, 0, 2)]
    convert_element_type x12 -> x0, other arithmetic: 21.1 us -> none  [the longest x11 13.7 us: on_device(): summed = [lax.psum(v.astype(BF16), 'expert').astype(F32) for v in pieces]]
    convert_element_type x7 -> x0, local copies, waits for them, and re-layouts: 20.5 us -> none  [the longest x4 18.9 us: blocks_of_columns(): value.astype(BF16).reshape(value.shape[0], shards, width).transpose(1, 0, 2)]
    unnamed x158 -> x52, local copies, waits for them, and re-layouts: 25.1 us -> 23.6 us
  transfers between devices with their start and end apart: 5 -> 1, of which waited for: 1 -> 0; matrix products, arithmetic and copies ran while one was open for 32% -> 1% of each run, Pallas kernels for 29% -> 58%
where the time goes in v3:
time: 542 us; the launch traced here: 536 us
  Pallas kernels  499 us (92%)
  local copies, waits for them, and re-layouts  28.6 us (5%)
    pallas_call x1, Pallas kernels, last(): pl.pallas_call(functools.partial(last_kernel, chips=chips, shards=shards)...  117 us
    pallas_call x1, Pallas kernels, rear(): pl.pallas_call(functools.partial(rear_kernel, plane=plane, chips=chips, s...  115 us
    pallas_call x1, Pallas kernels, middle(): pl.pallas_call(functools.partial(middle_kernel, chips=chips, shards=shard...  104 us
    pallas_call x1, Pallas kernels, front(): pl.pallas_call(functools.partial(front_kernel, plane=plane, chips=chips),...  82.6 us
    pallas_call x1, Pallas kernels, weights(): pl.pallas_call(functools.partial(weights_kernel, plane=plane, chips=chips...  81.2 us
    unnamed x52, local copies, waits for them, and re-layouts  23.6 us
  transfers between devices with their start and end apart: 1, of which 0 were waited for; matrix products, arithmetic and copies ran while one was open for 1% of the time, Pallas kernels for 58%

profile of v3, /device:TPU:0, one launch (start us, length us, event | category | flops | bytes accessed | tf_op | source)
XLA Modules:
  0.0 535.5 jit_solution(10355354016044144445)
XLA Ops:
  0.6 0.0 copy-start.11
  0.7 0.0 copy-start.12
  0.7 0.0 copy-start.8
  0.7 1.0 fusion.2
  2.4 0.7 broadcast_in_dim.38
  3.0 0.7 broadcast_in_dim.39
  3.7 0.5 pad_maximum_fusion
  4.2 0.0 copy-start
  4.2 0.0 copy-start.1
  4.2 0.5 dynamic_update_slice.3.refs_9_
  4.7 82.6 %shard_map.246 = (bf16[8,512,768]{2,1,0:T(8,128)(2,1)}, f32[8,16,512]{2,1,0:T(8,128)S(1)}, bf16[512,768]{1,0:T(8,128)(2,1)S(1)}, bf16[512,2304]{1,0:T(8,128)(2,1...) custom-call(s32[1]{0:T(128)S(6)} %copy.43.refs_0_, ...), custom_call_target="tpu_custom_call" | custom-call | tf_op jit(solution)/shard_map/pallas_call | solution.py:404
  87.3 0.0 copy-done
  87.3 0.0 copy-done.1
  87.3 0.0 copy-start.2
  87.3 0.9 copy-done.2
  88.2 0.9 copy-done.3
  89.1 0.9 copy-done.5
  90.0 0.9 copy-done.6
  90.8 0.7 copy-done.7
  91.6 0.7 copy-done.9
  92.3 0.7 copy-done.10
  93.0 103.7 %shard_map.247 = (bf16[4,512,768]{2,1,0:T(8,128)(2,1)}, bf16[4,512,768]{2,1,0:T(8,128)(2,1)}, bf16[4,512,2048]{2,1,0:T(8,128)(2,1)}, bf16[4,512,2048]{2,1,0:T(8,...) custom-call(bf16[512,768]{1,0:T(8,128)(2,1)} %copy-done.2, ...), custom_call_target="tpu_custom_call" | custom-call | tf_op jit(solution)/shard_map/pallas_call | solution.py:742
  196.7 3.7 all-to-all-start
  200.4 81.2 %shard_map.248 = (f32[768,512]{1,0:T(8,128)}, f32[768,512]{1,0:T(8,128)}, bf16[4,512,768]{2,1,0:T(8,128)(2,1)}, f32[512,768]{1,0:T(8,128)}) custom-call(bf16[2048,768]{1,0:T(8,128)(2,1)} %bitcast.24, bf16[2048,768]{1,0:T(8,128)(2,1)} %bitcast.25, f32[512,768]{1,0:T(8,128)} %get-tuple-element.72.refs_2_, bf16[2048,2048]{1,0:T(8,128)(2,1)} %bitcast.20, ...), custom_call_target="tpu_custom_call" | custom-call | tf_op jit(solution)/shard_map/pallas_call | solution.py:969
  281.7 115.0 %shard_map.249 = (f32[512,768]{1,0:T(8,128)}, f32[512,768]{1,0:T(8,128)}, bf16[768,2304]{1,0:T(8,128)(2,1)}, bf16[4,256,768]{2,1,0:T(8,128)(2,1)}, bf16[4,96,512...) custom-call(s32[1]{0:T(128)S(6)} %copy.43.refs_0_, f32[512,768]{1,0:T(8,128)} %refs_1_.3, ...), custom_call_target="tpu_custom_call" | custom-call | tf_op jit(solution)/shard_map/pallas_call | solution.py:1154
  396.7 116.6 %shard_map.250 = (f32[512,768]{1,0:T(8,128)}, f32[192,2304]{1,0:T(8,128)}, f32[256,768]{1,0:T(8,128)}, f32[768,512]{1,0:T(8,128)}, f32[768,512]{1,0:T(8,128)}, /*index=5*/f32[512,768]{1,0:T(8,128)}, f32[512,768]{1,0:T(8,128)}) custom-call(f32[512,768]{1,0:T(8,128)} %get-tuple-element.62.refs_3_.refs_0_, f32[512,768]{1,0:T(8,128)} %get-tuple-element.92.refs_1_, ...), custom_call_target="tpu_custom_call" | custom-call | tf_op jit(solution)/shard_map/pallas_call | solution.py:1311
  513.3 0.7 slice.12
  514.0 0.6 fusion.3
  514.7 1.9 slice.14
  516.6 0.0 all-to-all-done
  516.6 0.6 select_reduce_fusion
  517.2 2.8 copy.44
  520.0 0.0 copy-done.16
  520.0 1.1 copy.45
  521.1 0.9 copy-done.13
  522.0 1.2 copy.46
  523.2 0.8 copy-done.20
  524.1 1.1 copy.47
  525.2 0.8 copy-done.19
  526.1 1.1 copy.48
  527.2 0.8 copy-done.18
  528.0 1.1 copy.49
  529.2 0.8 copy-done.15
  530.0 1.1 copy.50
  531.1 0.8 copy-done.14
  532.0 1.1 copy.51
  533.1 0.8 copy-done.17
  534.0 1.1 copy.52
  (23 shorter events, 0.1 us)
Async XLA Ops:
  0.6 4.0 copy-start.11
  0.7 4.0 copy-start.12
  0.7 4.0 copy-start.8
  0.7 4.0 copy-start.4
  4.2 83.1 %copy-start = (f32[512,128]{1,0:T(8,128)}, f32[512,128]{1,0:T(8,128)S(1)}, u32[]{:S(2)}) copy-start(f32[512,128]{1,0:T(8,128)S(1)} %get-tuple-element.116.refs_5_.refs_12_) | copy-start | bytes 786436
  4.2 83.1 %copy-start.1 = (f32[512,128]{1,0:T(8,128)}, f32[512,128]{1,0:T(8,128)S(1)}, u32[]{:S(2)}) copy-start(f32[512,128]{1,0:T(8,128)S(1)} %get-tuple-element.117.refs_6_.refs_13_) | copy-start | bytes 786436
  87.3 0.9 copy-start.2
  88.2 0.9 copy-start.3
  89.1 0.9 copy-start.5
  90.0 0.9 copy-start.6
  90.8 0.7 copy-start.7
  91.6 0.7 copy-start.9
  92.3 0.7 copy-start.10
  196.7 319.9 %all-to-all-start = ((f32[8,1,512]{2,1,0:T(1,128)}), f32[8,1,512]{2,1,0:T(1,128)S(1)}, u32[]{:S(2)}, u32[]{:S(2)}) async-start(f32[8,1,512]{2,1,0:T(1,128)} %get-tuple-element.110), calls=%async_computation | async-start | bytes 32768 | tf_op jit(solution)/shard_map/all_to_all | solution.py:1399
  517.2 2.8 copy-start.16
  520.0 2.0 copy-start.13
  522.0 2.0 copy-start.20
  524.1 2.0 copy-start.19
  526.0 2.0 copy-start.18
  528.0 2.0 copy-start.15
  530.0 2.0 copy-start.14
  532.0 2.0 copy-start.17

commit v4 on v3

--- a/solution.py
+++ b/solution.py
@@ -2,6 +2,7 @@
 
 import jax
 import jax.numpy as jnp
+import numpy as np
 from jax import lax
 from jax.experimental import pallas as pl
 from jax.experimental.pallas import tpu as pltpu
@@ -14,6 +15,7 @@
 MESH = pl.DeviceIdType.MESH
 F32 = jnp.float32
 BF16 = jnp.bfloat16
+VMEM_BYTES = 61 << 20
 
 
 def place():
@@ -51,61 +53,52 @@
 class PlaneGather:
     COPIES = 7
 
-    def __init__(self, src, dst, axis, send, recv, local, at):
-        self.src, self.dst, self.axis, self.at = src, dst, axis, at
+    def __init__(self, src, dst, send, recv, local, at):
+        self.src, self.dst, self.at = src, dst, at
         self.send, self.recv, self.local = send, recv, local
-        self.rows, self.cols = src.shape
+        self.rows = src.shape[0]
         self.copies = []
 
     def view(self, shard, start, count):
-        if self.axis == 0:
-            return self.dst.at[pl.ds(pl.multiple_of(shard * self.rows + start, 16), count), :]
-        return self.dst.at[
-            pl.ds(pl.multiple_of(start, 16), count),
-            pl.ds(pl.multiple_of(shard * self.cols, 128), self.cols),
-        ]
-
-    def copy(self, src, dst, index, device):
-        made = remote(src, dst, self.send.at[index], self.recv.at[index], device)
+        return self.dst.at[pl.ds(pl.multiple_of(shard * self.rows + start, 16), count), :]
+
+    def copy(self, part, index, device):
+        made = remote(part, part, self.send.at[index], self.recv.at[index], device)
         made.start()
         self.copies.append(made)
 
+    def load(self):
+        self.own = pltpu.make_async_copy(self.src, self.view(self.at["shard"], 0, self.rows), self.local)
+        self.own.start()
+
     def first(self):
         at, half = self.at, self.rows // 2
-        src = self.src.at[pl.ds(pl.multiple_of(at["core"] * half, 16), half), :]
-        dst = self.view(at["shard"], at["core"] * half, half)
-        self.copy(src, dst, 0, at["dev_x"])
-        self.copy(src, dst, 1, at["dev_y"])
-        self.own = pltpu.make_async_copy(self.src, self.view(at["shard"], 0, self.rows), self.local)
-        self.own.start()
+        self.own.wait()
+        part = self.view(at["shard"], at["core"] * half, half)
+        self.copy(part, 0, at["dev_x"])
+        self.copy(part, 1, at["dev_y"])
 
     def second(self):
         at, half, quarter = self.at, self.rows // 2, self.rows // 4
         start = at["core"] * half
         self.copies[0].wait_recv()
-        part = self.view(at["sx"], start, quarter)
-        self.copy(part, part, 2, at["dev_y"])
-        part = self.view(at["sx"], start, half)
-        self.copy(part, part, 3, at["dev_c"])
+        self.copy(self.view(at["sx"], start, quarter), 2, at["dev_y"])
+        self.copy(self.view(at["sx"], start, half), 3, at["dev_c"])
         self.copies[1].wait_recv()
-        part = self.view(at["sy"], start + quarter, quarter)
-        self.copy(part, part, 4, at["dev_x"])
-        part = self.view(at["sy"], start, half)
-        self.copy(part, part, 5, at["dev_c"])
+        self.copy(self.view(at["sy"], start + quarter, quarter), 4, at["dev_x"])
+        self.copy(self.view(at["sy"], start, half), 5, at["dev_c"])
 
     def third(self):
         at, half = self.at, self.rows // 2
         self.copies[2].wait_recv()
         self.copies[4].wait_recv()
-        part = self.view(at["sd"], at["core"] * half, half)
-        self.copy(part, part, 6, at["dev_c"])
+        self.copy(self.view(at["sd"], at["core"] * half, half), 6, at["dev_c"])
 
     def finish(self):
         for index in (3, 5, 6):
             self.copies[index].wait_recv()
         for made in self.copies:
             made.wait_send()
-        self.own.wait()
 
 
 class ChainGather:
@@ -221,10 +214,13 @@
 
 def rope_lanes(length):
     half = HEAD_DIM // 2
-    frequency = 10000.0 ** (-jnp.arange(half, dtype=F32) * 2.0 / HEAD_DIM)
-    angles = jnp.arange(length, dtype=F32)[:, None] * frequency[None, :]
-    cosine, sine = jnp.cos(angles), jnp.sin(angles)
-    return jnp.concatenate([cosine] * 4, axis=1), jnp.concatenate([-sine, sine] * 2, axis=1)
+    frequency = 10000.0 ** (-np.arange(half) * 2.0 / HEAD_DIM)
+    angles = np.arange(length)[:, None] * frequency[None, :]
+    cosine, sine = np.cos(angles), np.sin(angles)
+    return (
+        jnp.asarray(np.concatenate([cosine] * 4, axis=1), F32),
+        jnp.asarray(np.concatenate([-sine, sine] * 2, axis=1), F32),
+    )
 
 
 def partner(values):
@@ -235,28 +231,45 @@
     return jnp.where(lane % HEAD_DIM < half, ahead, behind)
 
 
+def set_bias(bias_ref, prefix):
+    shape = bias_ref.shape
+    row = lax.broadcasted_iota(jnp.int32, shape, 0)
+    col = lax.broadcasted_iota(jnp.int32, shape, 1)
+    bias_ref[...] = jnp.where((col < prefix[0]) | (col <= row), 0.0, -1e30)
+
+
+def two_heads(values):
+    low = lax.broadcasted_iota(jnp.int32, values.shape, 1) < HEAD_DIM
+    zero = jnp.zeros_like(values)
+    return jnp.concatenate([jnp.where(low, values, zero), jnp.where(low, zero, values)], axis=0)
+
+
 def front_kernel(*refs, plane, chips):
     (prefix, x_ref, cot_ref, route_ref, weight_ref, cos_ref, sin_ref), refs = refs[:7], refs[7:]
-    if plane:
-        (qkv_part, out_part, gains_part, sg, su, sd), refs = refs[:6], refs[6:]
-    else:
-        (qkv_full, out_full, gains_full), refs = refs[:3], refs[3:]
-    (cot_all, table_all, h1_ref, rot_ref, att_ref, lse_ref, resid_ref, h2_ref, cot_low), refs = refs[:9], refs[9:]
-    if plane:
-        (qkv_full, out_full, gains_full, sg_full, su_full, sd_full), refs = refs[:6], refs[6:]
-    bias_ref, table_ref, chain_send, chain_recv, chain_local = refs[:5]
+    (one_ref, two_ref), refs = refs[:2], refs[2:]
+    weights, refs = (refs[:5], refs[5:]) if plane else (refs[:2], refs[2:])
+    (cot_out, table_out, h1_ref, rot_ref, att_ref, lse_ref, resid_ref, h2_ref, cot_low, gains_ref), refs = refs[:10], refs[10:]
+    full_out, refs = (refs[:5], refs[5:]) if plane else ([], refs)
+    (bias_ref, table_ref, table_all, cot_all, out_sem, chain_send, chain_recv, chain_local), refs = refs[:8], refs[8:]
     length, width = x_ref.shape
     experts = table_ref.shape[0] // 2
     at = place()
+    if plane:
+        gains_src, gains_full, full, (send, recv, local, full_sem) = refs[0], refs[1], refs[2:7], refs[7:]
+        gathers = [
+            PlaneGather(a, b, send.at[k], recv.at[k], local.at[k], at)
+            for k, (a, b) in enumerate(zip([*weights, gains_src], [*full, gains_full]))
+        ]
+        first, later = [gathers[5], gathers[1], gathers[0]], gathers[2:5]
+        gains_src[:32, :] = jnp.broadcast_to(one_ref[...], (32, one_ref.shape[1]))
+        gains_src[32:, :] = jnp.broadcast_to(two_ref[...], (32, two_ref.shape[1]))
+        for gather in first + later:
+            gather.load()
+        qkv_full, out_full = full[:2]
+    else:
+        qkv_full, out_full = weights
     chain_meet(at, chips, [at["dev_x"], at["dev_y"], at["dev_c"]] if plane else [at["dev_c"]])
     if plane:
-        send, recv, local = refs[5:8]
-        parts = [(qkv_part, qkv_full), (out_part, out_full), (gains_part, gains_full)]
-        shared = [(sg, sg_full), (su, su_full), (sd, sd_full)]
-        gathers = [
-            PlaneGather(a, b, 0, send.at[k], recv.at[k], local.at[k], at) for k, (a, b) in enumerate(parts + shared)
-        ]
-        first, later = gathers[2::-1], gathers[3:]
         for gather in first:
             gather.first()
     cot_low[...] = cot_ref[...].astype(BF16)
@@ -278,21 +291,26 @@
     ]
     for chain in chains:
         chain.start()
-    row = lax.broadcasted_iota(jnp.int32, (length, length), 0)
-    col = lax.broadcasted_iota(jnp.int32, (length, length), 1)
-    bias_ref[...] = jnp.where((col < prefix[0]) | (col <= row), 0.0, -1e30)
+    set_bias(bias_ref, prefix)
     if plane:
         for step in ("second", "third", "finish"):
             for gather in first:
                 getattr(gather, step)()
         for gather in later:
             gather.first()
-    blocks = gains_full.shape[0] // 64
-    gain_one = sum(gains_full[pl.ds(64 * k, 1), :].astype(F32) for k in range(blocks))
-    gain_two = sum(gains_full[pl.ds(64 * k + 32, 1), :].astype(F32) for k in range(blocks))
+        outs = [pltpu.make_async_copy(a, b, full_sem.at[k]) for k, (a, b) in enumerate(zip(full, full_out))]
+        for made in outs[:2]:
+            made.start()
+        blocks = range(gains_full.shape[0] // 64)
+        for k in range(2):
+            row = [gains_full[pl.ds(64 * n + 32 * k, 1), :].astype(F32) for n in blocks]
+            gains_ref[pl.ds(k, 1), :] = jnp.concatenate(row, axis=1)
+    else:
+        gains_ref[pl.ds(0, 1), :] = one_ref[...].astype(F32)
+        gains_ref[pl.ds(1, 1), :] = two_ref[...].astype(F32)
     x = x_ref[...]
     inverse = lax.rsqrt(jnp.mean(x * x, axis=-1, keepdims=True) + EPS)
-    h1_ref[...] = (x * inverse * gain_one).astype(BF16)
+    h1_ref[...] = (x * inverse * gains_ref[pl.ds(0, 1), :]).astype(BF16)
 
     def project(block, turned):
         cols = columns(block * 256, 256)
@@ -308,72 +326,82 @@
     for chain in chains:
         chain.step(1)
     lse_ref[...] = jnp.zeros_like(lse_ref)
-    rows_at_once = min(256, length)
+    count = length // 2
 
     def pair(j):
         queries, keys, values = (
             rot_ref[:, columns(part * width + j * 128, 128)] for part in range(3)
         )
-        low_lanes = lax.broadcasted_iota(jnp.int32, (rows_at_once, 128), 1) < HEAD_DIM
-        for start in range(0, length, rows_at_once):
-            rows = pl.ds(start, rows_at_once)
-            outs = []
-            for head in range(2):
-                mine = low_lanes if head == 0 else ~low_lanes
-                query = jnp.where(mine, queries[start : start + rows_at_once], 0.0) * HEAD_DIM**-0.5
-                scores = dot_nt(query.astype(BF16), keys) + bias_ref[rows, :]
-                peak = jnp.max(scores, axis=-1, keepdims=True)
-                exponent = jnp.exp(scores - peak)
-                total = jnp.sum(exponent, axis=-1, keepdims=True)
-                outs.append(dot_nn((exponent / total).astype(BF16), values))
-                lanes = lax.broadcasted_iota(jnp.int32, (rows_at_once, 128), 1)
-                lse_ref[rows, :] = jnp.where(lanes == 2 * j + head, peak + jnp.log(total), lse_ref[rows, :])
-            att_ref[rows, columns(j * 128, 128)] = jnp.where(low_lanes, *outs).astype(BF16)
+        low = lax.broadcasted_iota(jnp.int32, (count, 128), 1) < HEAD_DIM
+        lanes = lax.broadcasted_iota(jnp.int32, (count, 128), 1)
+        for start in range(0, length, count):
+            rows, seen = pl.ds(start, count), start + count
+            scores = dot_nt(two_heads(queries[start:seen] * HEAD_DIM**-0.5), keys[:seen])
+            bias = bias_ref[rows, :seen]
+            scores = jnp.concatenate([scores[:count] + bias, scores[count:] + bias], axis=0)
+            peak = jnp.max(scores, axis=-1, keepdims=True)
+            exponent = jnp.exp(scores - peak)
+            total = jnp.sum(exponent, axis=-1, keepdims=True)
+            out = dot_nn(exponent.astype(BF16), values[:seen]) * (1.0 / total)
+            att_ref[rows, columns(j * 128, 128)] = jnp.where(low, out[:count], out[count:]).astype(BF16)
+            logsum = peak + jnp.log(total)
+            lse_ref[rows, :] = jnp.where(
+                lanes == 2 * j,
+                logsum[:count],
+                jnp.where(lanes == 2 * j + 1, logsum[count:], lse_ref[rows, :]),
+            )
 
     pairs = width // 128
     pl.loop(0, pairs // 2)(pair)
     for step in range(2, chips - 1):
         for chain in chains:
             chain.step(step)
+    pl.loop(pairs // 2, pairs)(pair)
     if plane:
         for gather in later:
             gather.second()
-    pl.loop(pairs // 2, pairs)(pair)
     resid = x_ref[...] + dot_nn(att_ref[...], out_full[...])
     resid_ref[...] = resid
     inverse = lax.rsqrt(jnp.mean(resid * resid, axis=-1, keepdims=True) + EPS)
-    h2_ref[...] = (resid * inverse * gain_two).astype(BF16)
+    h2_ref[...] = (resid * inverse * gains_ref[pl.ds(1, 1), :]).astype(BF16)
     for chain in chains:
         chain.step(chips - 1)
     if plane:
         for step in ("third", "finish"):
             for gather in later:
                 getattr(gather, step)()
+        for made in outs[2:]:
+            made.start()
     for chain in chains:
         for step in range(chips):
             chain.finish(step)
+    keep = [
+        pltpu.make_async_copy(a, b, out_sem.at[k])
+        for k, (a, b) in enumerate([(table_all, table_out), (cot_all, cot_out)])
+    ]
+    for made in keep:
+        made.start()
+    for chain in chains:
         chain.sent()
-
-
-def front(prefix, inputs, cotangent, route_rows, weight_rows, qkv_weight, out_weight, gains, shared, ident):
+    for made in keep + (outs if plane else []):
+        made.wait()
+
+
+def front(prefix, inputs, cotangent, route_rows, weight_rows, gains, weights, ident):
     length, width = inputs.shape
-    group = lax.axis_size("expert")
-    chips, plane = group // 2, lax.axis_size("shard") == 4
-    shards = lax.axis_size("shard")
+    group, shards = lax.axis_size("expert"), lax.axis_size("shard")
+    chips, plane = group // 2, shards == 4
     cosine, sine = rope_lanes(length)
-    operands = [prefix, inputs, cotangent, route_rows, weight_rows, cosine, sine]
     vmem, anywhere = pl.BlockSpec(memory_space=pltpu.VMEM), pl.BlockSpec(memory_space=pl.ANY)
-    in_specs = [pl.BlockSpec(memory_space=pltpu.SMEM)] + [vmem] * 6
-    weights = [qkv_weight, out_weight, gains]
-    if plane:
-        operands += weights + shared
-        in_specs += [anywhere] * 6
-    else:
+    gains = [v[None, :] for v in gains]
+    if not plane:
+        gains = [lax.all_gather(v, "shard", axis=1, tiled=True) for v in gains]
         weights = [lax.all_gather(v, "shard", axis=0, tiled=True) for v in weights]
-        shared = [lax.all_gather(v, "shard", axis=0, tiled=True) for v in shared]
-        operands += weights
-        in_specs += [vmem] * 3
-    shape = jax.ShapeDtypeStruct
+    operands = [prefix, inputs, cotangent, route_rows, weight_rows, cosine, sine, *gains]
+    in_specs = [pl.BlockSpec(memory_space=pltpu.SMEM)] + [vmem] * 8
+    operands += weights if plane else weights[:2]
+    in_specs += [anywhere] * 5 if plane else [vmem] * 2
+    shape, dma = jax.ShapeDtypeStruct, pltpu.SemaphoreType.DMA
     out_shape = [
         shape((group, length, width), BF16),
         shape((group, 2 * group, length), F32),
@@ -384,23 +412,27 @@
         shape((length, width), F32),
         shape((length, width), BF16),
         shape((length, width), BF16),
+        shape((8, width), F32),
     ]
-    out_specs = [anywhere] * 2 + [vmem] * 7
+    out_specs = [anywhere] * 2 + [vmem] * 8
     scratch = [
         pltpu.VMEM((length, length), F32),
         pltpu.VMEM((2 * group, length), F32),
-        pltpu.SemaphoreType.DMA((2, ChainGather.copies(chips))),
-        pltpu.SemaphoreType.DMA((2, ChainGather.copies(chips))),
-        pltpu.SemaphoreType.DMA((2,)),
+        pltpu.VMEM((group, 2 * group, length), F32),
+        pltpu.VMEM((group, length, width), BF16),
+        dma((2,)),
+        dma((2, ChainGather.copies(chips))),
+        dma((2, ChainGather.copies(chips))),
+        dma((2,)),
     ]
     if plane:
-        out_shape += [shape((shards * v.shape[0], v.shape[1]), BF16) for v in weights + shared]
-        out_specs += [vmem] * 3 + [anywhere] * 3
-        scratch += [
-            pltpu.SemaphoreType.DMA((6, PlaneGather.COPIES)),
-            pltpu.SemaphoreType.DMA((6, PlaneGather.COPIES)),
-            pltpu.SemaphoreType.DMA((6,)),
-        ]
+        full = [(shards * v.shape[0], v.shape[1]) for v in weights]
+        out_shape += [shape(s, BF16) for s in full]
+        out_specs += [anywhere] * 5
+        part = gains[0].shape[1]
+        scratch += [pltpu.VMEM((64, part), BF16), pltpu.VMEM((64 * shards, part), BF16)]
+        scratch += [pltpu.VMEM(s, BF16) for s in full]
+        scratch += [dma((6, PlaneGather.COPIES)), dma((6, PlaneGather.COPIES)), dma((6,)), dma((5,))]
     outs = pl.pallas_call(
         functools.partial(front_kernel, plane=plane, chips=chips),
         out_shape=out_shape,
@@ -408,12 +440,10 @@
         out_specs=out_specs,
         scratch_shapes=scratch,
         compiler_params=pltpu.CompilerParams(
-            collective_id=ident, has_side_effects=True, vmem_limit_bytes=48 << 20
+            collective_id=ident, has_side_effects=True, vmem_limit_bytes=VMEM_BYTES
         ),
     )(*operands)
-    if not plane:
-        outs = list(outs) + weights + shared
-    return outs
+    return outs if plane else [*outs, *weights]
 
 
 def near_order(chips):
@@ -604,23 +634,21 @@
     sy_ref[...] = jnp.zeros_like(sy_ref)
     dh_ref[...] = jnp.zeros_like(dh_ref)
 
-    def shared_copies(k, arrival=False):
-        copies = []
+    def shared_copies(k):
+        stay, over = [], []
         for n, held in enumerate((sgg_s, sug_s, sdg_s)):
             half = held.shape[0] // 2
-            mine, other = (pl.ds(pl.multiple_of(c * half, 16), half) for c in (core, 1 - core))
-            over = remote(held.at[other, :], sgot[n].at[k], sg_send.at[n], sg_recv.at[n, k], at["dev_c"])
-            if arrival:
-                copies.append(over)
-            else:
-                copies += [pltpu.make_async_copy(held.at[mine, :], sown[n].at[k], sg_sem.at[n]), over]
-        return copies
+            mine, other = (held.at[pl.ds(pl.multiple_of(c * half, 16), half), :] for c in (core, 1 - core))
+            stay.append((mine, sown[n].at[k], sg_sem.at[n]))
+            over.append((other, sgot[n].at[k], sg_send.at[n], sg_recv.at[n, k], at["dev_c"]))
+        return stay, over
 
     def shared_settle(k):
-        for copy in shared_copies(k)[::2]:
-            copy.wait()
-        for copy in shared_copies(k, True):
-            copy.wait_send()
+        stay, over = shared_copies(k)
+        for copy in stay:
+            pltpu.make_async_copy(*copy).wait()
+        for copy in over:
+            remote(*copy).wait_send()
 
     def shared_block(k):
         slot = k % 2
@@ -641,8 +669,11 @@
         sgg_s[...] = dot_tn(h2_ref[...], gate_grad).astype(BF16)
         sug_s[...] = dot_tn(h2_ref[...], up_grad).astype(BF16)
         sdg_s[...] = dot_tn(hidden, cot_ref[...]).astype(BF16)
-        for copy in shared_copies(k):
-            copy.start()
+        stay, over = shared_copies(k)
+        for copy in stay:
+            pltpu.make_async_copy(*copy).start()
+        for copy in over:
+            remote(*copy).start()
 
     chain.finish(0)
     expert_rows(0)
@@ -659,8 +690,8 @@
 
     @pl.loop(0, shards)
     def _(k):
-        for copy in shared_copies(k, True):
-            copy.wait_recv()
+        for copy in shared_copies(k)[1]:
+            remote(*copy).wait_recv()
 
     for copy in total_copies(chips - 1):
         copy.wait()
@@ -746,7 +777,7 @@
         out_specs=[anywhere] * 13 + [vmem] * 3,
         scratch_shapes=scratch,
         compiler_params=pltpu.CompilerParams(
-            collective_id=ident, has_side_effects=True, vmem_limit_bytes=60 << 20
+            collective_id=ident, has_side_effects=True, vmem_limit_bytes=VMEM_BYTES
         ),
     )(h2, cot_low, table_all, cot_all, *expert_weights, *shared_full)
 
@@ -771,12 +802,13 @@
             self.at["dev_right" if right else "dev_left"],
         )
 
-    def move(self, step):
+    def tick(self, step):
         z, chips = self.at["z"], self.chips
-        far = chips - step
-
-        @pl.when(z < far)
+
+        @pl.when(step >= z)
         def _():
+            far = chips - 1 - step + z
+
             @pl.when(z > 0)
             def _():
                 self.copy(far, True).wait_recv()
@@ -784,10 +816,10 @@
 
             self.copy(far, True).start()
 
-        near = step - 1
-
-        @pl.when(z > near)
+        @pl.when(step >= chips - 1 - z)
         def _():
+            near = step - (chips - 1 - z)
+
             @pl.when(z < chips - 1)
             def _():
                 self.copy(near, False).wait_recv()
@@ -795,19 +827,13 @@
 
             self.copy(near, False).start()
 
-    def result(self, dst):
+    def value(self):
         z, chips = self.at["z"], self.chips
-        dst[...] += self.own[z].astype(F32)
-
-        @pl.when(z > 0)
-        def _():
-            self.copy(z, True).wait_recv()
-            dst[...] += self.from_left[z].astype(F32)
-
-        @pl.when(z < chips - 1)
-        def _():
-            self.copy(z, False).wait_recv()
-            dst[...] += self.from_right[z].astype(F32)
+        pl.when(z > 0)(lambda: self.copy(z, True).wait_recv())
+        pl.when(z < chips - 1)(lambda: self.copy(z, False).wait_recv())
+        total = self.own[z].astype(F32)
+        total += jnp.where(z > 0, self.from_left[z].astype(F32), 0.0)
+        return total + jnp.where(z < chips - 1, self.from_right[z].astype(F32), 0.0)
 
     def sent(self):
         for step in range(1, self.chips):
@@ -881,18 +907,19 @@
 
 
 def weights_kernel(*refs, plane, chips, shards):
-    (rows_ref, grad_ref, dh_ref, hid_hbm, da_hbm, db_hbm, back_hbm), refs = refs[:7], refs[7:]
-    (gate_out, up_out, down_out, sum_ref), refs = refs[:4], refs[4:]
-    (chunk, own, from_left, from_right), refs = refs[:4], refs[4:]
-    own_sem, chunk_sem, chain_send, chain_recv = refs[:4]
+    (rows_ref, grad_ref, dh_ref, dots_ref, route_ref, hid_hbm, da_hbm, db_hbm, back_hbm), refs = refs[:9], refs[9:]
+    (gate_out, up_out, down_out, sum_ref, chosen_ref), refs = refs[:5], refs[5:]
+    (chunk, own, from_left, from_right, dots_got), refs = refs[:5], refs[5:]
+    (own_sem, chunk_sem, dots_send, dots_recv, chain_send, chain_recv), refs = refs[:6], refs[6:]
     block = chunk.shape[-1]
     at = place()
-    chain_meet(at, chips, [at["dev_x"], at["dev_y"]] if plane else [])
+    me, group = at["expert"], 2 * chips
     load = pltpu.make_async_copy(back_hbm, own, own_sem)
     load.start()
+    peers = [(lax.rem(me + k, group), at["shard"]) for k in range(1, group)]
+    meet(peers + ([at["dev_x"], at["dev_y"]] if plane else []))
     if plane:
-        send, recv = refs[4:6]
-        work = refs[6:]
+        send, recv, *work = refs
         reduces = [
             PlaneReduce(work[4 * k], *work[4 * k + 1 : 4 * k + 4], send.at[k], recv.at[k], at) for k in range(2)
         ]
@@ -900,6 +927,10 @@
     else:
         targets = [gate_out, up_out, down_out]
     sources = [da_hbm, db_hbm, hid_hbm]
+    dots = [
+        remote(dots_ref.at[peer[0]], dots_got.at[me], dots_send.at[k], dots_recv.at[k], peer)
+        for k, peer in enumerate(peers)
+    ]
 
     def fetch(array, index):
         shard = plane_blocks(at, index, plane)
@@ -908,8 +939,8 @@
             sources[array].at[:, columns(shard * block, block)], chunk.at[slot], chunk_sem.at[slot]
         )
 
-    def make(array):
-        @pl.loop(0, shards)
+    def make(array, low, high):
+        @pl.loop(low, high)
         def _(index):
             fetch(array, index).wait()
             pl.when(index + 1 < shards)(lambda: fetch(array, index + 1).start())
@@ -925,30 +956,43 @@
     fetch(0, 0).start()
     chain = ChainReduce(own, from_left, from_right, chain_send, chain_recv, at, chips)
     load.wait()
-    chain.move(1)
-    for array in range(3):
-        make(array)
-        if plane and array < 2:
-            reduces[array].first()
-        if array == 1:
-            for step in range(2, chips - 1):
-                chain.move(step)
+    chain.tick(0)
+    for made in dots:
+        made.start()
+    dots_got[me] = dots_ref[me]
+    make(0, 0, shards)
+    if plane:
+        reduces[0].first()
+    make(1, 0, shards // 2)
+    for step in range(1, chips - 2):
+        chain.tick(step)
+    make(1, shards // 2, shards)
+    if plane:
+        reduces[1].first()
+    make(2, 0, shards)
     if plane:
         reduces[0].second()
-    chain.move(chips - 1)
+    chain.tick(chips - 2)
+    for made in dots:
+        made.wait()
+    for k in range(TOP):
+        chosen_ref[pl.ds(k, 1), :] = sum(
+            jnp.where(route_ref[pl.ds(k, 1), :] == e, dots_got[e], 0.0) for e in range(group)
+        )
     if plane:
         reduces[1].second()
-    sum_ref[...] = dh_ref[...]
-    chain.result(sum_ref)
+        for turn in range(2):
+            gate_out[pl.ds(turn * reduces[0].half, reduces[0].half), :] = reduces[0].value(turn)
+    sum_ref[...] = dh_ref[...] + chain.value()
     chain.sent()
     if plane:
-        for reduce, out in zip(reduces, (gate_out, up_out)):
-            for turn in range(2):
-                out[pl.ds(turn * reduce.half, reduce.half), :] = reduce.value(turn)
+        for turn in range(2):
+            up_out[pl.ds(turn * reduces[1].half, reduces[1].half), :] = reduces[1].value(turn)
+        for reduce in reduces:
             reduce.sent()
 
 
-def weights(rows, grad_rows, shared_back, hidden, gate_grad, up_grad, back_part, ident):
+def weights(rows, grad_rows, shared_back, dots, route_rows, hidden, gate_grad, up_grad, back_part, ident):
     chips, length, width = back_part.shape
     shards = lax.axis_size("shard")
     plane = shards == 4
@@ -958,24 +1002,25 @@
     shape, dma = jax.ShapeDtypeStruct, pltpu.SemaphoreType.DMA
     wide = (shards, width, block)
     scratch = [pltpu.VMEM((2, count, block), BF16)] + ChainReduce.scratch((chips, length, width))
-    scratch += [dma, dma((2,)), dma((2 * chips,)), dma((2 * chips,))]
+    scratch += [pltpu.VMEM(dots.shape, F32)]
+    scratch += [dma, dma((2,)), dma((2 * chips - 1,)), dma((2 * chips - 1,)), dma((2 * chips,)), dma((2 * chips,))]
     if plane:
         out_shape = [shape((width, block), F32)] * 2
         scratch += [dma((2, PlaneReduce.COPIES))] * 2
         scratch += ([pltpu.VMEM(wide, BF16)] + PlaneReduce.scratch(wide)) * 2
     else:
         out_shape = [shape(wide, BF16)] * 2
-    out_shape += [shape((shards, block, width), BF16), shape((length, width), F32)]
+    out_shape += [shape((shards, block, width), BF16), shape((length, width), F32), shape((TOP, length), F32)]
     return pl.pallas_call(
         functools.partial(weights_kernel, plane=plane, chips=chips, shards=shards),
         out_shape=out_shape,
-        in_specs=[vmem] * 3 + [anywhere] * 4,
-        out_specs=[vmem] * 4,
+        in_specs=[vmem] * 5 + [anywhere] * 4,
+        out_specs=[vmem] * 5,
         scratch_shapes=scratch,
         compiler_params=pltpu.CompilerParams(
-            collective_id=ident, has_side_effects=True, vmem_limit_bytes=60 << 20
+            collective_id=ident, has_side_effects=True, vmem_limit_bytes=VMEM_BYTES
         ),
-    )(rows, grad_rows, shared_back, hidden, gate_grad, up_grad, back_part)
+    )(rows, grad_rows, shared_back, dots, route_rows, hidden, gate_grad, up_grad, back_part)
 
 
 def norm_back(source, inverse, gain, grad_in):
@@ -990,143 +1035,139 @@
 def rear_kernel(*refs, plane, chips, shards):
     (prefix, x_ref, cot_ref, resid_ref, dh_ref, gains_ref, rot_ref, att_ref, h1_ref, lse_ref), refs = refs[:10], refs[10:]
     (qkv_ref, out_ref, cos_ref, sin_ref, mix_hbm), refs = refs[:5], refs[5:]
-    if plane:
-        halves, refs = refs[:6], refs[6:]
+    halves, refs = (refs[:6], refs[6:]) if plane else ([], refs)
     (mix_out, input_grad_ref, qkv_grad_ref, out_grad_ref), refs = refs[:4], refs[4:]
-    if plane:
-        pieces, refs = refs[:3], refs[3:]
+    pieces, refs = (refs[:3], refs[3:]) if plane else ([], refs)
     (bias_ref, dres_ref, datt_ref, dqkv_ref, own, from_left, from_right), refs = refs[:7], refs[7:]
-    own_sem, chain_send, chain_recv = refs[:3]
+    (own_sem, chain_send, chain_recv), refs = refs[:3], refs[3:]
     length, width = x_ref.shape
     at = place()
-    chain_meet(at, chips, [at["dev_x"], at["dev_y"]] if plane else [])
     load = pltpu.make_async_copy(mix_hbm, own, own_sem)
     load.start()
+    reduces = []
     if plane:
-        send, recv, half_sem = refs[3:6]
-        work = [refs[6 + 5 * k : 11 + 5 * k] for k in range(3)]
+        send, recv, half_sem = refs[:3]
+        work = [refs[3 + 5 * k : 8 + 5 * k] for k in range(3)]
         loads = [
-            [
-                pltpu.make_async_copy(halves[2 * k + n], work[k][n], half_sem.at[k, n])
-                for n in range(2)
-            ]
+            [pltpu.make_async_copy(halves[2 * k + n], work[k][n], half_sem.at[k, n]) for n in range(2)]
             for k in range(3)
         ]
         for two in loads:
             for made in two:
                 made.start()
         reduces = [PlaneReduce(work[k][0], *work[k][2:], send.at[k], recv.at[k], at) for k in range(3)]
+    chain_meet(at, chips, [at["dev_x"], at["dev_y"]] if plane else [])
     chain = ChainReduce(own, from_left, from_right, chain_send, chain_recv, at, chips)
     load.wait()
-    chain.move(1)
-    if plane:
-        for k in range(3):
-            for made in loads[k]:
-                made.wait()
-
-            @pl.loop(0, shards)
-            def _(shard):
-                work[k][0][shard] = (
-                    work[k][0][shard].astype(F32) + work[k][1][shard].astype(F32)
-                ).astype(BF16)
-
-            reduces[k].first()
-    blocks = gains_ref.shape[0] // 64
-    gain_one = sum(gains_ref[pl.ds(64 * k, 1), :].astype(F32) for k in range(blocks))
-    gain_two = sum(gains_ref[pl.ds(64 * k + 32, 1), :].astype(F32) for k in range(blocks))
+    chain.tick(0)
+    for k, reduce in enumerate(reduces):
+        for made in loads[k]:
+            made.wait()
+
+        @pl.loop(0, shards)
+        def _(shard):
+            work[k][0][shard] = (
+                work[k][0][shard].astype(F32) + work[k][1][shard].astype(F32)
+            ).astype(BF16)
+
+        reduce.first()
     resid = resid_ref[...]
     inverse = lax.rsqrt(jnp.mean(resid * resid, axis=-1, keepdims=True) + EPS)
-    gain_two_grad, extra = norm_back(resid, inverse, gain_two, dh_ref[...])
+    gain_two_grad, extra = norm_back(resid, inverse, gains_ref[pl.ds(1, 1), :], dh_ref[...])
     dres = cot_ref[...] + extra
     dres_ref[...] = dres
-    low = dres.astype(BF16)
-    datt_ref[...] = dot_nt(low, out_ref[...]).astype(BF16)
-    out_grad = dot_tn(att_ref[...], low).astype(BF16)
+    low_dres = dres.astype(BF16)
+    datt_ref[...] = dot_nt(low_dres, out_ref[...]).astype(BF16)
+    out_grad = dot_tn(att_ref[...], low_dres).astype(BF16)
     rows = width // shards
     for k in range(shards):
         out_grad_ref[k, :rows, :] = out_grad[k * rows : (k + 1) * rows]
-    row = lax.broadcasted_iota(jnp.int32, (length, length), 0)
-    col = lax.broadcasted_iota(jnp.int32, (length, length), 1)
-    bias_ref[...] = jnp.where((col < prefix[0]) | (col <= row), 0.0, -1e30)
+    set_bias(bias_ref, prefix)
     scale = HEAD_DIM**-0.5
+    count = length // 2
 
     def pair(j):
-        cols = columns(j * 128, 128)
         queries, keys, values = (
             rot_ref[:, columns(part * width + j * 128, 128)] for part in range(3)
         )
-        grads = datt_ref[:, cols]
-        low_lanes = lax.broadcasted_iota(jnp.int32, (length, 128), 1) < HEAD_DIM
-        lanes = lax.broadcasted_iota(jnp.int32, (length, 128), 1)
-        parts = []
-        for head in range(2):
-            mine = low_lanes if head == 0 else ~low_lanes
-            query = jnp.where(mine, queries, 0.0) * scale
-            grad = jnp.where(mine, grads, 0.0).astype(BF16)
-            logsum = jnp.sum(jnp.where(lanes == 2 * j + head, lse_ref[...], 0.0), axis=1, keepdims=True)
-            probs = jnp.exp(dot_nt(query.astype(BF16), keys) + bias_ref[...] - logsum)
-            probs_grad = dot_nt(grad, values)
+        grads = datt_ref[:, columns(j * 128, 128)]
+        low = lax.broadcasted_iota(jnp.int32, (count, 128), 1) < HEAD_DIM
+        lanes = lax.broadcasted_iota(jnp.int32, (count, 128), 1)
+
+        def keep(part, rows, value):
+            if part < 2:
+                value = value * cos_ref[rows, :] - partner(value) * sin_ref[rows, :]
+            dqkv_ref[rows, columns(part * width + j * 128, 128)] = value.astype(BF16)
+
+        sums = []
+        for start in range(0, length, count):
+            rows, seen = pl.ds(start, count), start + count
+            query = two_heads(queries[start:seen] * scale)
+            grad = two_heads(grads[start:seen])
+            bias, lse = bias_ref[rows, :seen], lse_ref[rows, :]
+            logsum = jnp.concatenate(
+                [
+                    jnp.sum(jnp.where(lanes == 2 * j + head, lse, 0.0), axis=1, keepdims=True)
+                    for head in range(2)
+                ],
+                axis=0,
+            )
+            scores = dot_nt(query, keys[:seen])
+            scores = jnp.concatenate([scores[:count] + bias, scores[count:] + bias], axis=0)
+            probs = jnp.exp(scores - logsum)
+            probs_grad = dot_nt(grad, values[:seen])
             inner = jnp.sum(probs * probs_grad, axis=-1, keepdims=True)
             score_grad = (probs * (probs_grad - inner)).astype(BF16)
-            parts.append(
-                (
-                    dot_nn(score_grad, keys) * scale,
-                    dot_tn(score_grad, queries) * scale,
-                    dot_tn(probs.astype(BF16), grads),
-                )
-            )
-        for part in range(3):
-            both = jnp.where(low_lanes, parts[0][part], parts[1][part])
-            if part < 2:
-                both = both * cos_ref[...] - partner(both) * sin_ref[...]
-            dqkv_ref[:, columns(part * width + j * 128, 128)] = both.astype(BF16)
+            query_grad = dot_nn(score_grad, keys[:seen]) * scale
+            keep(0, rows, jnp.where(low, query_grad[:count], query_grad[count:]))
+            sums.append((dot_tn(score_grad, query), dot_tn(probs.astype(BF16), grad)))
+        for part in range(2):
+            keep(1 + part, pl.ds(0, count), sums[0][part] + sums[1][part][:count])
+            keep(1 + part, pl.ds(count, count), sums[1][part][count:])
 
     pairs = width // 128
     pl.loop(0, pairs // 2)(pair)
-    for step in range(2, chips - 1):
-        chain.move(step)
-    if plane:
-        reduces[0].second()
+    for step in range(1, chips - 2):
+        chain.tick(step)
     pl.loop(pairs // 2, pairs)(pair)
-    chain.move(chips - 1)
-    if plane:
-        reduces[1].second()
-        reduces[2].second()
+    for reduce in reduces[:2]:
+        reduce.second()
+    chain.tick(chips - 2)
 
     @pl.loop(0, 3 * width // 256)
     def _(k):
         cols = columns(k * 256, 256)
         qkv_grad_ref[:, cols] = dot_tn(h1_ref[...], dqkv_ref[:, cols]).astype(BF16)
 
+    for reduce in reduces[2:]:
+        reduce.second()
     dh1 = dot_nt(dqkv_ref[...], qkv_ref[...])
     x = x_ref[...]
     inverse = lax.rsqrt(jnp.mean(x * x, axis=-1, keepdims=True) + EPS)
-    gain_one_grad, extra = norm_back(x, inverse, gain_one, dh1)
+    gain_one_grad, extra = norm_back(x, inverse, gains_ref[pl.ds(0, 1), :], dh1)
     input_grad_ref[...] = dres_ref[...] + extra
     index = lax.broadcasted_iota(jnp.int32, (64, width), 0)
     gain_rows = jnp.where(index == 0, gain_one_grad, jnp.where(index == 1, gain_two_grad, 0.0)).astype(BF16)
     for k in range(shards):
         out_grad_ref[k, rows:, :] = gain_rows
-    mix_out[...] = jnp.zeros_like(mix_out)
-    chain.result(mix_out)
+    for reduce, piece in zip(reduces, pieces):
+        count = piece.shape[1]
+        both = jnp.concatenate([reduce.value(0), reduce.value(1)], axis=0)
+        for k in range(chips):
+            piece[k] = both[k * count : (k + 1) * count].astype(BF16)
+        reduce.sent()
+    mix_out[...] = chain.value()
     chain.sent()
-    if plane:
-        for reduce, piece in zip(reduces, pieces):
-            count = piece.shape[1]
-            both = jnp.concatenate([reduce.value(0), reduce.value(1)], axis=0)
-            for k in range(chips):
-                piece[k] = both[k * count : (k + 1) * count].astype(BF16)
-            reduce.sent()
-
-
-def rear(prefix, inputs, cotangent, resid, dh2, gains_full, kept, full, mix_part, halves, ident):
+
+
+def rear(prefix, inputs, cotangent, resid, dh2, gains, kept, full, mix_part, halves, ident):
     length, width = inputs.shape
     chips, shards = mix_part.shape[0], lax.axis_size("shard")
     plane = shards == 4
     cosine, sine = rope_lanes(length)
     vmem, anywhere = pl.BlockSpec(memory_space=pltpu.VMEM), pl.BlockSpec(memory_space=pl.ANY)
     shape, dma = jax.ShapeDtypeStruct, pltpu.SemaphoreType.DMA
-    operands = [prefix, inputs, cotangent, resid, dh2, gains_full, *kept, *full, cosine, sine, mix_part]
+    operands = [prefix, inputs, cotangent, resid, dh2, gains, *kept, *full, cosine, sine, mix_part]
     in_specs = [pl.BlockSpec(memory_space=pltpu.SMEM)] + [vmem] * 13 + [anywhere]
     out_shape = [
         shape((length, width), F32),
@@ -1158,146 +1199,125 @@
         out_specs=[vmem] * len(out_shape),
         scratch_shapes=scratch,
         compiler_params=pltpu.CompilerParams(
-            collective_id=ident, has_side_effects=True, vmem_limit_bytes=60 << 20
+            collective_id=ident, has_side_effects=True, vmem_limit_bytes=VMEM_BYTES
         ),
     )(*operands)
 
 
 def last_kernel(*refs, chips, shards):
-    (resid_ref, mix_ref, sy_ref), refs = refs[:3], refs[3:]
-    attention, pieces, down_hbm, refs = refs[:2], refs[2:5], refs[5], refs[6:]
-    output_ref, grads, refs = refs[0], refs[1:7], refs[7:]
-    halves, refs = refs[:4], refs[4:]
+    (attention, pieces, down_hbm), refs = (refs[:2], refs[2:5], refs[5]), refs[6:]
+    alls_out, down_out, refs = refs[:5], refs[5], refs[6:]
+    halves, refs = [refs[3 * k : 3 * k + 3] for k in range(2)], refs[6:]
     plane_work, refs = refs[:10], refs[10:]
-    chain_work, refs = refs[:25], refs[25:]
+    chain_work, refs = [refs[4 * k : 4 * k + 4] for k in range(5)], refs[20:]
     load_sem, core_send, core_recv, plane_send, plane_recv, sums_send, sums_recv, all_send, all_recv, all_local = refs
     at = place()
     core = at["core"]
-    chain_meet(at, chips, [at["dev_x"], at["dev_y"], at["dev_c"]])
-    swaps, loads = [], []
+    loads, swaps = [], []
     for k in range(2):
         rows = attention[k].shape[1] // 2
-        part = lambda c: attention[k].at[:, pl.ds(pl.multiple_of(c * rows, 16), rows), :]
-        swaps.append(
-            remote(part(1 - core), halves[2 * k + 1], core_send.at[k], core_recv.at[k], at["dev_c"])
-        )
-        loads.append(pltpu.make_async_copy(part(core), halves[2 * k], load_sem.at[k]))
-    chain_work = [chain_work[5 * k : 5 * k + 5] for k in range(5)]
-    loads += [pltpu.make_async_copy(pieces[k], chain_work[2 + k][0], load_sem.at[2 + k]) for k in range(3)]
-    loads.append(pltpu.make_async_copy(down_hbm, plane_work[0], load_sem.at[5]))
-    for made in swaps + loads:
+        for n, c in enumerate((core, 1 - core)):
+            part = attention[k].at[:, pl.ds(pl.multiple_of(c * rows, 16), rows), :]
+            loads.append(pltpu.make_async_copy(part, halves[k][n], load_sem.at[2 * k + n]))
+        swaps.append(remote(halves[k][1], halves[k][2], core_send.at[k], core_recv.at[k], at["dev_c"]))
+    loads += [pltpu.make_async_copy(pieces[k], chain_work[2 + k][0], load_sem.at[4 + k]) for k in range(3)]
+    loads.append(pltpu.make_async_copy(down_hbm, plane_work[0], load_sem.at[7]))
+    for made in loads:
         made.start()
     sums = [
         ChainReduce(*chain_work[k][:3], sums_send.at[k], sums_recv.at[k], at, chips) for k in range(5)
     ]
     alls = [
-        ChainGather(chain_work[k][3], chain_work[k][4], all_send.at[k], all_recv.at[k], all_local.at[k], at, chips)
+        ChainGather(chain_work[k][3], alls_out[k], all_send.at[k], all_recv.at[k], all_local.at[k], at, chips)
         for k in range(5)
     ]
     planes = [
         PlaneReduce(src, *plane_work[1 + 3 * k : 4 + 3 * k], plane_send.at[k], plane_recv.at[k], at)
-        for k, src in enumerate([plane_work[0], halves[0], halves[2]])
+        for k, src in enumerate([plane_work[0], halves[0][0], halves[1][0]])
     ]
-    ahead = (2, 3, 4)
-    for k in ahead:
+    shared, attn = (2, 3, 4), (0, 1)
+    chain_meet(at, chips, [at["dev_x"], at["dev_y"], at["dev_c"]])
+    for k in attn:
+        loads[2 * k].wait()
+        loads[2 * k + 1].wait()
+        swaps[k].start()
+
+    def tick(group, step):
+        for k in group:
+            sums[k].tick(step)
+
+    def step_all(group, step):
+        for k in group:
+            alls[k].step(step)
+
+    def total(group):
+        for k in group:
+            chain_work[k][3][...] = sums[k].value().astype(BF16)
+            alls[k].start()
+
+    for k in range(4, 8):
         loads[k].wait()
-        sums[k].move(1)
-    for k in range(2):
+    tick(shared, 0)
+    for k in attn:
         swaps[k].wait()
-        loads[k].wait()
 
         @pl.loop(0, shards)
         def _(shard):
-            halves[2 * k][shard] = (
-                halves[2 * k][shard].astype(F32) + halves[2 * k + 1][shard].astype(F32)
+            halves[k][0][shard] = (
+                halves[k][0][shard].astype(F32) + halves[k][2][shard].astype(F32)
             ).astype(BF16)
 
         planes[1 + k].first()
-    loads[5].wait()
+    for step in range(1, chips - 1):
+        tick(shared, step)
+    for k in attn:
+        planes[1 + k].second()
     planes[0].first()
-    output_ref[...] = resid_ref[...] + mix_ref[...] + sy_ref[...]
-    for step in range(2, chips):
-        for k in ahead:
-            sums[k].move(step)
-        if step == 2:
-            planes[1].second()
-            planes[2].second()
-
-    def total(k):
-        total_ref = chain_work[k][3]
-        z = at["z"]
-        value = sums[k].own[z].astype(F32)
-        pl.when(z > 0)(lambda: sums[k].copy(z, True).wait_recv())
-        pl.when(z < chips - 1)(lambda: sums[k].copy(z, False).wait_recv())
-        value += jnp.where(z > 0, sums[k].from_left[z].astype(F32), 0.0)
-        value += jnp.where(z < chips - 1, sums[k].from_right[z].astype(F32), 0.0)
-        total_ref[...] = value.astype(BF16)
-        alls[k].start()
-
-    for k in ahead:
-        total(k)
-    for k in range(2):
+    total(shared)
+    step_all(shared, 1)
+    for k in attn:
         count = chain_work[k][0].shape[1]
         both = jnp.concatenate([planes[1 + k].value(0), planes[1 + k].value(1)], axis=0)
         for n in range(chips):
             sums[k].own[n] = both[n * count : (n + 1) * count].astype(BF16)
-        sums[k].move(1)
-    for step in range(2, chips):
-        for k in range(2):
-            sums[k].move(step)
-        for k in ahead:
-            alls[k].step(step - 1)
-    for k in range(2):
-        total(k)
-    for k in ahead:
-        alls[k].step(chips - 1)
+    for step in range(chips - 1):
+        tick(attn, step)
+        if step:
+            step_all(shared, step + 1)
+    total(attn)
     planes[0].second()
     for step in range(1, chips):
-        for k in range(2):
-            alls[k].step(step)
-
-    def spread(k):
+        step_all(attn, step)
+    for turn in range(2):
+        down_out[pl.ds(turn * planes[0].half, planes[0].half), :] = planes[0].value(turn)
+    for k in shared + attn:
         for step in range(chips):
             alls[k].finish(step)
         alls[k].sent()
         sums[k].sent()
-        count = chain_work[k][0].shape[1]
-        for n in range(chips):
-            for c in range(2):
-                grads[k][pl.ds((c * chips + n) * count, count), :] = chain_work[k][4][2 * n + c].astype(F32)
-
-    for k in ahead:
-        spread(k)
-    for turn in range(2):
-        grads[5][pl.ds(turn * planes[0].half, planes[0].half), :] = planes[0].value(turn)
-    for k in range(2):
-        spread(k)
     for reduce in planes:
         reduce.sent()
 
 
-def last(resid, mixture, shared_out, qkv_grad, out_grad, pieces, down_blocks, ident):
-    length, width = resid.shape
+def last(qkv_grad, out_grad, pieces, down_blocks, ident):
     shards, chips = lax.axis_size("shard"), lax.axis_size("expert") // 2
     vmem, anywhere = pl.BlockSpec(memory_space=pltpu.VMEM), pl.BlockSpec(memory_space=pl.ANY)
     shape, dma = jax.ShapeDtypeStruct, pltpu.SemaphoreType.DMA
     attention = [qkv_grad, out_grad]
     half_shapes = [(shards, v.shape[1] // 2, v.shape[2]) for v in attention]
     chain_shapes = [(chips, v.shape[1] // 2 // chips, v.shape[2]) for v in attention] + [v.shape for v in pieces]
-    out_shape = [shape((length, width), F32)]
-    out_shape += [shape((2 * s[0] * s[1], s[2]), F32) for s in chain_shapes]
+    out_shape = [shape((2 * chips,) + s[1:], BF16) for s in chain_shapes]
     out_shape.append(shape(down_blocks.shape[1:], F32))
     scratch = []
     for s in half_shapes:
-        scratch += [pltpu.VMEM(s, BF16)] * 2
+        scratch += [pltpu.VMEM(s, BF16)] * 3
     scratch.append(pltpu.VMEM(down_blocks.shape, BF16))
     for s in [down_blocks.shape] + half_shapes:
         scratch += PlaneReduce.scratch(s)
     for s in chain_shapes:
-        scratch += ChainReduce.scratch(s)
-        scratch += [pltpu.VMEM(s[1:], BF16), pltpu.VMEM((2 * chips,) + s[1:], BF16)]
+        scratch += ChainReduce.scratch(s) + [pltpu.VMEM(s[1:], BF16)]
     scratch += [
-        dma((6,)),
+        dma((8,)),
         dma((2,)),
         dma((2,)),
         dma((3, PlaneReduce.COPIES)),
@@ -1311,13 +1331,67 @@
     return pl.pallas_call(
         functools.partial(last_kernel, chips=chips, shards=shards),
         out_shape=out_shape,
-        in_specs=[vmem] * 3 + [anywhere] * 6,
-        out_specs=[vmem] * 7,
+        in_specs=[anywhere] * 6,
+        out_specs=[vmem] * 6,
         scratch_shapes=scratch,
         compiler_params=pltpu.CompilerParams(
-            collective_id=ident, has_side_effects=True, vmem_limit_bytes=60 << 20
+            collective_id=ident, has_side_effects=True, vmem_limit_bytes=VMEM_BYTES
         ),
-    )(resid, mixture, shared_out, qkv_grad, out_grad, *pieces, down_blocks)
+    )(qkv_grad, out_grad, *pieces, down_blocks)
+
+
+def finish_kernel(*refs, chips):
+    (summands, sums, plain), refs = (refs[:3], refs[3:8], refs[8:12]), refs[12:]
+    (output, grads, plain_out), refs = (refs[0], refs[1:6], refs[6:10]), refs[10:]
+    (add_in, sum_in, plain_in, add_out, sum_out), (load_sem, store_sem) = (
+        (refs[:3], refs[3:8], refs[8:12], refs[12], refs[13:18]),
+        refs[18:],
+    )
+    held = [*plain_in, *sum_in, *add_in]
+    loads = [
+        pltpu.make_async_copy(a, b, load_sem.at[k]) for k, (a, b) in enumerate(zip([*plain, *sums, *summands], held))
+    ]
+    stores = [
+        pltpu.make_async_copy(a, b, store_sem.at[k])
+        for k, (a, b) in enumerate(zip([*plain_in, *sum_out, add_out], [*plain_out, *grads, output]))
+    ]
+    for made in loads:
+        made.start()
+    for k in range(4):
+        loads[k].wait()
+        stores[k].start()
+    for k in range(5):
+        loads[4 + k].wait()
+        count = sum_in[k].shape[1]
+        for n in range(chips):
+            for c in range(2):
+                sum_out[k][pl.ds((c * chips + n) * count, count), :] = sum_in[k][2 * n + c].astype(F32)
+        stores[4 + k].start()
+    for made in loads[9:]:
+        made.wait()
+    add_out[...] = add_in[0][...] + add_in[1][...] + add_in[2][...]
+    stores[9].start()
+    for made in stores:
+        made.wait()
+
+
+def finish(summands, sums, plain):
+    chips = sums[0].shape[0] // 2
+    shape, dma = jax.ShapeDtypeStruct, pltpu.SemaphoreType.DMA
+    anywhere = pl.BlockSpec(memory_space=pl.ANY)
+    inputs = [*summands, *sums, *plain]
+    out_shape = [shape(summands[0].shape, F32)]
+    out_shape += [shape((v.shape[0] * v.shape[1], v.shape[2]), F32) for v in sums]
+    scratch = [pltpu.VMEM(v.shape, v.dtype) for v in inputs] + [pltpu.VMEM(s.shape, F32) for s in out_shape]
+    out_shape += [shape(v.shape, F32) for v in plain]
+    return pl.pallas_call(
+        functools.partial(finish_kernel, chips=chips),
+        out_shape=out_shape,
+        in_specs=[anywhere] * len(inputs),
+        out_specs=[anywhere] * len(out_shape),
+        scratch_shapes=scratch + [dma((len(inputs),)), dma((len(out_shape),))],
+        compiler_params=pltpu.CompilerParams(vmem_limit_bytes=VMEM_BYTES),
+    )(*inputs)
 
 
 def on_device(
@@ -1340,12 +1414,7 @@
     length, width = inputs.shape
     experts, shards = lax.axis_size("expert"), lax.axis_size("shard")
     me, shard = lax.axis_index("expert"), lax.axis_index("shard")
-    gains = jnp.concatenate(
-        [jnp.broadcast_to(v, (32, v.shape[0])) for v in (norm_one, norm_two)], axis=0
-    )
-    gains = lax.dynamic_update_slice(
-        jnp.zeros((64, width), BF16), gains, (0, shard * norm_one.shape[0])
-    )
+    route_rows = routes.T
     (
         cot_all,
         table_all,
@@ -1356,9 +1425,9 @@
         resid,
         normed_two,
         cot_low,
+        gains,
         qkv_full,
         out_full,
-        gains_full,
         gate_blocks,
         up_blocks,
         down_full,
@@ -1366,12 +1435,10 @@
         prefix,
         inputs,
         cotangent,
-        routes.T,
+        route_rows,
         gate_weights.T,
-        qkv_weight,
-        out_weight,
-        gains,
-        [shared_gate, shared_up, shared_down],
+        [norm_one, norm_two],
+        [qkv_weight, out_weight, shared_gate, shared_up, shared_down],
         1,
     )
     (
@@ -1396,16 +1463,11 @@
         2,
     )
     shared_halves = [shared_halves[k + n] for k in range(3) for n in (0, 3)]
-    weight_got = lax.all_to_all(
-        weight_back.reshape(experts, length), "expert", split_axis=0, concat_axis=0, tiled=True
-    )
-    chosen = routes[:, :, None] == jnp.arange(experts, dtype=jnp.int32)[None, None, :]
-    gate_weights_grad = jnp.sum(jnp.where(chosen, weight_got.T[:, None, :], 0.0), axis=2)
     rows, grad_rows, hidden, gate_pre_grad, up_pre_grad = (
         v.reshape(-1, v.shape[-1]) for v in (rows, grad_rows, hidden, gate_pre_grad, up_pre_grad)
     )
-    gate_term, up_term, down_term, normed_two_grad = weights(
-        rows, grad_rows, shared_back, hidden, gate_pre_grad, up_pre_grad, back_part, 3
+    gate_term, up_term, down_term, normed_two_grad, gate_weights_grad = weights(
+        rows, grad_rows, shared_back, weight_back, route_rows, hidden, gate_pre_grad, up_pre_grad, back_part, 3
     )
     mixture, input_grad, qkv_grad, out_grad, *pieces = rear(
         prefix,
@@ -1413,7 +1475,7 @@
         cotangent,
         resid,
         normed_two_grad,
-        gains_full,
+        gains,
         [turned, attended, normed_one, logsum],
         [qkv_full, out_full],
         mix_part,
@@ -1422,8 +1484,9 @@
     )
     qkv_grad = qkv_grad.reshape(shards, width // shards, 3 * width)
     if shards == 4:
-        output, qkv_sum, out_sum, *shared_sums, down_term = last(
-            resid, mixture, shared_out, qkv_grad, out_grad, pieces, down_term, 5
+        *sums, down_term = last(qkv_grad, out_grad, pieces, down_term, 5)
+        output, qkv_sum, out_sum, *shared_sums, input_grad, gate_term, up_term, down_term = finish(
+            [resid, mixture, shared_out], sums, [input_grad, gate_term, up_term, down_term]
         )
     else:
 
@@ -1456,7 +1519,7 @@
         gate_term[None],
         up_term[None],
         down_term[None],
-        gate_weights_grad,
+        gate_weights_grad.T,
     )
 
 

time: 542 us -> 414 us (0.76)
  Pallas kernels: 499 us -> 402 us
  local copies, waits for them, and re-layouts: 28.6 us -> 6.33 us
    pallas_call x1, Pallas kernels: 117 us -> 63.9 us  [last(): pl.pallas_call(functools.partial(last_kernel, chips=chips, shards=shards)...]
    pallas_call x1, Pallas kernels: 115 us -> 67.6 us  [rear(): pl.pallas_call(functools.partial(rear_kernel, plane=plane, chips=chips, s...]
    unnamed x52 -> x3, local copies, waits for them, and re-layouts: 23.6 us -> 0.6 us
    pallas_call x0 -> x1, Pallas kernels: none -> 11.6 us  [finish(): pl.pallas_call(functools.partial(finish_kernel, chips=chips), out_shape=o...]
    pallas_call x1, Pallas kernels: 81.2 us -> 70.6 us  [weights(): pl.pallas_call(functools.partial(weights_kernel, plane=plane, chips=chips...]
  transfers between devices with their start and end apart: 1 -> 0, of which waited for: 0 -> 0; matrix products, arithmetic and copies ran while one was open for 1% -> 0% of each run, Pallas kernels for 58% -> 0%
where the time goes in v4:
time: 414 us; the launch traced here: 409 us
  Pallas kernels  402 us (97%)
  local copies, waits for them, and re-layouts  6.33 us (2%)
    pallas_call x1, Pallas kernels, middle(): pl.pallas_call(functools.partial(middle_kernel, chips=chips, shards=shard...  102 us
    pallas_call x1, Pallas kernels, front(): pl.pallas_call(functools.partial(front_kernel, plane=plane, chips=chips),...  86.1 us
    pallas_call x1, Pallas kernels, weights(): pl.pallas_call(functools.partial(weights_kernel, plane=plane, chips=chips...  70.6 us
    pallas_call x1, Pallas kernels, rear(): pl.pallas_call(functools.partial(rear_kernel, plane=plane, chips=chips, s...  67.6 us
    pallas_call x1, Pallas kernels, last(): pl.pallas_call(functools.partial(last_kernel, chips=chips, shards=shards)...  63.9 us
    pallas_call x1, Pallas kernels, finish(): pl.pallas_call(functools.partial(finish_kernel, chips=chips), out_shape=o...  11.6 us

profile of v4, /device:TPU:0, one launch (start us, length us, event | category | flops | bytes accessed | tf_op | source)
XLA Modules:
  0.0 409.5 jit_solution(9645395399625435472)
XLA Ops:
  1.3 1.2 broadcast_in_dim.15.refs_7_
  2.5 1.2 broadcast_in_dim.16.refs_8_
  3.7 86.1 %shard_map.282 = (bf16[8,512,768]{2,1,0:T(8,128)(2,1)}, f32[8,16,512]{2,1,0:T(8,128)}, bf16[512,768]{1,0:T(8,128)(2,1)}, bf16[512,2304]{1,0:T(8,128)(2,1)}, bf16...) custom-call(s32[1]{0:T(128)S(6)} %copy.33.refs_0_, ...), custom_call_target="tpu_custom_call" | custom-call | tf_op jit(solution)/shard_map/pallas_call | solution.py:436
  89.8 101.8 %shard_map.283 = (bf16[4,512,768]{2,1,0:T(8,128)(2,1)}, bf16[4,512,768]{2,1,0:T(8,128)(2,1)}, bf16[4,512,2048]{2,1,0:T(8,128)(2,1)}, bf16[4,512,2048]{2,1,0:T(8,...) custom-call(bf16[512,768]{1,0:T(8,128)(2,1)} %get-tuple-element.73.r, ...), custom_call_target="tpu_custom_call" | custom-call | tf_op jit(solution)/shard_map/pallas_call | solution.py:773
  191.6 70.6 %shard_map.284 = (f32[768,512]{1,0:T(8,128)}, f32[768,512]{1,0:T(8,128)}, bf16[4,512,768]{2,1,0:T(8,128)(2,1)}, f32[512,768]{1,0:T(8,128)}, f32[2,512]{1,0:T(2,128)}) custom-call(bf16[2048,768]{1,0:T(8,128)(2,1)} %bitcast.18, bf16[2048,768]{1,0:T(8,128)(2,1)} %bitcast.19, f32[512,768]{1,0:T(8,128)} %get-tuple-element.82.refs_2_, ...), custom_call_target="tpu_custom_call" | custom-call | tf_op jit(solution)/shard_map/pallas_call | solution.py:1014
  262.2 67.6 %shard_map.285 = (f32[512,768]{1,0:T(8,128)}, f32[512,768]{1,0:T(8,128)}, bf16[768,2304]{1,0:T(8,128)(2,1)}, bf16[4,256,768]{2,1,0:T(8,128)(2,1)}, bf16[4,96,512...) custom-call(s32[1]{0:T(128)S(6)} %copy.33.refs_0_, f32[512,768]{1,0:T(8,128)} %refs_1_.3, ...), custom_call_target="tpu_custom_call" | custom-call | tf_op jit(solution)/shard_map/pallas_call | solution.py:1195
  329.8 63.9 %shard_map.286 = (bf16[8,24,2304]{2,1,0:T(8,128)(2,1)}, bf16[8,32,768]{2,1,0:T(8,128)(2,1)}, bf16[8,96,512]{2,1,0:T(8,128)(2,1)}, bf16[8,96,512]{2,1,0:T(8,128)(...) custom-call(bf16[4,192,2304]{2,1,0:T(8,128)(2,1)} %bitcast.17, bf16[4,256,768]{2,1,0:T(8,128)(2,1)} %get-tuple-element.106.refs_1_, ...), custom_call_target="tpu_custom_call" | custom-call | tf_op jit(solution)/shard_map/pallas_call | solution.py:1331
  393.8 0.0 copy-start
  393.8 11.6 %shard_map.287 = (f32[512,768]{1,0:T(8,128)}, f32[192,2304]{1,0:T(8,128)}, f32[256,768]{1,0:T(8,128)}, f32[768,512]{1,0:T(8,128)}, f32[768,512]{1,0:T(8,128)}, /...) custom-call(f32[512,768]{1,0:T(8,128)} %get-tuple-element.72.refs_3_, ...), custom_call_target="tpu_custom_call" | custom-call | tf_op jit(solution)/shard_map/pallas_call | solution.py:1387
  405.4 1.9 slice.14
  407.3 0.7 slice.12
  408.0 0.6 fusion
  408.7 0.0 copy-done
  408.7 0.6 copy.34
Async XLA Ops:
  393.8 14.9 %copy-start = (f32[2,512]{1,0:T(2,128)S(1)}, f32[2,512]{1,0:T(2,128)}, u32[]{:S(2)}) copy-start(f32[2,512]{1,0:T(2,128)} %get-tuple-element.130) | copy-start | bytes 12292

commit v5 on v4

--- a/solution.py
+++ b/solution.py
@@ -15,7 +15,7 @@
 MESH = pl.DeviceIdType.MESH
 F32 = jnp.float32
 BF16 = jnp.bfloat16
-VMEM_BYTES = 61 << 20
+VMEM_BYTES = 63 << 20
 
 
 def place():
@@ -248,14 +248,15 @@
     (prefix, x_ref, cot_ref, route_ref, weight_ref, cos_ref, sin_ref), refs = refs[:7], refs[7:]
     (one_ref, two_ref), refs = refs[:2], refs[2:]
     weights, refs = (refs[:5], refs[5:]) if plane else (refs[:2], refs[2:])
-    (cot_out, table_out, h1_ref, rot_ref, att_ref, lse_ref, resid_ref, h2_ref, cot_low, gains_ref), refs = refs[:10], refs[10:]
+    (cot_out, table_out, h1_out, rot_out, att_out, resid_out, h2_out, cot_low, lse_ref, gains_ref), refs = refs[:10], refs[10:]
     full_out, refs = (refs[:5], refs[5:]) if plane else ([], refs)
-    (bias_ref, table_ref, table_all, cot_all, out_sem, chain_send, chain_recv, chain_local), refs = refs[:8], refs[8:]
+    (h1_ref, rot_ref, att_ref, resid_ref, h2_ref, cot_low_ref), refs = refs[:6], refs[6:]
+    (bias_ref, table_ref, table_all, cot_all, out_sem, chain_sem, chain_send, chain_recv, chain_local), refs = refs[:9], refs[9:]
     length, width = x_ref.shape
     experts = table_ref.shape[0] // 2
     at = place()
     if plane:
-        gains_src, gains_full, full, (send, recv, local, full_sem) = refs[0], refs[1], refs[2:7], refs[7:]
+        gains_src, gains_full, full, (send, recv, local) = refs[0], refs[1], refs[2:7], refs[7:]
         gathers = [
             PlaneGather(a, b, send.at[k], recv.at[k], local.at[k], at)
             for k, (a, b) in enumerate(zip([*weights, gains_src], [*full, gains_full]))
@@ -272,7 +273,7 @@
     if plane:
         for gather in first:
             gather.first()
-    cot_low[...] = cot_ref[...].astype(BF16)
+    cot_low_ref[...] = cot_ref[...].astype(BF16)
     names = lax.broadcasted_iota(jnp.int32, (experts, length), 0)
     chosen = [route_ref[pl.ds(k, 1), :] == names for k in range(TOP)]
     member = (chosen[0] | chosen[1]).astype(F32)
@@ -287,25 +288,51 @@
     )
     chains = [
         ChainGather(a, b, chain_send.at[k], chain_recv.at[k], chain_local.at[k], at, chips)
-        for k, (a, b) in enumerate([(table_ref, table_all), (cot_low, cot_all)])
+        for k, (a, b) in enumerate([(table_ref, table_all), (cot_low_ref, cot_all)])
     ]
     for chain in chains:
         chain.start()
     set_bias(bias_ref, prefix)
+    keeps = []
+
+    def keep(src, dst):
+        made = pltpu.make_async_copy(src, dst, out_sem.at[len(keeps)])
+        made.start()
+        keeps.append(made)
+
+    def each_kept(step, act):
+        for n, side in enumerate((-1, 1) if step else (1,)):
+            chip = at["z"] + side * step
+
+            @pl.when((chip >= 0) & (chip < chips))
+            def _():
+                for k, (src, dst) in enumerate([(table_all, table_out), (cot_all, cot_out)]):
+                    part = pl.ds(2 * chip, 2)
+                    act(pltpu.make_async_copy(src.at[part], dst.at[part], chain_sem.at[step, n, k]))
+
+    def keep_chain(step):
+        each_kept(step, lambda made: made.start())
+
+    keep(cot_low_ref, cot_low)
     if plane:
-        for step in ("second", "third", "finish"):
+        for gather in first:
+            gather.second()
+        for gather in later:
+            gather.first()
+        for chain in chains:
+            chain.step(1)
+        for step in ("third", "finish"):
             for gather in first:
                 getattr(gather, step)()
-        for gather in later:
-            gather.first()
-        outs = [pltpu.make_async_copy(a, b, full_sem.at[k]) for k, (a, b) in enumerate(zip(full, full_out))]
-        for made in outs[:2]:
-            made.start()
+        for k in range(2):
+            keep(full[k], full_out[k])
         blocks = range(gains_full.shape[0] // 64)
         for k in range(2):
             row = [gains_full[pl.ds(64 * n + 32 * k, 1), :].astype(F32) for n in blocks]
             gains_ref[pl.ds(k, 1), :] = jnp.concatenate(row, axis=1)
     else:
+        for chain in chains:
+            chain.step(1)
         gains_ref[pl.ds(0, 1), :] = one_ref[...].astype(F32)
         gains_ref[pl.ds(1, 1), :] = two_ref[...].astype(F32)
     x = x_ref[...]
@@ -323,8 +350,8 @@
 
     pl.loop(0, 2 * width // 256)(lambda block: project(block, True))
     pl.loop(2 * width // 256, 3 * width // 256)(lambda block: project(block, False))
-    for chain in chains:
-        chain.step(1)
+    keep(h1_ref, h1_out)
+    keep(rot_ref, rot_out)
     lse_ref[...] = jnp.zeros_like(lse_ref)
     count = length // 2
 
@@ -357,33 +384,37 @@
         for chain in chains:
             chain.step(step)
     pl.loop(pairs // 2, pairs)(pair)
+    keep(att_ref, att_out)
+    resid = x_ref[...] + dot_nn(att_ref[...], out_full[...])
+    resid_ref[...] = resid
+    keep(resid_ref, resid_out)
+    inverse = lax.rsqrt(jnp.mean(resid * resid, axis=-1, keepdims=True) + EPS)
+    h2_ref[...] = (resid * inverse * gains_ref[pl.ds(1, 1), :]).astype(BF16)
+    keep(h2_ref, h2_out)
+    for step in range(chips - 1):
+        for chain in chains:
+            chain.finish(step)
+        keep_chain(step)
     if plane:
         for gather in later:
             gather.second()
-    resid = x_ref[...] + dot_nn(att_ref[...], out_full[...])
-    resid_ref[...] = resid
-    inverse = lax.rsqrt(jnp.mean(resid * resid, axis=-1, keepdims=True) + EPS)
-    h2_ref[...] = (resid * inverse * gains_ref[pl.ds(1, 1), :]).astype(BF16)
     for chain in chains:
         chain.step(chips - 1)
     if plane:
-        for step in ("third", "finish"):
-            for gather in later:
-                getattr(gather, step)()
-        for made in outs[2:]:
-            made.start()
+        for gather in later:
+            gather.third()
     for chain in chains:
-        for step in range(chips):
-            chain.finish(step)
-    keep = [
-        pltpu.make_async_copy(a, b, out_sem.at[k])
-        for k, (a, b) in enumerate([(table_all, table_out), (cot_all, cot_out)])
-    ]
-    for made in keep:
-        made.start()
+        chain.finish(chips - 1)
+    keep_chain(chips - 1)
+    if plane:
+        for k, gather in enumerate(later):
+            gather.finish()
+            keep(full[2 + k], full_out[2 + k])
     for chain in chains:
         chain.sent()
-    for made in keep + (outs if plane else []):
+    for step in range(chips):
+        each_kept(step, lambda made: made.wait())
+    for made in keeps:
         made.wait()
 
 
@@ -393,7 +424,7 @@
     chips, plane = group // 2, shards == 4
     cosine, sine = rope_lanes(length)
     vmem, anywhere = pl.BlockSpec(memory_space=pltpu.VMEM), pl.BlockSpec(memory_space=pl.ANY)
-    gains = [v[None, :] for v in gains]
+    gains = [v.reshape(1, -1) for v in gains]
     if not plane:
         gains = [lax.all_gather(v, "shard", axis=1, tiled=True) for v in gains]
         weights = [lax.all_gather(v, "shard", axis=0, tiled=True) for v in weights]
@@ -408,19 +439,21 @@
         shape((length, width), BF16),
         shape((length, 3 * width), BF16),
         shape((length, width), BF16),
-        shape((length, 128), F32),
         shape((length, width), F32),
         shape((length, width), BF16),
         shape((length, width), BF16),
+        shape((length, 128), F32),
         shape((8, width), F32),
     ]
-    out_specs = [anywhere] * 2 + [vmem] * 8
-    scratch = [
+    out_specs = [anywhere] * 8 + [vmem] * 2
+    scratch = [pltpu.VMEM(s.shape, s.dtype) for s in out_shape[2:8]]
+    scratch += [
         pltpu.VMEM((length, length), F32),
         pltpu.VMEM((2 * group, length), F32),
         pltpu.VMEM((group, 2 * group, length), F32),
         pltpu.VMEM((group, length, width), BF16),
-        dma((2,)),
+        dma((11,)),
+        dma((chips, 2, 2)),
         dma((2, ChainGather.copies(chips))),
         dma((2, ChainGather.copies(chips))),
         dma((2,)),
@@ -432,7 +465,7 @@
         part = gains[0].shape[1]
         scratch += [pltpu.VMEM((64, part), BF16), pltpu.VMEM((64 * shards, part), BF16)]
         scratch += [pltpu.VMEM(s, BF16) for s in full]
-        scratch += [dma((6, PlaneGather.COPIES)), dma((6, PlaneGather.COPIES)), dma((6,)), dma((5,))]
+        scratch += [dma((6, PlaneGather.COPIES)), dma((6, PlaneGather.COPIES)), dma((6,))]
     outs = pl.pallas_call(
         functools.partial(front_kernel, plane=plane, chips=chips),
         out_shape=out_shape,
@@ -472,20 +505,18 @@
     return hidden, gate_grad, up_grad, result, back
 
 
-def middle_kernel(*refs, chips, shards, capacity):
-    (h2_ref, cot_ref, table_ref, cot_all, gate_hbm, up_hbm, down_hbm, sg_hbm, su_hbm, sd_hbm), refs = refs[:10], refs[10:]
+def middle_kernel(*refs, chips, capacity):
+    (h2_ref, table_ref, cot_all, gate_hbm, up_hbm, down_hbm), refs = refs[:6], refs[6:]
     (rows_out, grad_out, hid_out, da_out, db_out, mix_out, back_out), refs = refs[:7], refs[7:]
-    sown, sgot, (dots_out, sy_ref, dh_ref), refs = refs[:3], refs[3:6], refs[6:9], refs[9:]
-    (sgg_s, sug_s, sdg_s, sg_sem, sg_send, sg_recv), refs = refs[:6], refs[6:]
-    (gate_w, up_w, down_w, sg_w, su_w, sd_w, h2_all, cot_buf, rows_ref, grad_ref, cotr_ref, scale_ref), refs = refs[:12], refs[12:]
+    dots_out, refs = refs[0], refs[1:]
+    (gate_w, up_w, down_w, h2_all, cot_buf, rows_ref, grad_ref, cotr_ref, scale_ref), refs = refs[:9], refs[9:]
     (y_acc, r_acc, stage_f, stage_s, stage_t, got, total), refs = refs[:7], refs[7:]
-    w_sem, s_sem, cot_sem, row_sem, f_sem, tot_sem, core_send, core_recv, chain_send, chain_recv, chain_local = refs
+    w_sem, cot_sem, row_sem, f_sem, tot_sem, core_send, core_recv, chain_send, chain_recv, chain_local = refs
     length, width = h2_ref.shape
     experts = 2 * chips
     hidden_width = gate_w.shape[1]
     unit = stage_f.shape[-1]
     units = hidden_width // unit
-    block = sg_w.shape[-1]
     at = place()
     me, core, z = at["expert"], at["core"], at["z"]
     order = near_order(chips)
@@ -507,24 +538,14 @@
     for load in loads:
         load.start()
 
-    def load_shared(k, slot):
-        return [
-            pltpu.make_async_copy(sg_hbm.at[pl.ds(k * width, width), :], sg_w.at[slot], s_sem.at[slot, 0]),
-            pltpu.make_async_copy(su_hbm.at[pl.ds(k * width, width), :], su_w.at[slot], s_sem.at[slot, 1]),
-            pltpu.make_async_copy(sd_hbm.at[pl.ds(k * block, block), :], sd_w.at[slot], s_sem.at[slot, 2]),
-        ]
-
-    for load in load_shared(0, 0):
-        load.start()
-
     def one_hot(source):
         slots = table_ref[source, pl.ds(me, 1), :]
         return lax.broadcasted_iota(jnp.int32, (capacity, length), 0).astype(F32) == slots
 
     def row_copies(step):
         return [
-            pltpu.make_async_copy(rows_ref.at[step % 2], rows_out.at[step], row_sem.at[step % 2, 0]),
-            pltpu.make_async_copy(grad_ref.at[step % 2], grad_out.at[step], row_sem.at[step % 2, 1]),
+            pltpu.make_async_copy(rows_ref, rows_out.at[step], row_sem.at[0]),
+            pltpu.make_async_copy(grad_ref, grad_out.at[step], row_sem.at[1]),
         ]
 
     def hidden_copies(step, k, slot):
@@ -566,19 +587,19 @@
         load_cot(step).wait()
         if step + 1 < chips:
             load_cot(step + 1).start()
-        if step >= 2:
-            for copy in row_copies(step - 2):
+        if step > 0:
+            for copy in row_copies(step - 1):
                 copy.wait()
         for d in range(2):
             source, part = 2 * chip + d, pl.ds(d * capacity, capacity)
             chosen = one_hot(source)
             select = chosen.astype(F32).astype(BF16)
-            rows_ref[slot, part, :] = dot_nn(select, h2_all[source]).astype(BF16)
+            rows_ref[part, :] = dot_nn(select, h2_all[source]).astype(BF16)
             cot_rows = dot_nn(select, cot_buf[slot, d])
             scale = jnp.sum(
                 jnp.where(chosen, table_ref[source, pl.ds(experts + me, 1), :], 0.0), axis=1, keepdims=True
             )
-            grad_ref[slot, part, :] = (cot_rows * scale).astype(BF16)
+            grad_ref[part, :] = (cot_rows * scale).astype(BF16)
             cotr_ref[part, :] = cot_rows.astype(BF16)
             scale_ref[part, :] = scale
         for copy in row_copies(step):
@@ -589,11 +610,10 @@
             for load in loads:
                 load.wait()
 
-        @pl.loop(0, units)
-        def _(k):
+        def one_unit(k):
             cols = columns(k * unit, unit)
             hidden, gate_grad, up_grad, result, back = gated_block(
-                rows_ref[slot], grad_ref[slot], gate_w[:, cols], up_w[:, cols],
+                rows_ref[...], grad_ref[...], gate_w[:, cols], up_w[:, cols],
                 down_w[pl.ds(pl.multiple_of(k * unit, unit), unit), :],
             )
             turn = k % 2
@@ -614,6 +634,12 @@
             y_acc[...] += result
             r_acc[...] += back
 
+        if step + 1 < chips:
+            pl.loop(0, units - 1)(one_unit)
+            chain.step(step + 1)
+            pl.loop(units - 1, units)(one_unit)
+        else:
+            pl.loop(0, units)(one_unit)
         if step > 0:
             join(step - 1)
         result = y_acc[...].astype(BF16).astype(F32)
@@ -631,86 +657,26 @@
         for copy in core_copies(step):
             copy.start()
 
-    sy_ref[...] = jnp.zeros_like(sy_ref)
-    dh_ref[...] = jnp.zeros_like(dh_ref)
-
-    def shared_copies(k):
-        stay, over = [], []
-        for n, held in enumerate((sgg_s, sug_s, sdg_s)):
-            half = held.shape[0] // 2
-            mine, other = (held.at[pl.ds(pl.multiple_of(c * half, 16), half), :] for c in (core, 1 - core))
-            stay.append((mine, sown[n].at[k], sg_sem.at[n]))
-            over.append((other, sgot[n].at[k], sg_send.at[n], sg_recv.at[n, k], at["dev_c"]))
-        return stay, over
-
-    def shared_settle(k):
-        stay, over = shared_copies(k)
-        for copy in stay:
-            pltpu.make_async_copy(*copy).wait()
-        for copy in over:
-            remote(*copy).wait_send()
-
-    def shared_block(k):
-        slot = k % 2
-        for load in load_shared(k, slot):
-            load.wait()
-
-        @pl.when(k + 1 < shards)
-        def _():
-            for load in load_shared(k + 1, 1 - slot):
-                load.start()
-
-        hidden, gate_grad, up_grad, result, back = gated_block(
-            h2_ref[...], cot_ref[...], sg_w[slot], su_w[slot], sd_w[slot]
-        )
-        sy_ref[...] += result
-        dh_ref[...] += back
-        pl.when(k > 0)(lambda: shared_settle(k - 1))
-        sgg_s[...] = dot_tn(h2_ref[...], gate_grad).astype(BF16)
-        sug_s[...] = dot_tn(h2_ref[...], up_grad).astype(BF16)
-        sdg_s[...] = dot_tn(hidden, cot_ref[...]).astype(BF16)
-        stay, over = shared_copies(k)
-        for copy in stay:
-            pltpu.make_async_copy(*copy).start()
-        for copy in over:
-            remote(*copy).start()
-
-    chain.finish(0)
-    expert_rows(0)
-    pl.loop(0, shards // 2)(shared_block)
-    chain.step(1)
-    pl.loop(shards // 2, shards)(shared_block)
-    for step in range(1, chips):
-        if step > 1:
-            chain.step(step)
+    for step in range(chips):
         chain.finish(step)
         expert_rows(step)
     join(chips - 1)
-    shared_settle(shards - 1)
-
-    @pl.loop(0, shards)
-    def _(k):
-        for copy in shared_copies(k)[1]:
-            remote(*copy).wait_recv()
-
     for copy in total_copies(chips - 1):
         copy.wait()
-    for step in range(max(0, chips - 2), chips):
-        for copy in row_copies(step):
-            copy.wait()
+    for copy in row_copies(chips - 1):
+        copy.wait()
     for k in range(max(0, units - 2), units):
         for copy in hidden_copies(chips - 1, k, k % 2):
             copy.wait()
     chain.sent()
 
 
-def middle(h2, cot_low, table_all, cot_all, expert_weights, shared_full, ident):
+def middle(h2, table_all, cot_all, expert_weights, ident):
     length, width = h2.shape
-    group, shards = lax.axis_size("expert"), lax.axis_size("shard")
+    group = lax.axis_size("expert")
     chips = group // 2
     capacity = 4 * length // group
     hidden_width = expert_weights[0].shape[2]
-    block = shared_full[0].shape[1]
     unit = min(512, hidden_width)
     vmem, anywhere = pl.BlockSpec(memory_space=pltpu.VMEM), pl.BlockSpec(memory_space=pl.ANY)
     shape = jax.ShapeDtypeStruct
@@ -723,32 +689,17 @@
         shape((chips, both, hidden_width), BF16),
         shape((chips, length, width), BF16),
         shape((chips, length, width), BF16),
-        *[shape((shards, width // 2, block), BF16)] * 2,
-        shape((shards, block // 2, width), BF16),
-        *[shape((shards, width // 2, block), BF16)] * 2,
-        shape((shards, block // 2, width), BF16),
         shape((group, 1, length), F32),
-        shape((length, width), F32),
-        shape((length, width), F32),
     ]
     dma = pltpu.SemaphoreType.DMA
     scratch = [
-        pltpu.VMEM((width, block), BF16),
-        pltpu.VMEM((width, block), BF16),
-        pltpu.VMEM((block, width), BF16),
-        dma((3,)),
-        dma((3,)),
-        dma((3, shards)),
         pltpu.VMEM((width, hidden_width), BF16),
         pltpu.VMEM((width, hidden_width), BF16),
         pltpu.VMEM((hidden_width, width), BF16),
-        pltpu.VMEM((2, width, block), BF16),
-        pltpu.VMEM((2, width, block), BF16),
-        pltpu.VMEM((2, block, width), BF16),
         pltpu.VMEM((group, length, width), BF16),
         pltpu.VMEM((2, 2, length, width), BF16),
-        pltpu.VMEM((2, both, width), BF16),
-        pltpu.VMEM((2, both, width), BF16),
+        pltpu.VMEM((both, width), BF16),
+        pltpu.VMEM((both, width), BF16),
         pltpu.VMEM((both, width), BF16),
         pltpu.VMEM((both, 1), F32),
         pltpu.VMEM((both, width), F32),
@@ -759,9 +710,8 @@
         pltpu.VMEM((2, chips, length, width), BF16),
         pltpu.VMEM((2, length, width), BF16),
         dma((3,)),
-        dma((2, 3)),
         dma((2,)),
-        dma((2, 2)),
+        dma((2,)),
         dma((2, 3)),
         dma((2,)),
         dma((2, chips)),
@@ -771,15 +721,15 @@
         dma,
     ]
     return pl.pallas_call(
-        functools.partial(middle_kernel, chips=chips, shards=shards, capacity=capacity),
+        functools.partial(middle_kernel, chips=chips, capacity=capacity),
         out_shape=out_shape,
-        in_specs=[vmem] * 3 + [anywhere] * 7,
-        out_specs=[anywhere] * 13 + [vmem] * 3,
+        in_specs=[vmem] * 2 + [anywhere] * 4,
+        out_specs=[anywhere] * 7 + [vmem],
         scratch_shapes=scratch,
         compiler_params=pltpu.CompilerParams(
             collective_id=ident, has_side_effects=True, vmem_limit_bytes=VMEM_BYTES
         ),
-    )(h2, cot_low, table_all, cot_all, *expert_weights, *shared_full)
+    )(h2, table_all, cot_all, *expert_weights)
 
 
 class ChainReduce:
@@ -858,45 +808,53 @@
             pltpu.VMEM((2, half, shape[2]), BF16),
         ]
 
-    def send_to(self, src, dst, index, device):
-        made = remote(src, dst, self.send.at[index], self.recv.at[index], device)
-        made.start()
-        return made
-
-    def first(self):
+    def copy(self, slot):
         at, half = self.at, self.half
-        upper, lower = pl.ds(0, half), pl.ds(half, half)
-        self.out = [
-            self.send_to(self.src.at[shard, rows, :], self.got.at[slot], slot, device)
-            for slot, (shard, rows, device) in enumerate(
-                [
-                    (at["sx"], upper, at["dev_x"]),
-                    (at["sd"], upper, at["dev_x"]),
-                    (at["sy"], lower, at["dev_y"]),
-                    (at["sd"], lower, at["dev_y"]),
-                ]
-            )
-        ]
+        shard = (at["sx"], at["sd"], at["sy"], at["sd"])[slot]
+        rows = pl.ds(slot // 2 * half, half)
+        device = at["dev_x"] if slot < 2 else at["dev_y"]
+        return remote(
+            self.src.at[shard, rows, :], self.got.at[slot], self.send.at[slot], self.recv.at[slot], device
+        )
+
+    def first(self, slots=(1, 3, 0, 2)):
+        for slot in slots:
+            self.copy(slot).start()
+
+    def first_of(self, index):
+        for k, slots in enumerate(((1, 3), (0,), (2,))):
+            pl.when(index == k)(lambda: self.first(slots))
+
+    def onward(self, turn):
+        return remote(
+            self.hold.at[turn],
+            self.last.at[turn],
+            self.send.at[4 + turn],
+            self.recv.at[4 + turn],
+            self.at["dev_x"] if turn else self.at["dev_y"],
+        )
 
     def second(self):
         at, half = self.at, self.half
-        for slot, shard, device in ((1, at["sy"], at["dev_y"]), (3, at["sx"], at["dev_x"])):
-            self.out[slot].wait_recv()
-            turn = slot // 2
+        for turn, shard in enumerate((at["sy"], at["sx"])):
+            slot = 2 * turn + 1
+            self.copy(slot).wait_recv()
             mine = self.src[shard, pl.ds(turn * half, half), :]
             self.hold[turn] = (mine.astype(F32) + self.got[slot].astype(F32)).astype(BF16)
-            self.out.append(self.send_to(self.hold.at[turn], self.last.at[turn], 4 + turn, device))
+            self.onward(turn).start()
 
     def value(self, turn):
         half = self.half
-        self.out[2 * turn].wait_recv()
-        self.out[4 + turn].wait_recv()
+        self.copy(2 * turn).wait_recv()
+        self.onward(turn).wait_recv()
         mine = self.src[self.at["shard"], pl.ds(turn * half, half), :]
         return (mine.astype(F32) + self.got[2 * turn].astype(F32)) + self.last[turn].astype(F32)
 
     def sent(self):
-        for made in self.out:
-            made.wait_send()
+        for slot in range(4):
+            self.copy(slot).wait_send()
+        for turn in range(2):
+            self.onward(turn).wait_send()
 
 
 def plane_blocks(at, index, plane):
@@ -907,15 +865,28 @@
 
 
 def weights_kernel(*refs, plane, chips, shards):
-    (rows_ref, grad_ref, dh_ref, dots_ref, route_ref, hid_hbm, da_hbm, db_hbm, back_hbm), refs = refs[:9], refs[9:]
-    (gate_out, up_out, down_out, sum_ref, chosen_ref), refs = refs[:5], refs[5:]
+    (dots_ref, route_ref, rows_hbm, grad_hbm, h2_hbm, cot_hbm, hid_hbm, da_hbm, db_hbm, back_hbm), refs = refs[:10], refs[10:]
+    (sg_hbm, su_hbm, sd_hbm), refs = refs[:3], refs[3:]
+    (down_out, sown, sgot, refs) = refs[0], refs[1:4], refs[4:7], refs[7:]
+    (gate_out, up_out, sum_ref, sy_ref, chosen_ref), refs = refs[:5], refs[5:]
+    (rows_ref, grad_ref, h2_ref, cot_ref, down_blocks, in_sem, down_sem), refs = refs[:7], refs[7:]
+    (sg_w, su_w, sd_w, sgg_s, sug_s, sdg_s, s_sem, sg_sem, sg_send, sg_recv), refs = refs[:10], refs[10:]
     (chunk, own, from_left, from_right, dots_got), refs = refs[:5], refs[5:]
     (own_sem, chunk_sem, dots_send, dots_recv, chain_send, chain_recv), refs = refs[:6], refs[6:]
     block = chunk.shape[-1]
     at = place()
-    me, group = at["expert"], 2 * chips
+    me, group, core = at["expert"], 2 * chips, at["core"]
+    width = h2_ref.shape[1]
     load = pltpu.make_async_copy(back_hbm, own, own_sem)
     load.start()
+    inputs = [
+        pltpu.make_async_copy(a, b, in_sem.at[k])
+        for k, (a, b) in enumerate(
+            [(rows_hbm, rows_ref), (grad_hbm, grad_ref), (h2_hbm, h2_ref), (cot_hbm, cot_ref)]
+        )
+    ]
+    for made in inputs:
+        made.start()
     peers = [(lax.rem(me + k, group), at["shard"]) for k in range(1, group)]
     meet(peers + ([at["dev_x"], at["dev_y"]] if plane else []))
     if plane:
@@ -923,9 +894,9 @@
         reduces = [
             PlaneReduce(work[4 * k], *work[4 * k + 1 : 4 * k + 4], send.at[k], recv.at[k], at) for k in range(2)
         ]
-        targets = [work[0], work[4], down_out]
+        targets = [work[0], work[4], down_blocks]
     else:
-        targets = [gate_out, up_out, down_out]
+        targets = [gate_out, up_out, down_blocks]
     sources = [da_hbm, db_hbm, hid_hbm]
     dots = [
         remote(dots_ref.at[peer[0]], dots_got.at[me], dots_send.at[k], dots_recv.at[k], peer)
@@ -950,9 +921,65 @@
             held = chunk[index % 2]
             if array < 2:
                 targets[array][shard] = dot_tn(rows_ref[...], held).astype(BF16)
+                if plane:
+                    reduces[array].first_of(index)
             else:
                 targets[array][shard] = dot_tn(held, grad_ref[...]).astype(BF16)
 
+    def load_shared(k, slot):
+        return [
+            pltpu.make_async_copy(sg_hbm.at[pl.ds(k * width, width), :], sg_w.at[slot], s_sem.at[slot, 0]),
+            pltpu.make_async_copy(su_hbm.at[pl.ds(k * width, width), :], su_w.at[slot], s_sem.at[slot, 1]),
+            pltpu.make_async_copy(sd_hbm.at[pl.ds(k * block, block), :], sd_w.at[slot], s_sem.at[slot, 2]),
+        ]
+
+
+    sy_ref[...] = jnp.zeros_like(sy_ref)
+    sum_ref[...] = jnp.zeros_like(sum_ref)
+
+    def shared_copies(k):
+        stay, over = [], []
+        for n, held in enumerate((sgg_s, sug_s, sdg_s)):
+            half = held.shape[0] // 2
+            mine, other = (held.at[pl.ds(pl.multiple_of(c * half, 16), half), :] for c in (core, 1 - core))
+            stay.append((mine, sown[n].at[k], sg_sem.at[n]))
+            over.append((other, sgot[n].at[k], sg_send.at[n], sg_recv.at[n, k], at["dev_c"]))
+        return stay, over
+
+    def shared_settle(k):
+        stay, over = shared_copies(k)
+        for copy in stay:
+            pltpu.make_async_copy(*copy).wait()
+        for copy in over:
+            remote(*copy).wait_send()
+
+    def shared_block(k):
+        slot = k % 2
+        for load in load_shared(k, slot):
+            load.wait()
+
+        @pl.when(k + 1 < shards)
+        def _():
+            for load in load_shared(k + 1, 1 - slot):
+                load.start()
+
+        hidden, gate_grad, up_grad, result, back = gated_block(
+            h2_ref[...], cot_ref[...], sg_w[slot], su_w[slot], sd_w[slot]
+        )
+        sy_ref[...] += result
+        sum_ref[...] += back
+        pl.when(k > 0)(lambda: shared_settle(k - 1))
+        sgg_s[...] = dot_tn(h2_ref[...], gate_grad).astype(BF16)
+        sug_s[...] = dot_tn(h2_ref[...], up_grad).astype(BF16)
+        sdg_s[...] = dot_tn(hidden, cot_ref[...]).astype(BF16)
+        stay, over = shared_copies(k)
+        for copy in stay:
+            pltpu.make_async_copy(*copy).start()
+        for copy in over:
+            remote(*copy).start()
+
+    for made in load_shared(0, 0):
+        made.start()
     fetch(0, 0).start()
     chain = ChainReduce(own, from_left, from_right, chain_send, chain_recv, at, chips)
     load.wait()
@@ -960,19 +987,25 @@
     for made in dots:
         made.start()
     dots_got[me] = dots_ref[me]
+    for made in inputs[:1]:
+        made.wait()
     make(0, 0, shards)
-    if plane:
-        reduces[0].first()
     make(1, 0, shards // 2)
     for step in range(1, chips - 2):
         chain.tick(step)
     make(1, shards // 2, shards)
-    if plane:
-        reduces[1].first()
+    for made in inputs[1:]:
+        made.wait()
     make(2, 0, shards)
+    store_down = pltpu.make_async_copy(down_blocks, down_out, down_sem)
+    store_down.start()
+    chain.tick(chips - 2)
     if plane:
         reduces[0].second()
-    chain.tick(chips - 2)
+    pl.loop(0, shards // 2)(shared_block)
+    if plane:
+        reduces[1].second()
+    pl.loop(shards // 2, shards)(shared_block)
     for made in dots:
         made.wait()
     for k in range(TOP):
@@ -980,29 +1013,56 @@
             jnp.where(route_ref[pl.ds(k, 1), :] == e, dots_got[e], 0.0) for e in range(group)
         )
     if plane:
-        reduces[1].second()
         for turn in range(2):
             gate_out[pl.ds(turn * reduces[0].half, reduces[0].half), :] = reduces[0].value(turn)
-    sum_ref[...] = dh_ref[...] + chain.value()
+    sum_ref[...] += chain.value()
     chain.sent()
+    shared_settle(shards - 1)
+
+    @pl.loop(0, shards)
+    def _(k):
+        for copy in shared_copies(k)[1]:
+            remote(*copy).wait_recv()
+
     if plane:
         for turn in range(2):
             up_out[pl.ds(turn * reduces[1].half, reduces[1].half), :] = reduces[1].value(turn)
         for reduce in reduces:
             reduce.sent()
-
-
-def weights(rows, grad_rows, shared_back, dots, route_rows, hidden, gate_grad, up_grad, back_part, ident):
+    store_down.wait()
+
+
+def weights(dots, route_rows, rows, grad_rows, h2, cot_low, hidden, gate_grad, up_grad, back_part, shared, ident):
     chips, length, width = back_part.shape
     shards = lax.axis_size("shard")
     plane = shards == 4
     count, hidden_width = hidden.shape
-    block = hidden_width // shards
+    block, part = hidden_width // shards, shared[0].shape[1]
     vmem, anywhere = pl.BlockSpec(memory_space=pltpu.VMEM), pl.BlockSpec(memory_space=pl.ANY)
     shape, dma = jax.ShapeDtypeStruct, pltpu.SemaphoreType.DMA
     wide = (shards, width, block)
-    scratch = [pltpu.VMEM((2, count, block), BF16)] + ChainReduce.scratch((chips, length, width))
-    scratch += [pltpu.VMEM(dots.shape, F32)]
+    scratch = [
+        pltpu.VMEM((count, width), BF16),
+        pltpu.VMEM((count, width), BF16),
+        pltpu.VMEM((length, width), BF16),
+        pltpu.VMEM((length, width), BF16),
+        pltpu.VMEM((shards, block, width), BF16),
+        dma((4,)),
+        dma,
+        pltpu.VMEM((2, width, part), BF16),
+        pltpu.VMEM((2, width, part), BF16),
+        pltpu.VMEM((2, part, width), BF16),
+        pltpu.VMEM((width, part), BF16),
+        pltpu.VMEM((width, part), BF16),
+        pltpu.VMEM((part, width), BF16),
+        dma((2, 3)),
+        dma((3,)),
+        dma((3,)),
+        dma((3, shards)),
+        pltpu.VMEM((2, count, block), BF16),
+        *ChainReduce.scratch((chips, length, width)),
+        pltpu.VMEM(dots.shape, F32),
+    ]
     scratch += [dma, dma((2,)), dma((2 * chips - 1,)), dma((2 * chips - 1,)), dma((2 * chips,)), dma((2 * chips,))]
     if plane:
         out_shape = [shape((width, block), F32)] * 2
@@ -1010,17 +1070,19 @@
         scratch += ([pltpu.VMEM(wide, BF16)] + PlaneReduce.scratch(wide)) * 2
     else:
         out_shape = [shape(wide, BF16)] * 2
-    out_shape += [shape((shards, block, width), BF16), shape((length, width), F32), shape((TOP, length), F32)]
+    halves = [shape((shards, width // 2, part), BF16)] * 2 + [shape((shards, part // 2, width), BF16)]
+    out_shape = [shape((shards, block, width), BF16), *halves, *halves, *out_shape]
+    out_shape += [shape((length, width), F32)] * 2 + [shape((TOP, length), F32)]
     return pl.pallas_call(
         functools.partial(weights_kernel, plane=plane, chips=chips, shards=shards),
         out_shape=out_shape,
-        in_specs=[vmem] * 5 + [anywhere] * 4,
-        out_specs=[vmem] * 5,
+        in_specs=[vmem] * 2 + [anywhere] * 11,
+        out_specs=[anywhere] * 7 + [vmem] * 5,
         scratch_shapes=scratch,
         compiler_params=pltpu.CompilerParams(
             collective_id=ident, has_side_effects=True, vmem_limit_bytes=VMEM_BYTES
         ),
-    )(rows, grad_rows, shared_back, dots, route_rows, hidden, gate_grad, up_grad, back_part)
+    )(dots, route_rows, rows, grad_rows, h2, cot_low, hidden, gate_grad, up_grad, back_part, *shared)
 
 
 def norm_back(source, inverse, gain, grad_in):
@@ -1033,66 +1095,100 @@
 
 
 def rear_kernel(*refs, plane, chips, shards):
-    (prefix, x_ref, cot_ref, resid_ref, dh_ref, gains_ref, rot_ref, att_ref, h1_ref, lse_ref), refs = refs[:10], refs[10:]
-    (qkv_ref, out_ref, cos_ref, sin_ref, mix_hbm), refs = refs[:5], refs[5:]
+    (prefix, gains_ref, cos_ref, sin_ref), sources, refs = refs[:4], refs[4:15], refs[15:]
     halves, refs = (refs[:6], refs[6:]) if plane else ([], refs)
-    (mix_out, input_grad_ref, qkv_grad_ref, out_grad_ref), refs = refs[:4], refs[4:]
-    pieces, refs = (refs[:3], refs[3:]) if plane else ([], refs)
-    (bias_ref, dres_ref, datt_ref, dqkv_ref, own, from_left, from_right), refs = refs[:7], refs[7:]
-    (own_sem, chain_send, chain_recv), refs = refs[:3], refs[3:]
+    (mix_out, input_grad_out, qkv_grad_out, gain_out), refs = refs[:4], refs[4:]
+    pieces, refs = (refs[:4], refs[4:]) if plane else (refs[:1], refs[1:])
+    held, refs = refs[:11], refs[11:]
+    own, resid_ref, dh_ref, cot_ref, out_ref, att_ref, rot_ref, lse_ref, h1_ref, qkv_ref, x_ref = held
+    (bias_ref, dres_ref, datt_ref, dqkv_ref, qkv_grad_ref, out_grad_ref, from_left, from_right), refs = refs[:8], refs[8:]
+    (load_sem, store_sem, chain_send, chain_recv), refs = refs[:4], refs[4:]
     length, width = x_ref.shape
     at = place()
-    load = pltpu.make_async_copy(mix_hbm, own, own_sem)
-    load.start()
+    core = at["core"]
+    loads = [pltpu.make_async_copy(a, b, load_sem.at[k]) for k, (a, b) in enumerate(zip(sources, held))]
+    loads[0].start()
     reduces = []
     if plane:
-        send, recv, half_sem = refs[:3]
-        work = [refs[3 + 5 * k : 8 + 5 * k] for k in range(3)]
-        loads = [
+        (send, recv, half_sem, core_send, core_recv), work = refs[:5], refs[5:]
+        work = [work[5 * k : 5 * k + 5] for k in range(4)]
+        half_loads = [
             [pltpu.make_async_copy(halves[2 * k + n], work[k][n], half_sem.at[k, n]) for n in range(2)]
             for k in range(3)
         ]
-        for two in loads:
+        for two in half_loads:
             for made in two:
                 made.start()
-        reduces = [PlaneReduce(work[k][0], *work[k][2:], send.at[k], recv.at[k], at) for k in range(3)]
-    chain_meet(at, chips, [at["dev_x"], at["dev_y"]] if plane else [])
+        reduces = [PlaneReduce(work[k][0], *work[k][2:], send.at[k], recv.at[k], at) for k in range(4)]
+        count = work[3][0].shape[1]
+        swaps = [
+            remote(
+                out_grad_ref.at[k, pl.ds(pl.multiple_of((1 - core) * count, 16), count), :],
+                work[3][1].at[k],
+                core_send.at[k],
+                core_recv.at[k],
+                at["dev_c"],
+            )
+            for k in range(shards)
+        ]
+    for made in loads[1:]:
+        made.start()
+    chain_meet(at, chips, [at["dev_x"], at["dev_y"], at["dev_c"]] if plane else [])
     chain = ChainReduce(own, from_left, from_right, chain_send, chain_recv, at, chips)
-    load.wait()
+    loads[0].wait()
     chain.tick(0)
-    for k, reduce in enumerate(reduces):
-        for made in loads[k]:
-            made.wait()
-
-        @pl.loop(0, shards)
-        def _(shard):
-            work[k][0][shard] = (
-                work[k][0][shard].astype(F32) + work[k][1][shard].astype(F32)
-            ).astype(BF16)
-
-        reduce.first()
+    for made in loads[1:6]:
+        made.wait()
     resid = resid_ref[...]
     inverse = lax.rsqrt(jnp.mean(resid * resid, axis=-1, keepdims=True) + EPS)
     gain_two_grad, extra = norm_back(resid, inverse, gains_ref[pl.ds(1, 1), :], dh_ref[...])
     dres = cot_ref[...] + extra
     dres_ref[...] = dres
     low_dres = dres.astype(BF16)
-    datt_ref[...] = dot_nt(low_dres, out_ref[...]).astype(BF16)
     out_grad = dot_tn(att_ref[...], low_dres).astype(BF16)
     rows = width // shards
     for k in range(shards):
-        out_grad_ref[k, :rows, :] = out_grad[k * rows : (k + 1) * rows]
+        out_grad_ref[k] = out_grad[k * rows : (k + 1) * rows]
+
+    def add_halves(k):
+        @pl.loop(0, shards)
+        def _(shard):
+            work[k][0][shard] = (
+                work[k][0][shard].astype(F32) + work[k][1][shard].astype(F32)
+            ).astype(BF16)
+
+        reduces[k].first()
+
+    if plane:
+        for made in swaps:
+            made.start()
+        for k in range(3):
+            for made in half_loads[k]:
+                made.wait()
+            add_halves(k)
+        for k in range(shards):
+            work[3][0][k] = out_grad_ref[k, pl.ds(pl.multiple_of(core * count, 16), count), :]
+        for made in swaps:
+            made.wait()
+        add_halves(3)
+    else:
+        store_out = pltpu.make_async_copy(out_grad_ref, pieces[0], store_sem.at[3])
+        store_out.start()
+    datt_ref[...] = dot_nt(low_dres, out_ref[...]).astype(BF16)
     set_bias(bias_ref, prefix)
     scale = HEAD_DIM**-0.5
-    count = length // 2
+    for made in loads[6:]:
+        made.wait()
+
+    block = length // 2
 
     def pair(j):
         queries, keys, values = (
             rot_ref[:, columns(part * width + j * 128, 128)] for part in range(3)
         )
         grads = datt_ref[:, columns(j * 128, 128)]
-        low = lax.broadcasted_iota(jnp.int32, (count, 128), 1) < HEAD_DIM
-        lanes = lax.broadcasted_iota(jnp.int32, (count, 128), 1)
+        low = lax.broadcasted_iota(jnp.int32, (block, 128), 1) < HEAD_DIM
+        lanes = lax.broadcasted_iota(jnp.int32, (block, 128), 1)
 
         def keep(part, rows, value):
             if part < 2:
@@ -1100,8 +1196,8 @@
             dqkv_ref[rows, columns(part * width + j * 128, 128)] = value.astype(BF16)
 
         sums = []
-        for start in range(0, length, count):
-            rows, seen = pl.ds(start, count), start + count
+        for start in range(0, length, block):
+            rows, seen = pl.ds(start, block), start + block
             query = two_heads(queries[start:seen] * scale)
             grad = two_heads(grads[start:seen])
             bias, lse = bias_ref[rows, :seen], lse_ref[rows, :]
@@ -1113,51 +1209,59 @@
                 axis=0,
             )
             scores = dot_nt(query, keys[:seen])
-            scores = jnp.concatenate([scores[:count] + bias, scores[count:] + bias], axis=0)
+            scores = jnp.concatenate([scores[:block] + bias, scores[block:] + bias], axis=0)
             probs = jnp.exp(scores - logsum)
             probs_grad = dot_nt(grad, values[:seen])
             inner = jnp.sum(probs * probs_grad, axis=-1, keepdims=True)
             score_grad = (probs * (probs_grad - inner)).astype(BF16)
             query_grad = dot_nn(score_grad, keys[:seen]) * scale
-            keep(0, rows, jnp.where(low, query_grad[:count], query_grad[count:]))
+            keep(0, rows, jnp.where(low, query_grad[:block], query_grad[block:]))
             sums.append((dot_tn(score_grad, query), dot_tn(probs.astype(BF16), grad)))
         for part in range(2):
-            keep(1 + part, pl.ds(0, count), sums[0][part] + sums[1][part][:count])
-            keep(1 + part, pl.ds(count, count), sums[1][part][count:])
+            keep(1 + part, pl.ds(0, block), sums[0][part] + sums[1][part][:block])
+            keep(1 + part, pl.ds(block, block), sums[1][part][block:])
 
     pairs = width // 128
-    pl.loop(0, pairs // 2)(pair)
+    pl.loop(0, pairs // 3)(pair)
     for step in range(1, chips - 2):
         chain.tick(step)
-    pl.loop(pairs // 2, pairs)(pair)
-    for reduce in reduces[:2]:
-        reduce.second()
-    chain.tick(chips - 2)
+    pl.loop(pairs // 3, pairs)(pair)
 
     @pl.loop(0, 3 * width // 256)
     def _(k):
         cols = columns(k * 256, 256)
         qkv_grad_ref[:, cols] = dot_tn(h1_ref[...], dqkv_ref[:, cols]).astype(BF16)
 
-    for reduce in reduces[2:]:
+    stores = [pltpu.make_async_copy(qkv_grad_ref, qkv_grad_out, store_sem.at[0])]
+    stores[0].start()
+    chain.tick(chips - 2)
+    for reduce in reduces:
         reduce.second()
     dh1 = dot_nt(dqkv_ref[...], qkv_ref[...])
     x = x_ref[...]
     inverse = lax.rsqrt(jnp.mean(x * x, axis=-1, keepdims=True) + EPS)
     gain_one_grad, extra = norm_back(x, inverse, gains_ref[pl.ds(0, 1), :], dh1)
-    input_grad_ref[...] = dres_ref[...] + extra
-    index = lax.broadcasted_iota(jnp.int32, (64, width), 0)
+    dres_ref[...] += extra
+    stores.append(pltpu.make_async_copy(dres_ref, input_grad_out, store_sem.at[1]))
+    stores[1].start()
+    index = lax.broadcasted_iota(jnp.int32, gain_out.shape[1:], 0)
     gain_rows = jnp.where(index == 0, gain_one_grad, jnp.where(index == 1, gain_two_grad, 0.0)).astype(BF16)
     for k in range(shards):
-        out_grad_ref[k, rows:, :] = gain_rows
+        gain_out[k] = gain_rows
     for reduce, piece in zip(reduces, pieces):
         count = piece.shape[1]
         both = jnp.concatenate([reduce.value(0), reduce.value(1)], axis=0)
         for k in range(chips):
             piece[k] = both[k * count : (k + 1) * count].astype(BF16)
         reduce.sent()
-    mix_out[...] = chain.value()
+    resid_ref[...] = chain.value()
+    stores.append(pltpu.make_async_copy(resid_ref, mix_out, store_sem.at[2]))
+    stores[2].start()
     chain.sent()
+    if not plane:
+        stores.append(store_out)
+    for made in stores:
+        made.wait()
 
 
 def rear(prefix, inputs, cotangent, resid, dh2, gains, kept, full, mix_part, halves, ident):
@@ -1165,38 +1269,51 @@
     chips, shards = mix_part.shape[0], lax.axis_size("shard")
     plane = shards == 4
     cosine, sine = rope_lanes(length)
+    turned, attended, normed_one, logsum = kept
     vmem, anywhere = pl.BlockSpec(memory_space=pltpu.VMEM), pl.BlockSpec(memory_space=pl.ANY)
     shape, dma = jax.ShapeDtypeStruct, pltpu.SemaphoreType.DMA
-    operands = [prefix, inputs, cotangent, resid, dh2, gains, *kept, *full, cosine, sine, mix_part]
-    in_specs = [pl.BlockSpec(memory_space=pltpu.SMEM)] + [vmem] * 13 + [anywhere]
+    sources = [mix_part, resid, dh2, cotangent, full[1], attended, turned, logsum, normed_one, full[0], inputs]
+    operands = [prefix, gains, cosine, sine, *sources]
+    in_specs = [pl.BlockSpec(memory_space=pltpu.SMEM)] + [vmem] * 3 + [anywhere] * 11
+    out_blocks = (shards, width // shards, width)
     out_shape = [
         shape((length, width), F32),
         shape((length, width), F32),
         shape((width, 3 * width), BF16),
-        shape((shards, width // shards + 64, width), BF16),
+        shape((shards, 64, width), BF16),
     ]
-    scratch = [
+    out_specs = [anywhere] * 3 + [vmem]
+    scratch = [pltpu.VMEM(v.shape, v.dtype) for v in sources]
+    scratch += [
         pltpu.VMEM((length, length), F32),
         pltpu.VMEM((length, width), F32),
         pltpu.VMEM((length, width), BF16),
         pltpu.VMEM((length, 3 * width), BF16),
-        *ChainReduce.scratch((chips, length, width)),
-        dma,
+        pltpu.VMEM((width, 3 * width), BF16),
+        pltpu.VMEM(out_blocks, BF16),
+        *ChainReduce.scratch((chips, length, width))[:2],
+        dma((11,)),
+        dma((4,)),
         dma((2 * chips,)),
         dma((2 * chips,)),
     ]
     if plane:
         operands += halves
         in_specs += [anywhere] * 6
-        scratch += [dma((3, PlaneReduce.COPIES))] * 2 + [dma((3, 2))]
-        for half in halves[::2]:
-            out_shape.append(shape((chips, half.shape[1] // chips, half.shape[2]), BF16))
-            scratch += [pltpu.VMEM(half.shape, BF16)] * 2 + PlaneReduce.scratch(half.shape)
+        out_specs += [vmem] * 4
+        scratch += [dma((4, PlaneReduce.COPIES))] * 2 + [dma((3, 2))] + [dma((shards,))] * 2
+        half_shapes = [v.shape for v in halves[::2]] + [(shards, out_blocks[1] // 2, width)]
+        for s in half_shapes:
+            out_shape.append(shape((chips, s[1] // chips, s[2]), BF16))
+            scratch += [pltpu.VMEM(s, BF16)] * 2 + PlaneReduce.scratch(s)
+    else:
+        out_shape.append(shape(out_blocks, BF16))
+        out_specs.append(anywhere)
     return pl.pallas_call(
         functools.partial(rear_kernel, plane=plane, chips=chips, shards=shards),
         out_shape=out_shape,
         in_specs=in_specs,
-        out_specs=[vmem] * len(out_shape),
+        out_specs=out_specs,
         scratch_shapes=scratch,
         compiler_params=pltpu.CompilerParams(
             collective_id=ident, has_side_effects=True, vmem_limit_bytes=VMEM_BYTES
@@ -1205,11 +1322,11 @@
 
 
 def last_kernel(*refs, chips, shards):
-    (attention, pieces, down_hbm), refs = (refs[:2], refs[2:5], refs[5]), refs[6:]
-    alls_out, down_out, refs = refs[:5], refs[5], refs[6:]
+    (attention, pieces, down_hbm), refs = (refs[:2], refs[2:6], refs[6]), refs[7:]
+    alls_out, down_out, refs = refs[:6], refs[6], refs[7:]
     halves, refs = [refs[3 * k : 3 * k + 3] for k in range(2)], refs[6:]
     plane_work, refs = refs[:10], refs[10:]
-    chain_work, refs = [refs[4 * k : 4 * k + 4] for k in range(5)], refs[20:]
+    chain_work, refs = [refs[4 * k : 4 * k + 4] for k in range(6)], refs[24:]
     load_sem, core_send, core_recv, plane_send, plane_recv, sums_send, sums_recv, all_send, all_recv, all_local = refs
     at = place()
     core = at["core"]
@@ -1220,22 +1337,22 @@
             part = attention[k].at[:, pl.ds(pl.multiple_of(c * rows, 16), rows), :]
             loads.append(pltpu.make_async_copy(part, halves[k][n], load_sem.at[2 * k + n]))
         swaps.append(remote(halves[k][1], halves[k][2], core_send.at[k], core_recv.at[k], at["dev_c"]))
-    loads += [pltpu.make_async_copy(pieces[k], chain_work[2 + k][0], load_sem.at[4 + k]) for k in range(3)]
-    loads.append(pltpu.make_async_copy(down_hbm, plane_work[0], load_sem.at[7]))
+    loads += [pltpu.make_async_copy(pieces[k], chain_work[2 + k][0], load_sem.at[4 + k]) for k in range(4)]
+    loads.append(pltpu.make_async_copy(down_hbm, plane_work[0], load_sem.at[8]))
     for made in loads:
         made.start()
     sums = [
-        ChainReduce(*chain_work[k][:3], sums_send.at[k], sums_recv.at[k], at, chips) for k in range(5)
+        ChainReduce(*chain_work[k][:3], sums_send.at[k], sums_recv.at[k], at, chips) for k in range(6)
     ]
     alls = [
         ChainGather(chain_work[k][3], alls_out[k], all_send.at[k], all_recv.at[k], all_local.at[k], at, chips)
-        for k in range(5)
+        for k in range(6)
     ]
     planes = [
         PlaneReduce(src, *plane_work[1 + 3 * k : 4 + 3 * k], plane_send.at[k], plane_recv.at[k], at)
         for k, src in enumerate([plane_work[0], halves[0][0], halves[1][0]])
     ]
-    shared, attn = (2, 3, 4), (0, 1)
+    shared, attn = (2, 3, 4, 5), (0, 1)
     chain_meet(at, chips, [at["dev_x"], at["dev_y"], at["dev_c"]])
     for k in attn:
         loads[2 * k].wait()
@@ -1255,7 +1372,7 @@
             chain_work[k][3][...] = sums[k].value().astype(BF16)
             alls[k].start()
 
-    for k in range(4, 8):
+    for k in range(4, 9):
         loads[k].wait()
     tick(shared, 0)
     for k in attn:
@@ -1299,11 +1416,11 @@
         reduce.sent()
 
 
-def last(qkv_grad, out_grad, pieces, down_blocks, ident):
+def last(qkv_grad, gain_grads, pieces, down_blocks, ident):
     shards, chips = lax.axis_size("shard"), lax.axis_size("expert") // 2
     vmem, anywhere = pl.BlockSpec(memory_space=pltpu.VMEM), pl.BlockSpec(memory_space=pl.ANY)
     shape, dma = jax.ShapeDtypeStruct, pltpu.SemaphoreType.DMA
-    attention = [qkv_grad, out_grad]
+    attention = [qkv_grad, gain_grads]
     half_shapes = [(shards, v.shape[1] // 2, v.shape[2]) for v in attention]
     chain_shapes = [(chips, v.shape[1] // 2 // chips, v.shape[2]) for v in attention] + [v.shape for v in pieces]
     out_shape = [shape((2 * chips,) + s[1:], BF16) for s in chain_shapes]
@@ -1317,75 +1434,75 @@
     for s in chain_shapes:
         scratch += ChainReduce.scratch(s) + [pltpu.VMEM(s[1:], BF16)]
     scratch += [
-        dma((8,)),
+        dma((9,)),
         dma((2,)),
         dma((2,)),
         dma((3, PlaneReduce.COPIES)),
         dma((3, PlaneReduce.COPIES)),
-        dma((5, 2 * chips)),
-        dma((5, 2 * chips)),
-        dma((5, ChainGather.copies(chips))),
-        dma((5, ChainGather.copies(chips))),
-        dma((5,)),
+        dma((6, 2 * chips)),
+        dma((6, 2 * chips)),
+        dma((6, ChainGather.copies(chips))),
+        dma((6, ChainGather.copies(chips))),
+        dma((6,)),
     ]
     return pl.pallas_call(
         functools.partial(last_kernel, chips=chips, shards=shards),
         out_shape=out_shape,
-        in_specs=[anywhere] * 6,
-        out_specs=[vmem] * 6,
+        in_specs=[anywhere] * 7,
+        out_specs=[vmem] * 7,
         scratch_shapes=scratch,
         compiler_params=pltpu.CompilerParams(
             collective_id=ident, has_side_effects=True, vmem_limit_bytes=VMEM_BYTES
         ),
-    )(qkv_grad, out_grad, *pieces, down_blocks)
-
-
-def finish_kernel(*refs, chips):
-    (summands, sums, plain), refs = (refs[:3], refs[3:8], refs[8:12]), refs[12:]
-    (output, grads, plain_out), refs = (refs[0], refs[1:6], refs[6:10]), refs[10:]
-    (add_in, sum_in, plain_in, add_out, sum_out), (load_sem, store_sem) = (
-        (refs[:3], refs[3:8], refs[8:12], refs[12], refs[13:18]),
-        refs[18:],
-    )
-    held = [*plain_in, *sum_in, *add_in]
-    loads = [
-        pltpu.make_async_copy(a, b, load_sem.at[k]) for k, (a, b) in enumerate(zip([*plain, *sums, *summands], held))
+    )(qkv_grad, gain_grads, *pieces, down_blocks)
+
+
+def finish_kernel(*refs, chips, counts):
+    total, results = sum(counts), sum(counts[:2]) + 1
+    inputs, outputs, refs = refs[:total], refs[total : total + results], refs[total + results :]
+    held, made, (load_sem, store_sem) = refs[:total], refs[total:-2], refs[-2:]
+    plain, sums = counts[:2]
+    loads = [pltpu.make_async_copy(a, b, load_sem.at[k]) for k, (a, b) in enumerate(zip(inputs, held))]
+    ready = [*held[:plain], *made]
+    stores = [
+        pltpu.make_async_copy(a, b, store_sem.at[k]) for k, (a, b) in enumerate(zip(ready, outputs))
     ]
-    stores = [
-        pltpu.make_async_copy(a, b, store_sem.at[k])
-        for k, (a, b) in enumerate(zip([*plain_in, *sum_out, add_out], [*plain_out, *grads, output]))
-    ]
-    for made in loads:
-        made.start()
-    for k in range(4):
+    for copy in loads:
+        copy.start()
+    for k in range(plain):
         loads[k].wait()
         stores[k].start()
-    for k in range(5):
-        loads[4 + k].wait()
-        count = sum_in[k].shape[1]
-        for n in range(chips):
-            for c in range(2):
-                sum_out[k][pl.ds((c * chips + n) * count, count), :] = sum_in[k][2 * n + c].astype(F32)
-        stores[4 + k].start()
-    for made in loads[9:]:
-        made.wait()
-    add_out[...] = add_in[0][...] + add_in[1][...] + add_in[2][...]
-    stores[9].start()
-    for made in stores:
-        made.wait()
-
-
-def finish(summands, sums, plain):
+    for k in range(plain, plain + sums):
+        loads[k].wait()
+        count = held[k].shape[1]
+        if ready[k].shape[0] == count:
+            ready[k][...] = held[k][0].astype(F32)
+        else:
+            for n in range(chips):
+                for c in range(2):
+                    ready[k][pl.ds((c * chips + n) * count, count), :] = held[k][2 * n + c].astype(F32)
+        stores[k].start()
+    for copy in loads[plain + sums :]:
+        copy.wait()
+    ready[-1][...] = sum(v[...] for v in held[plain + sums :])
+    for copy in stores[plain + sums :]:
+        copy.start()
+    for copy in stores:
+        copy.wait()
+
+
+def finish(plain, sums, summands):
     chips = sums[0].shape[0] // 2
     shape, dma = jax.ShapeDtypeStruct, pltpu.SemaphoreType.DMA
     anywhere = pl.BlockSpec(memory_space=pl.ANY)
-    inputs = [*summands, *sums, *plain]
-    out_shape = [shape(summands[0].shape, F32)]
-    out_shape += [shape((v.shape[0] * v.shape[1], v.shape[2]), F32) for v in sums]
-    scratch = [pltpu.VMEM(v.shape, v.dtype) for v in inputs] + [pltpu.VMEM(s.shape, F32) for s in out_shape]
-    out_shape += [shape(v.shape, F32) for v in plain]
+    inputs = [*plain, *sums, *summands]
+    made = [shape(sums[0].shape[1:], F32)]
+    made += [shape((v.shape[0] * v.shape[1], v.shape[2]), F32) for v in sums[1:]]
+    made.append(shape(summands[0].shape, F32))
+    out_shape = [shape(v.shape, F32) for v in plain] + made
+    scratch = [pltpu.VMEM(v.shape, v.dtype) for v in inputs] + [pltpu.VMEM(s.shape, F32) for s in made]
     return pl.pallas_call(
-        functools.partial(finish_kernel, chips=chips),
+        functools.partial(finish_kernel, chips=chips, counts=(len(plain), len(sums), len(summands))),
         out_shape=out_shape,
         in_specs=[anywhere] * len(inputs),
         out_specs=[anywhere] * len(out_shape),
@@ -1421,10 +1538,10 @@
         normed_one,
         turned,
         attended,
-        logsum,
         resid,
         normed_two,
         cot_low,
+        logsum,
         gains,
         qkv_full,
         out_full,
@@ -1449,27 +1566,27 @@
         up_pre_grad,
         mix_part,
         back_part,
-        *shared_halves,
         weight_back,
-        shared_out,
-        shared_back,
-    ) = middle(
-        normed_two,
-        cot_low,
-        table_all,
-        cot_all,
-        [expert_gate, expert_up, expert_down],
-        [gate_blocks, up_blocks, down_full],
-        2,
-    )
-    shared_halves = [shared_halves[k + n] for k in range(3) for n in (0, 3)]
+    ) = middle(normed_two, table_all, cot_all, [expert_gate, expert_up, expert_down], 2)
     rows, grad_rows, hidden, gate_pre_grad, up_pre_grad = (
         v.reshape(-1, v.shape[-1]) for v in (rows, grad_rows, hidden, gate_pre_grad, up_pre_grad)
     )
-    gate_term, up_term, down_term, normed_two_grad, gate_weights_grad = weights(
-        rows, grad_rows, shared_back, weight_back, route_rows, hidden, gate_pre_grad, up_pre_grad, back_part, 3
+    down_term, *shared_halves, gate_term, up_term, normed_two_grad, shared_out, gate_weights_grad = weights(
+        weight_back,
+        route_rows,
+        rows,
+        grad_rows,
+        normed_two,
+        cot_low,
+        hidden,
+        gate_pre_grad,
+        up_pre_grad,
+        back_part,
+        [gate_blocks, up_blocks, down_full],
+        3,
     )
-    mixture, input_grad, qkv_grad, out_grad, *pieces = rear(
+    shared_halves = [shared_halves[k + n] for k in range(3) for n in (0, 3)]
+    mixture, input_grad, qkv_grad, gain_grads, *pieces = rear(
         prefix,
         inputs,
         cotangent,
@@ -1484,9 +1601,9 @@
     )
     qkv_grad = qkv_grad.reshape(shards, width // shards, 3 * width)
     if shards == 4:
-        *sums, down_term = last(qkv_grad, out_grad, pieces, down_term, 5)
-        output, qkv_sum, out_sum, *shared_sums, input_grad, gate_term, up_term, down_term = finish(
-            [resid, mixture, shared_out], sums, [input_grad, gate_term, up_term, down_term]
+        qkv_sum, gain_sums, *pieces, down_term = last(qkv_grad, gain_grads, pieces, down_term, 5)
+        input_grad, gate_term, up_term, down_term, gain_sums, qkv_sum, *shared_sums, out_sum, output = finish(
+            [input_grad, gate_term, up_term, down_term], [gain_sums, qkv_sum, *pieces], [resid, mixture, shared_out]
         )
     else:
 
@@ -1500,21 +1617,21 @@
         gate_term, up_term, down_term = (
             over_plane(v).astype(F32) for v in (gate_term, up_term, down_term)
         )
-        qkv_sum, out_sum = over_all(qkv_grad), over_all(out_grad)
+        qkv_sum, gain_sums, out_sum = over_all(qkv_grad), over_all(gain_grads), over_all(pieces[0])
         shared_sums = []
         for own, got in zip(shared_halves[::2], shared_halves[1::2]):
             half = (own.astype(F32) + got.astype(F32)).astype(BF16)
             both = jnp.concatenate([jnp.where(me % 2 == c, half, 0) for c in range(2)], axis=1)
             shared_sums.append(over_all(both))
     part = width // shards
-    gain_grads = lax.dynamic_slice(out_sum[part : part + 2], (0, shard * part), (2, part))
+    gain_sums = lax.dynamic_slice(gain_sums[:2], (0, shard * part), (2, part))
     return (
         output,
         input_grad,
-        gain_grads[0],
+        gain_sums[0],
         qkv_sum,
-        out_sum[:part],
-        gain_grads[1],
+        out_sum,
+        gain_sums[1],
         *shared_sums,
         gate_term[None],
         up_term[None],

time: 414 us -> 369 us (0.89)
  Pallas kernels: 402 us -> 358 us
    pallas_call x2, Pallas kernels: 113 us -> 96.1 us  [the longest x1 84.6 us: middle(): pl.pallas_call(functools.partial(middle_kernel, chips=chips, capacity=cap...]
    pallas_call x1, Pallas kernels: 86.1 us -> 70.9 us  [front(): pl.pallas_call(functools.partial(front_kernel, plane=plane, chips=chips),...]
    pallas_call x1, Pallas kernels: 70.6 us -> 64.1 us  [weights(): pl.pallas_call(functools.partial(weights_kernel, plane=plane, chips=chips...]
    pallas_call x1, Pallas kernels: 67.6 us -> 63.4 us  [rear(): pl.pallas_call(functools.partial(rear_kernel, plane=plane, chips=chips, s...]
where the time goes in v5:
time: 369 us; the launch traced here: 365 us
  Pallas kernels  358 us (97%)
  local copies, waits for them, and re-layouts  4.42 us (1%)
    pallas_call x1, Pallas kernels, middle(): pl.pallas_call(functools.partial(middle_kernel, chips=chips, capacity=cap...  84.6 us
    pallas_call x1, Pallas kernels, front(): pl.pallas_call(functools.partial(front_kernel, plane=plane, chips=chips),...  70.9 us
    pallas_call x1, Pallas kernels, weights(): pl.pallas_call(functools.partial(weights_kernel, plane=plane, chips=chips...  64.1 us
    pallas_call x1, Pallas kernels, last(): pl.pallas_call(functools.partial(last_kernel, chips=chips, shards=shards)...  63.9 us
    pallas_call x1, Pallas kernels, rear(): pl.pallas_call(functools.partial(rear_kernel, plane=plane, chips=chips, s...  63.4 us
    pallas_call x1, Pallas kernels, finish(): pl.pallas_call(functools.partial(finish_kernel, chips=chips, counts=(len(...  11.5 us

profile of v5, /device:TPU:0, one launch (start us, length us, event | category | flops | bytes accessed | tf_op | source)
XLA Modules:
  0.0 364.7 jit_solution(13435175958596028241)
XLA Ops:
  1.3 1.2 reshape.50.refs_7_
  2.5 1.2 reshape.51.refs_8_
  3.7 70.9 %shard_map.282 = (bf16[8,512,768]{2,1,0:T(8,128)(2,1)}, f32[8,16,512]{2,1,0:T(8,128)}, bf16[512,768]{1,0:T(8,128)(2,1)}, bf16[512,2304]{1,0:T(8,128)(2,1)}, bf16...) custom-call(s32[1]{0:T(128)S(6)} %copy.33.refs_0_, ...), custom_call_target="tpu_custom_call" | custom-call | tf_op jit(solution)/shard_map/pallas_call | solution.py:469
  74.7 84.6 %shard_map.283 = (bf16[4,512,768]{2,1,0:T(8,128)(2,1)}, bf16[4,512,768]{2,1,0:T(8,128)(2,1)}, bf16[4,512,2048]{2,1,0:T(8,128)(2,1)}, bf16[4,512,2048]{2,1,0:T(8,...) custom-call(bf16[512,768]{1,0:T(8,128)(2,1)} %get-tuple-element.75.r, ...), custom_call_target="tpu_custom_call" | custom-call | tf_op jit(solution)/shard_map/pallas_call | solution.py:723
  159.3 64.1 %shard_map.284 = (bf16[4,512,768]{2,1,0:T(8,128)(2,1)}, bf16[4,384,512]{2,1,0:T(8,128)(2,1)}, bf16[4,384,512]{2,1,0:T(8,128)(2,1)}, bf16[4,256,768]{2,1,0:T(8,12...) custom-call(f32[8,1,512]{2,1,0:T(1,128)} %get-tuple-element.80.refs_, ...), custom_call_target="tpu_custom_call" | custom-call | tf_op jit(solution)/shard_map/pallas_call | solution.py:1076
  223.4 63.4 %shard_map.285 = (f32[512,768]{1,0:T(8,128)}, f32[512,768]{1,0:T(8,128)}, bf16[768,2304]{1,0:T(8,128)(2,1)}, bf16[4,64,768]{2,1,0:T(8,128)(2,1)}, bf16[4,96,512]...) custom-call(s32[1]{0:T(128)S(6)} %copy.33.refs_0_, ...), custom_call_target="tpu_custom_call" | custom-call | tf_op jit(solution)/shard_map/pallas_call | solution.py:1312
  286.8 63.9 %shard_map.286 = (bf16[8,24,2304]{2,1,0:T(8,128)(2,1)}, bf16[8,8,768]{2,1,0:T(8,128)(2,1)}, bf16[8,96,512]{2,1,0:T(8,128)(2,1)}, bf16[8,96,512]{2,1,0:T(8,128)(2...) custom-call(bf16[4,192,2304]{2,1,0:T(8,128)(2,1)} %bitcast.17, ...), custom_call_target="tpu_custom_call" | custom-call | tf_op jit(solution)/shard_map/pallas_call | solution.py:1448
  350.7 0.0 copy-start
  350.7 11.5 %shard_map.287 = (f32[512,768]{1,0:T(8,128)}, f32[768,512]{1,0:T(8,128)}, f32[768,512]{1,0:T(8,128)}, f32[512,768]{1,0:T(8,128)}, f32[8,768]{1,0:T(8,128)}, /*in...) custom-call(f32[512,768]{1,0:T(8,128)} %get-tuple-element.104.refs_0, ...), custom_call_target="tpu_custom_call" | custom-call | tf_op jit(solution)/shard_map/pallas_call | solution.py:1504
  362.3 0.7 slice.9
  363.0 0.6 fusion
  363.6 0.0 copy-done
  363.6 0.6 copy.34
Async XLA Ops:
  350.7 12.9 %copy-start = (f32[2,512]{1,0:T(2,128)S(1)}, f32[2,512]{1,0:T(2,128)}, u32[]{:S(2)}) copy-start(f32[2,512]{1,0:T(2,128)} %get-tuple-element.134) | copy-start | bytes 12292

commit v6 on v5

--- a/solution.py
+++ b/solution.py
@@ -62,43 +62,48 @@
     def view(self, shard, start, count):
         return self.dst.at[pl.ds(pl.multiple_of(shard * self.rows + start, 16), count), :]
 
-    def copy(self, part, index, device):
-        made = remote(part, part, self.send.at[index], self.recv.at[index], device)
-        made.start()
-        self.copies.append(made)
-
-    def load(self):
-        self.own = pltpu.make_async_copy(self.src, self.view(self.at["shard"], 0, self.rows), self.local)
-        self.own.start()
-
-    def first(self):
-        at, half = self.at, self.rows // 2
-        self.own.wait()
-        part = self.view(at["shard"], at["core"] * half, half)
-        self.copy(part, 0, at["dev_x"])
-        self.copy(part, 1, at["dev_y"])
-
-    def second(self):
+    def copy(self, index):
         at, half, quarter = self.at, self.rows // 2, self.rows // 4
         start = at["core"] * half
-        self.copies[0].wait_recv()
-        self.copy(self.view(at["sx"], start, quarter), 2, at["dev_y"])
-        self.copy(self.view(at["sx"], start, half), 3, at["dev_c"])
-        self.copies[1].wait_recv()
-        self.copy(self.view(at["sy"], start + quarter, quarter), 4, at["dev_x"])
-        self.copy(self.view(at["sy"], start, half), 5, at["dev_c"])
+        shard, low, count, device = (
+            (at["shard"], start, half, at["dev_x"]),
+            (at["shard"], start, half, at["dev_y"]),
+            (at["sx"], start, quarter, at["dev_y"]),
+            (at["sx"], start, half, at["dev_c"]),
+            (at["sy"], start + quarter, quarter, at["dev_x"]),
+            (at["sy"], start, half, at["dev_c"]),
+            (at["sd"], start, half, at["dev_c"]),
+        )[index]
+        part = self.view(shard, low, count)
+        return remote(part, part, self.send.at[index], self.recv.at[index], device)
+
+    def own(self):
+        return pltpu.make_async_copy(self.src, self.view(self.at["shard"], 0, self.rows), self.local)
+
+    def load(self):
+        self.own().start()
+
+    def first(self):
+        self.own().wait()
+        for index in (0, 1):
+            self.copy(index).start()
+
+    def second(self):
+        for index, onward in ((0, (2, 3)), (1, (4, 5))):
+            self.copy(index).wait_recv()
+            for k in onward:
+                self.copy(k).start()
 
     def third(self):
-        at, half = self.at, self.rows // 2
-        self.copies[2].wait_recv()
-        self.copies[4].wait_recv()
-        self.copy(self.view(at["sd"], at["core"] * half, half), 6, at["dev_c"])
+        for index in (2, 4):
+            self.copy(index).wait_recv()
+        self.copy(6).start()
 
     def finish(self):
         for index in (3, 5, 6):
-            self.copies[index].wait_recv()
-        for made in self.copies:
-            made.wait_send()
+            self.copy(index).wait_recv()
+        for index in range(self.COPIES):
+            self.copy(index).wait_send()
 
 
 class ChainGather:
@@ -106,12 +111,17 @@
     def copies(chips):
         return 4 * chips
 
-    def __init__(self, src, dst, send, recv, local, at, chips):
+    def __init__(self, src, dst, send, recv, local, at, chips, rows=None):
         self.src, self.dst, self.send, self.recv, self.local = src, dst, send, recv, local
-        self.at, self.chips = at, chips
+        self.at, self.chips, self.rows = at, chips, rows
+        if rows is not None:
+            self.src = src.at[rows, :]
+
+    def part(self, block):
+        return self.dst.at[block] if self.rows is None else self.dst.at[block, self.rows, :]
 
     def copy(self, block, index, device, first=False):
-        part = self.dst.at[block]
+        part = self.part(block)
         return remote(
             self.src if first else part, part, self.send.at[index], self.recv.at[index], self.at[device]
         )
@@ -143,7 +153,7 @@
         pl.when(at["z"] < self.chips - 1)(lambda: self.right(1).start())
         pl.when(at["z"] > 0)(lambda: self.left(1).start())
         self.over(0).start()
-        self.own = pltpu.make_async_copy(self.src, self.dst.at[at["expert"]], self.local)
+        self.own = pltpu.make_async_copy(self.src, self.part(at["expert"]), self.local)
         self.own.start()
 
     def step(self, step):
@@ -246,25 +256,28 @@
 
 def front_kernel(*refs, plane, chips):
     (prefix, x_ref, cot_ref, route_ref, weight_ref, cos_ref, sin_ref), refs = refs[:7], refs[7:]
-    (one_ref, two_ref), refs = refs[:2], refs[2:]
-    weights, refs = (refs[:5], refs[5:]) if plane else (refs[:2], refs[2:])
+    gains_in, refs = refs[0], refs[1:]
+    gain_pair = gains_in[...].astype(F32)
+    weights, refs = refs[:2], refs[2:]
     (cot_out, table_out, h1_out, rot_out, att_out, resid_out, h2_out, cot_low, lse_ref, gains_ref), refs = refs[:10], refs[10:]
-    full_out, refs = (refs[:5], refs[5:]) if plane else ([], refs)
+    full_out, refs = (refs[:2], refs[2:]) if plane else ([], refs)
     (h1_ref, rot_ref, att_ref, resid_ref, h2_ref, cot_low_ref), refs = refs[:6], refs[6:]
     (bias_ref, table_ref, table_all, cot_all, out_sem, chain_sem, chain_send, chain_recv, chain_local), refs = refs[:9], refs[9:]
     length, width = x_ref.shape
     experts = table_ref.shape[0] // 2
     at = place()
     if plane:
-        gains_src, gains_full, full, (send, recv, local) = refs[0], refs[1], refs[2:7], refs[7:]
+        gains_src, gains_full, full, (send, recv, local) = refs[0], refs[1], refs[2:4], refs[4:]
         gathers = [
             PlaneGather(a, b, send.at[k], recv.at[k], local.at[k], at)
             for k, (a, b) in enumerate(zip([*weights, gains_src], [*full, gains_full]))
         ]
-        first, later = [gathers[5], gathers[1], gathers[0]], gathers[2:5]
-        gains_src[:32, :] = jnp.broadcast_to(one_ref[...], (32, one_ref.shape[1]))
-        gains_src[32:, :] = jnp.broadcast_to(two_ref[...], (32, two_ref.shape[1]))
-        for gather in first + later:
+        first = gathers[::-1]
+        for k in range(2):
+            gains_src[pl.ds(32 * k, 32), :] = jnp.broadcast_to(
+                gain_pair[k : k + 1], (32, gain_pair.shape[1])
+            ).astype(BF16)
+        for gather in first:
             gather.load()
         qkv_full, out_full = full[:2]
     else:
@@ -274,6 +287,20 @@
         for gather in first:
             gather.first()
     cot_low_ref[...] = cot_ref[...].astype(BF16)
+    chains = [
+        ChainGather(a, b, chain_send.at[k], chain_recv.at[k], chain_local.at[k], at, chips)
+        for k, (a, b) in enumerate([(table_ref, table_all)])
+    ]
+    halves = [
+        ChainGather(
+            cot_low_ref, cot_all, chain_send.at[1 + k], chain_recv.at[1 + k], chain_local.at[1 + k], at, chips,
+            pl.ds(k * length // 2, length // 2),
+        )
+        for k in range(2)
+    ]
+    ahead, behind = [*chains, halves[0]], halves[1:]
+    for half in halves:
+        half.start()
     names = lax.broadcasted_iota(jnp.int32, (experts, length), 0)
     chosen = [route_ref[pl.ds(k, 1), :] == names for k in range(TOP)]
     member = (chosen[0] | chosen[1]).astype(F32)
@@ -286,12 +313,8 @@
     table_ref[experts:, :] = sum(
         jnp.where(chosen[k], weight_ref[pl.ds(k, 1), :], 0.0) for k in range(TOP)
     )
-    chains = [
-        ChainGather(a, b, chain_send.at[k], chain_recv.at[k], chain_local.at[k], at, chips)
-        for k, (a, b) in enumerate([(table_ref, table_all), (cot_low_ref, cot_all)])
-    ]
-    for chain in chains:
-        chain.start()
+    chains[0].start()
+    chains += halves
     set_bias(bias_ref, prefix)
     keeps = []
 
@@ -314,12 +337,12 @@
         each_kept(step, lambda made: made.start())
 
     keep(cot_low_ref, cot_low)
+    for chain in ahead:
+        chain.step(1)
     if plane:
         for gather in first:
             gather.second()
-        for gather in later:
-            gather.first()
-        for chain in chains:
+        for chain in behind:
             chain.step(1)
         for step in ("third", "finish"):
             for gather in first:
@@ -331,10 +354,9 @@
             row = [gains_full[pl.ds(64 * n + 32 * k, 1), :].astype(F32) for n in blocks]
             gains_ref[pl.ds(k, 1), :] = jnp.concatenate(row, axis=1)
     else:
-        for chain in chains:
+        for chain in behind:
             chain.step(1)
-        gains_ref[pl.ds(0, 1), :] = one_ref[...].astype(F32)
-        gains_ref[pl.ds(1, 1), :] = two_ref[...].astype(F32)
+        gains_ref[pl.ds(0, 2), :] = gain_pair
     x = x_ref[...]
     inverse = lax.rsqrt(jnp.mean(x * x, axis=-1, keepdims=True) + EPS)
     h1_ref[...] = (x * inverse * gains_ref[pl.ds(0, 1), :]).astype(BF16)
@@ -352,6 +374,8 @@
     pl.loop(2 * width // 256, 3 * width // 256)(lambda block: project(block, False))
     keep(h1_ref, h1_out)
     keep(rot_ref, rot_out)
+    for chain in ahead:
+        chain.step(2)
     lse_ref[...] = jnp.zeros_like(lse_ref)
     count = length // 2
 
@@ -379,11 +403,19 @@
             )
 
     pairs = width // 128
-    pl.loop(0, pairs // 2)(pair)
-    for step in range(2, chips - 1):
-        for chain in chains:
-            chain.step(step)
-    pl.loop(pairs // 2, pairs)(pair)
+
+    @pl.loop(0, pairs)
+    def _(j):
+        pair(j)
+
+        @pl.when(j == pairs // 2 - 1)
+        def _():
+            for step in range(2, chips - 1):
+                for chain in behind:
+                    chain.step(step)
+                for chain in ahead:
+                    chain.step(step + 1)
+
     keep(att_ref, att_out)
     resid = x_ref[...] + dot_nn(att_ref[...], out_full[...])
     resid_ref[...] = resid
@@ -395,21 +427,11 @@
         for chain in chains:
             chain.finish(step)
         keep_chain(step)
-    if plane:
-        for gather in later:
-            gather.second()
-    for chain in chains:
+    for chain in behind:
         chain.step(chips - 1)
-    if plane:
-        for gather in later:
-            gather.third()
     for chain in chains:
         chain.finish(chips - 1)
     keep_chain(chips - 1)
-    if plane:
-        for k, gather in enumerate(later):
-            gather.finish()
-            keep(full[2 + k], full_out[2 + k])
     for chain in chains:
         chain.sent()
     for step in range(chips):
@@ -424,14 +446,13 @@
     chips, plane = group // 2, shards == 4
     cosine, sine = rope_lanes(length)
     vmem, anywhere = pl.BlockSpec(memory_space=pltpu.VMEM), pl.BlockSpec(memory_space=pl.ANY)
-    gains = [v.reshape(1, -1) for v in gains]
     if not plane:
-        gains = [lax.all_gather(v, "shard", axis=1, tiled=True) for v in gains]
+        gains = lax.all_gather(gains, "shard", axis=1, tiled=True)
         weights = [lax.all_gather(v, "shard", axis=0, tiled=True) for v in weights]
-    operands = [prefix, inputs, cotangent, route_rows, weight_rows, cosine, sine, *gains]
-    in_specs = [pl.BlockSpec(memory_space=pltpu.SMEM)] + [vmem] * 8
-    operands += weights if plane else weights[:2]
-    in_specs += [anywhere] * 5 if plane else [vmem] * 2
+    operands = [prefix, inputs, cotangent, route_rows, weight_rows, cosine, sine, gains]
+    in_specs = [pl.BlockSpec(memory_space=pltpu.SMEM)] + [vmem] * 7
+    operands += weights
+    in_specs += [anywhere] * 2 if plane else [vmem] * 2
     shape, dma = jax.ShapeDtypeStruct, pltpu.SemaphoreType.DMA
     out_shape = [
         shape((group, length, width), BF16),
@@ -452,20 +473,20 @@
         pltpu.VMEM((2 * group, length), F32),
         pltpu.VMEM((group, 2 * group, length), F32),
         pltpu.VMEM((group, length, width), BF16),
-        dma((11,)),
+        dma((8,)),
         dma((chips, 2, 2)),
-        dma((2, ChainGather.copies(chips))),
-        dma((2, ChainGather.copies(chips))),
-        dma((2,)),
+        dma((3, ChainGather.copies(chips))),
+        dma((3, ChainGather.copies(chips))),
+        dma((3,)),
     ]
     if plane:
         full = [(shards * v.shape[0], v.shape[1]) for v in weights]
         out_shape += [shape(s, BF16) for s in full]
-        out_specs += [anywhere] * 5
-        part = gains[0].shape[1]
+        out_specs += [anywhere] * 2
+        part = gains.shape[1]
         scratch += [pltpu.VMEM((64, part), BF16), pltpu.VMEM((64 * shards, part), BF16)]
         scratch += [pltpu.VMEM(s, BF16) for s in full]
-        scratch += [dma((6, PlaneGather.COPIES)), dma((6, PlaneGather.COPIES)), dma((6,))]
+        scratch += [dma((3, PlaneGather.COPIES)), dma((3, PlaneGather.COPIES)), dma((3,))]
     outs = pl.pallas_call(
         functools.partial(front_kernel, plane=plane, chips=chips),
         out_shape=out_shape,
@@ -487,8 +508,10 @@
     return table
 
 
-def pick_static(table, step, z):
-    return sum(jnp.where(z == k, row[step], 0) for k, row in enumerate(table))
+def pick(table, step, z):
+    return sum(
+        jnp.where((z == k) & (step == n), chip, 0) for k, row in enumerate(table) for n, chip in enumerate(row)
+    )
 
 
 def gated_block(rows, grad, gate, up, down):
@@ -505,30 +528,34 @@
     return hidden, gate_grad, up_grad, result, back
 
 
-def middle_kernel(*refs, chips, capacity):
+def middle_kernel(*refs, plane, chips, capacity):
     (h2_ref, table_ref, cot_all, gate_hbm, up_hbm, down_hbm), refs = refs[:6], refs[6:]
-    (rows_out, grad_out, hid_out, da_out, db_out, mix_out, back_out), refs = refs[:7], refs[7:]
-    dots_out, refs = refs[0], refs[1:]
+    shared, refs = (refs[:3], refs[3:]) if plane else ([], refs)
+    (rows_out, grad_out, hid_out, da_out, db_out, mix_out, back_out, dots_out), refs = refs[:8], refs[8:]
+    shared_out, refs = (refs[:3], refs[3:]) if plane else ([], refs)
     (gate_w, up_w, down_w, h2_all, cot_buf, rows_ref, grad_ref, cotr_ref, scale_ref), refs = refs[:9], refs[9:]
     (y_acc, r_acc, stage_f, stage_s, stage_t, got, total), refs = refs[:7], refs[7:]
-    w_sem, cot_sem, row_sem, f_sem, tot_sem, core_send, core_recv, chain_send, chain_recv, chain_local = refs
+    (w_sem, cot_sem, row_sem, f_sem, tot_sem, core_send, core_recv, chain_send, chain_recv, chain_local), refs = refs[:10], refs[10:]
     length, width = h2_ref.shape
     experts = 2 * chips
-    hidden_width = gate_w.shape[1]
     unit = stage_f.shape[-1]
-    units = hidden_width // unit
+    units = gate_w.shape[1] // unit
     at = place()
     me, core, z = at["expert"], at["core"], at["z"]
     order = near_order(chips)
-    chain_meet(at, chips, [at["dev_c"]])
-    chain = ChainGather(h2_ref, h2_all, chain_send, chain_recv, chain_local, at, chips)
-    chain.start()
+    gathers = []
+    if plane:
+        full, (send, recv, local, full_sem) = refs[:3], refs[3:]
+        gathers = [
+            PlaneGather(a, b, send.at[k], recv.at[k], local.at[k], at) for k, (a, b) in enumerate(zip(shared, full))
+        ]
+        for gather in gathers:
+            gather.load()
+        keeps = [pltpu.make_async_copy(a, b, full_sem.at[k]) for k, (a, b) in enumerate(zip(full, shared_out))]
 
     def load_cot(step):
-        chip = pick_static(order, step, z)
-        return pltpu.make_async_copy(
-            cot_all.at[pl.ds(2 * chip, 2)], cot_buf.at[step % 2], cot_sem.at[step % 2]
-        )
+        chip = pick(order, step, z)
+        return pltpu.make_async_copy(cot_all.at[pl.ds(2 * chip, 2)], cot_buf, cot_sem)
 
     load_cot(0).start()
     loads = [
@@ -537,6 +564,18 @@
     ]
     for load in loads:
         load.start()
+    chain_meet(at, chips, [at["dev_x"], at["dev_y"], at["dev_c"]] if plane else [at["dev_c"]])
+    chains = [
+        ChainGather(
+            h2_ref, h2_all, chain_send.at[k], chain_recv.at[k], chain_local.at[k], at, chips,
+            pl.ds(k * length // 2, length // 2),
+        )
+        for k in range(2)
+    ]
+    for chain in chains:
+        chain.start()
+    for gather in gathers:
+        gather.first()
 
     def one_hot(source):
         slots = table_ref[source, pl.ds(me, 1), :]
@@ -548,10 +587,10 @@
             pltpu.make_async_copy(grad_ref, grad_out.at[step], row_sem.at[1]),
         ]
 
-    def hidden_copies(step, k, slot):
+    def hidden_copies(step, k):
         return [
             pltpu.make_async_copy(
-                stage_f.at[slot, n], out.at[step, :, columns(k * unit, unit)], f_sem.at[slot, n]
+                stage_f.at[k % 2, n], out.at[step, :, columns(k * unit, unit)], f_sem.at[k % 2, n]
             )
             for n, out in enumerate([hid_out, da_out, db_out])
         ]
@@ -565,83 +604,82 @@
         ]
 
     def total_copies(step):
-        chip = pick_static(order, step, z)
+        chip = pick(order, step, z)
         return [
             pltpu.make_async_copy(total.at[n], out.at[chip], tot_sem.at[n])
             for n, out in enumerate([mix_out, back_out])
         ]
 
+    def each(copies, act):
+        for copy in copies:
+            getattr(copy, act)()
+
     def join(step):
-        if step > 0:
-            for copy in total_copies(step - 1):
-                copy.wait()
+        pl.when(step > 0)(lambda: each(total_copies(step - 1), "wait"))
         for n, (copy, stage) in enumerate(zip(core_copies(step), [stage_s, stage_t])):
             copy.wait()
             total[n] = (stage[core].astype(F32) + got[n, step].astype(F32)).astype(BF16)
-        for copy in total_copies(step):
-            copy.start()
-
-    def expert_rows(step):
-        chip = pick_static(order, step, z)
-        slot = step % 2
+        each(total_copies(step), "start")
+
+    @pl.loop(0, chips)
+    def _(step):
+        for k in range(chips):
+
+            @pl.when(step == k)
+            def _():
+                for chain in chains:
+                    chain.finish(k)
+                if k == 0:
+                    each(loads, "wait")
+                for gather in gathers:
+                    if k == 1:
+                        gather.second()
+                    if k == 2:
+                        gather.third()
+                    if k == 3:
+                        gather.finish()
+                if plane and k == 3:
+                    each(keeps, "start")
+
+        chip = pick(order, step, z)
         load_cot(step).wait()
-        if step + 1 < chips:
-            load_cot(step + 1).start()
-        if step > 0:
-            for copy in row_copies(step - 1):
-                copy.wait()
+        pl.when(step > 0)(lambda: each(row_copies(step - 1), "wait"))
         for d in range(2):
             source, part = 2 * chip + d, pl.ds(d * capacity, capacity)
             chosen = one_hot(source)
             select = chosen.astype(F32).astype(BF16)
             rows_ref[part, :] = dot_nn(select, h2_all[source]).astype(BF16)
-            cot_rows = dot_nn(select, cot_buf[slot, d])
+            cot_rows = dot_nn(select, cot_buf[d])
             scale = jnp.sum(
                 jnp.where(chosen, table_ref[source, pl.ds(experts + me, 1), :], 0.0), axis=1, keepdims=True
             )
             grad_ref[part, :] = (cot_rows * scale).astype(BF16)
             cotr_ref[part, :] = cot_rows.astype(BF16)
             scale_ref[part, :] = scale
-        for copy in row_copies(step):
-            copy.start()
+        pl.when(step + 1 < chips)(lambda: load_cot(step + 1).start())
+        each(row_copies(step), "start")
         y_acc[...] = jnp.zeros_like(y_acc)
         r_acc[...] = jnp.zeros_like(r_acc)
-        if step == 0:
-            for load in loads:
-                load.wait()
-
-        def one_unit(k):
+
+        @pl.loop(0, units)
+        def _(k):
             cols = columns(k * unit, unit)
             hidden, gate_grad, up_grad, result, back = gated_block(
                 rows_ref[...], grad_ref[...], gate_w[:, cols], up_w[:, cols],
                 down_w[pl.ds(pl.multiple_of(k * unit, unit), unit), :],
             )
-            turn = k % 2
-
-            def settle():
-                for copy in hidden_copies(step, k, turn):
-                    copy.wait()
-
-            if step == 0:
-                pl.when(k >= 2)(settle)
-            else:
-                settle()
-            stage_f[turn, 0] = hidden
-            stage_f[turn, 1] = gate_grad
-            stage_f[turn, 2] = up_grad
-            for copy in hidden_copies(step, k, turn):
-                copy.start()
+            pl.when((step > 0) | (k >= 2))(lambda: each(hidden_copies(step, k), "wait"))
+            stage_f[k % 2, 0] = hidden
+            stage_f[k % 2, 1] = gate_grad
+            stage_f[k % 2, 2] = up_grad
+            each(hidden_copies(step, k), "start")
             y_acc[...] += result
             r_acc[...] += back
-
-        if step + 1 < chips:
-            pl.loop(0, units - 1)(one_unit)
-            chain.step(step + 1)
-            pl.loop(units - 1, units)(one_unit)
-        else:
-            pl.loop(0, units)(one_unit)
-        if step > 0:
-            join(step - 1)
+            for n in range(chips - 1):
+                for event, chain in zip((max(0, units - 4), units - 2), chains):
+                    pl.when((step == n) & (k == event))(lambda: chain.step(n + 1))
+
+        pl.when(step > 0)(lambda: join(step - 1))
         result = y_acc[...].astype(BF16).astype(F32)
         dots = jnp.sum(result * cotr_ref[...].astype(F32), axis=1, keepdims=True)
         weighted = (result * scale_ref[...]).astype(BF16)
@@ -654,27 +692,23 @@
             stage_s[d] = dot_tn(select, weighted[part]).astype(BF16)
             stage_t[d] = dot_tn(select, back[part]).astype(BF16)
             dots_out[source] = jnp.sum(jnp.where(chosen, dots[part], 0.0), axis=0, keepdims=True)
-        for copy in core_copies(step):
-            copy.start()
-
-    for step in range(chips):
-        chain.finish(step)
-        expert_rows(step)
+        each(core_copies(step), "start")
+
     join(chips - 1)
-    for copy in total_copies(chips - 1):
-        copy.wait()
-    for copy in row_copies(chips - 1):
-        copy.wait()
+    each(total_copies(chips - 1), "wait")
+    each(row_copies(chips - 1), "wait")
     for k in range(max(0, units - 2), units):
-        for copy in hidden_copies(chips - 1, k, k % 2):
-            copy.wait()
-    chain.sent()
-
-
-def middle(h2, table_all, cot_all, expert_weights, ident):
+        each(hidden_copies(chips - 1, k), "wait")
+    for chain in chains:
+        chain.sent()
+    if plane:
+        each(keeps, "wait")
+
+
+def middle(h2, table_all, cot_all, expert_weights, shared, ident):
     length, width = h2.shape
-    group = lax.axis_size("expert")
-    chips = group // 2
+    group, shards = lax.axis_size("expert"), lax.axis_size("shard")
+    chips, plane = group // 2, shards == 4
     capacity = 4 * length // group
     hidden_width = expert_weights[0].shape[2]
     unit = min(512, hidden_width)
@@ -697,7 +731,7 @@
         pltpu.VMEM((width, hidden_width), BF16),
         pltpu.VMEM((hidden_width, width), BF16),
         pltpu.VMEM((group, length, width), BF16),
-        pltpu.VMEM((2, 2, length, width), BF16),
+        pltpu.VMEM((2, length, width), BF16),
         pltpu.VMEM((both, width), BF16),
         pltpu.VMEM((both, width), BF16),
         pltpu.VMEM((both, width), BF16),
@@ -710,26 +744,38 @@
         pltpu.VMEM((2, chips, length, width), BF16),
         pltpu.VMEM((2, length, width), BF16),
         dma((3,)),
-        dma((2,)),
+        dma,
         dma((2,)),
         dma((2, 3)),
         dma((2,)),
         dma((2, chips)),
         dma((2, chips)),
-        dma((ChainGather.copies(chips),)),
-        dma((ChainGather.copies(chips),)),
-        dma,
+        dma((2, ChainGather.copies(chips))),
+        dma((2, ChainGather.copies(chips))),
+        dma((2,)),
     ]
-    return pl.pallas_call(
-        functools.partial(middle_kernel, chips=chips, capacity=capacity),
+    operands = [h2, table_all, cot_all, *expert_weights]
+    in_specs = [vmem] * 2 + [anywhere] * 4
+    out_specs = [anywhere] * 7 + [vmem]
+    if plane:
+        operands += shared
+        in_specs += [anywhere] * 3
+        full = [(shards * v.shape[0], v.shape[1]) for v in shared]
+        out_shape += [shape(s, BF16) for s in full]
+        out_specs += [anywhere] * 3
+        scratch += [pltpu.VMEM(s, BF16) for s in full]
+        scratch += [dma((3, PlaneGather.COPIES)), dma((3, PlaneGather.COPIES)), dma((3,)), dma((3,))]
+    outs = pl.pallas_call(
+        functools.partial(middle_kernel, plane=plane, chips=chips, capacity=capacity),
         out_shape=out_shape,
-        in_specs=[vmem] * 2 + [anywhere] * 4,
-        out_specs=[anywhere] * 7 + [vmem],
+        in_specs=in_specs,
+        out_specs=out_specs,
         scratch_shapes=scratch,
         compiler_params=pltpu.CompilerParams(
             collective_id=ident, has_side_effects=True, vmem_limit_bytes=VMEM_BYTES
         ),
-    )(h2, table_all, cot_all, *expert_weights)
+    )(*operands)
+    return outs if plane else [*outs, *[lax.all_gather(v, "shard", axis=0, tiled=True) for v in shared]]
 
 
 class ChainReduce:
@@ -868,7 +914,8 @@
     (dots_ref, route_ref, rows_hbm, grad_hbm, h2_hbm, cot_hbm, hid_hbm, da_hbm, db_hbm, back_hbm), refs = refs[:10], refs[10:]
     (sg_hbm, su_hbm, sd_hbm), refs = refs[:3], refs[3:]
     (down_out, sown, sgot, refs) = refs[0], refs[1:4], refs[4:7], refs[7:]
-    (gate_out, up_out, sum_ref, sy_ref, chosen_ref), refs = refs[:5], refs[5:]
+    grads_out, refs = (refs[:2], refs[2:]) if plane else (refs[:1], refs[1:])
+    (sum_ref, sy_ref, chosen_ref), refs = refs[:3], refs[3:]
     (rows_ref, grad_ref, h2_ref, cot_ref, down_blocks, in_sem, down_sem), refs = refs[:7], refs[7:]
     (sg_w, su_w, sd_w, sgg_s, sug_s, sdg_s, s_sem, sg_sem, sg_send, sg_recv), refs = refs[:10], refs[10:]
     (chunk, own, from_left, from_right, dots_got), refs = refs[:5], refs[5:]
@@ -889,14 +936,12 @@
         made.start()
     peers = [(lax.rem(me + k, group), at["shard"]) for k in range(1, group)]
     meet(peers + ([at["dev_x"], at["dev_y"]] if plane else []))
+    wide = grads_out[0]
     if plane:
-        send, recv, *work = refs
+        wide, send, recv, *work = refs
         reduces = [
-            PlaneReduce(work[4 * k], *work[4 * k + 1 : 4 * k + 4], send.at[k], recv.at[k], at) for k in range(2)
+            PlaneReduce(wide.at[n], *work[3 * n : 3 * n + 3], send.at[n], recv.at[n], at) for n in range(2)
         ]
-        targets = [work[0], work[4], down_blocks]
-    else:
-        targets = [gate_out, up_out, down_blocks]
     sources = [da_hbm, db_hbm, hid_hbm]
     dots = [
         remote(dots_ref.at[peer[0]], dots_got.at[me], dots_send.at[k], dots_recv.at[k], peer)
@@ -904,27 +949,15 @@
     ]
 
     def fetch(array, index):
-        shard = plane_blocks(at, index, plane)
+        shard = plane_blocks(at, index % shards, plane)
         slot = index % 2
         return pltpu.make_async_copy(
             sources[array].at[:, columns(shard * block, block)], chunk.at[slot], chunk_sem.at[slot]
         )
 
-    def make(array, low, high):
-        @pl.loop(low, high)
-        def _(index):
-            fetch(array, index).wait()
-            pl.when(index + 1 < shards)(lambda: fetch(array, index + 1).start())
-            if array < 2:
-                pl.when(index + 1 == shards)(lambda: fetch(array + 1, 0).start())
-            shard = plane_blocks(at, index, plane)
-            held = chunk[index % 2]
-            if array < 2:
-                targets[array][shard] = dot_tn(rows_ref[...], held).astype(BF16)
-                if plane:
-                    reduces[array].first_of(index)
-            else:
-                targets[array][shard] = dot_tn(held, grad_ref[...]).astype(BF16)
+    def fetch_next(index):
+        for array in range(3):
+            pl.when(index // shards == array)(lambda: fetch(array, index).start())
 
     def load_shared(k, slot):
         return [
@@ -987,25 +1020,43 @@
     for made in dots:
         made.start()
     dots_got[me] = dots_ref[me]
-    for made in inputs[:1]:
-        made.wait()
-    make(0, 0, shards)
-    make(1, 0, shards // 2)
-    for step in range(1, chips - 2):
-        chain.tick(step)
-    make(1, shards // 2, shards)
+    inputs[0].wait()
+
+    @pl.loop(0, 2 * shards)
+    def _(index):
+        fetch(0, index).wait()
+        fetch_next(index + 1)
+        array = index // shards
+        wide[array, plane_blocks(at, index % shards, plane)] = dot_tn(rows_ref[...], chunk[index % 2]).astype(BF16)
+        for n in range(2 if plane else 0):
+            pl.when(array == n)(lambda: reduces[n].first_of(index % shards))
+
+        @pl.when(index == 2 * shards - 3)
+        def _():
+            for step in range(1, chips - 2):
+                chain.tick(step)
+
     for made in inputs[1:]:
         made.wait()
-    make(2, 0, shards)
+
+    @pl.loop(2 * shards, 3 * shards)
+    def _(index):
+        fetch(2, index).wait()
+        pl.when(index + 1 < 3 * shards)(lambda: fetch_next(index + 1))
+        down_blocks[plane_blocks(at, index % shards, plane)] = dot_tn(chunk[index % 2], grad_ref[...]).astype(BF16)
+
     store_down = pltpu.make_async_copy(down_blocks, down_out, down_sem)
     store_down.start()
     chain.tick(chips - 2)
     if plane:
         reduces[0].second()
-    pl.loop(0, shards // 2)(shared_block)
-    if plane:
-        reduces[1].second()
-    pl.loop(shards // 2, shards)(shared_block)
+
+    @pl.loop(0, shards)
+    def _(index):
+        shared_block(index)
+        if plane:
+            pl.when(index == shards // 2 - 1)(reduces[1].second)
+
     for made in dots:
         made.wait()
     for k in range(TOP):
@@ -1014,7 +1065,7 @@
         )
     if plane:
         for turn in range(2):
-            gate_out[pl.ds(turn * reduces[0].half, reduces[0].half), :] = reduces[0].value(turn)
+            grads_out[0][pl.ds(turn * reduces[0].half, reduces[0].half), :] = reduces[0].value(turn)
     sum_ref[...] += chain.value()
     chain.sent()
     shared_settle(shards - 1)
@@ -1026,7 +1077,7 @@
 
     if plane:
         for turn in range(2):
-            up_out[pl.ds(turn * reduces[1].half, reduces[1].half), :] = reduces[1].value(turn)
+            grads_out[1][pl.ds(turn * reduces[1].half, reduces[1].half), :] = reduces[1].value(turn)
         for reduce in reduces:
             reduce.sent()
     store_down.wait()
@@ -1066,10 +1117,10 @@
     scratch += [dma, dma((2,)), dma((2 * chips - 1,)), dma((2 * chips - 1,)), dma((2 * chips,)), dma((2 * chips,))]
     if plane:
         out_shape = [shape((width, block), F32)] * 2
-        scratch += [dma((2, PlaneReduce.COPIES))] * 2
-        scratch += ([pltpu.VMEM(wide, BF16)] + PlaneReduce.scratch(wide)) * 2
+        scratch += [pltpu.VMEM((2,) + wide, BF16)] + [dma((2, PlaneReduce.COPIES))] * 2
+        scratch += PlaneReduce.scratch(wide) * 2
     else:
-        out_shape = [shape(wide, BF16)] * 2
+        out_shape = [shape((2,) + wide, BF16)]
     halves = [shape((shards, width // 2, part), BF16)] * 2 + [shape((shards, part // 2, width), BF16)]
     out_shape = [shape((shards, block, width), BF16), *halves, *halves, *out_shape]
     out_shape += [shape((length, width), F32)] * 2 + [shape((TOP, length), F32)]
@@ -1077,7 +1128,7 @@
         functools.partial(weights_kernel, plane=plane, chips=chips, shards=shards),
         out_shape=out_shape,
         in_specs=[vmem] * 2 + [anywhere] * 11,
-        out_specs=[anywhere] * 7 + [vmem] * 5,
+        out_specs=[anywhere] * 7 + [vmem] * (len(out_shape) - 7),
         scratch_shapes=scratch,
         compiler_params=pltpu.CompilerParams(
             collective_id=ident, has_side_effects=True, vmem_limit_bytes=VMEM_BYTES
@@ -1095,12 +1146,13 @@
 
 
 def rear_kernel(*refs, plane, chips, shards):
-    (prefix, gains_ref, cos_ref, sin_ref), sources, refs = refs[:4], refs[4:15], refs[15:]
+    (prefix, gains_ref, cos_ref, sin_ref), sources, refs = refs[:4], refs[4:16], refs[16:]
     halves, refs = (refs[:6], refs[6:]) if plane else ([], refs)
     (mix_out, input_grad_out, qkv_grad_out, gain_out), refs = refs[:4], refs[4:]
     pieces, refs = (refs[:4], refs[4:]) if plane else (refs[:1], refs[1:])
     held, refs = refs[:11], refs[11:]
     own, resid_ref, dh_ref, cot_ref, out_ref, att_ref, rot_ref, lse_ref, h1_ref, qkv_ref, x_ref = held
+    held = [*held, cot_ref]
     (bias_ref, dres_ref, datt_ref, dqkv_ref, qkv_grad_ref, out_grad_ref, from_left, from_right), refs = refs[:8], refs[8:]
     (load_sem, store_sem, chain_send, chain_recv), refs = refs[:4], refs[4:]
     length, width = x_ref.shape
@@ -1131,7 +1183,7 @@
             )
             for k in range(shards)
         ]
-    for made in loads[1:]:
+    for made in loads[1:11]:
         made.start()
     chain_meet(at, chips, [at["dev_x"], at["dev_y"], at["dev_c"]] if plane else [])
     chain = ChainReduce(own, from_left, from_right, chain_send, chain_recv, at, chips)
@@ -1144,6 +1196,7 @@
     gain_two_grad, extra = norm_back(resid, inverse, gains_ref[pl.ds(1, 1), :], dh_ref[...])
     dres = cot_ref[...] + extra
     dres_ref[...] = dres
+    loads[11].start()
     low_dres = dres.astype(BF16)
     out_grad = dot_tn(att_ref[...], low_dres).astype(BF16)
     rows = width // shards
@@ -1177,7 +1230,7 @@
     datt_ref[...] = dot_nt(low_dres, out_ref[...]).astype(BF16)
     set_bias(bias_ref, prefix)
     scale = HEAD_DIM**-0.5
-    for made in loads[6:]:
+    for made in loads[6:11]:
         made.wait()
 
     block = length // 2
@@ -1222,10 +1275,16 @@
             keep(1 + part, pl.ds(block, block), sums[1][part][block:])
 
     pairs = width // 128
-    pl.loop(0, pairs // 3)(pair)
-    for step in range(1, chips - 2):
-        chain.tick(step)
-    pl.loop(pairs // 3, pairs)(pair)
+
+    @pl.loop(0, pairs)
+    def _(j):
+        pair(j)
+
+        @pl.when(j == pairs // 3 - 1)
+        def _():
+            for step in range(1, chips - 2):
+                chain.tick(step)
+
 
     @pl.loop(0, 3 * width // 256)
     def _(k):
@@ -1254,7 +1313,8 @@
         for k in range(chips):
             piece[k] = both[k * count : (k + 1) * count].astype(BF16)
         reduce.sent()
-    resid_ref[...] = chain.value()
+    loads[11].wait()
+    resid_ref[...] += cot_ref[...] + chain.value()
     stores.append(pltpu.make_async_copy(resid_ref, mix_out, store_sem.at[2]))
     stores[2].start()
     chain.sent()
@@ -1264,7 +1324,7 @@
         made.wait()
 
 
-def rear(prefix, inputs, cotangent, resid, dh2, gains, kept, full, mix_part, halves, ident):
+def rear(prefix, inputs, cotangent, resid, dh2, shared_out, gains, kept, full, mix_part, halves, ident):
     length, width = inputs.shape
     chips, shards = mix_part.shape[0], lax.axis_size("shard")
     plane = shards == 4
@@ -1273,8 +1333,9 @@
     vmem, anywhere = pl.BlockSpec(memory_space=pltpu.VMEM), pl.BlockSpec(memory_space=pl.ANY)
     shape, dma = jax.ShapeDtypeStruct, pltpu.SemaphoreType.DMA
     sources = [mix_part, resid, dh2, cotangent, full[1], attended, turned, logsum, normed_one, full[0], inputs]
+    sources.append(shared_out)
     operands = [prefix, gains, cosine, sine, *sources]
-    in_specs = [pl.BlockSpec(memory_space=pltpu.SMEM)] + [vmem] * 3 + [anywhere] * 11
+    in_specs = [pl.BlockSpec(memory_space=pltpu.SMEM)] + [vmem] * 3 + [anywhere] * 12
     out_blocks = (shards, width // shards, width)
     out_shape = [
         shape((length, width), F32),
@@ -1283,7 +1344,7 @@
         shape((shards, 64, width), BF16),
     ]
     out_specs = [anywhere] * 3 + [vmem]
-    scratch = [pltpu.VMEM(v.shape, v.dtype) for v in sources]
+    scratch = [pltpu.VMEM(v.shape, v.dtype) for v in sources[:11]]
     scratch += [
         pltpu.VMEM((length, length), F32),
         pltpu.VMEM((length, width), F32),
@@ -1292,7 +1353,7 @@
         pltpu.VMEM((width, 3 * width), BF16),
         pltpu.VMEM(out_blocks, BF16),
         *ChainReduce.scratch((chips, length, width))[:2],
-        dma((11,)),
+        dma((12,)),
         dma((4,)),
         dma((2 * chips,)),
         dma((2 * chips,)),
@@ -1390,18 +1451,18 @@
     for k in attn:
         planes[1 + k].second()
     planes[0].first()
-    total(shared)
-    step_all(shared, 1)
     for k in attn:
         count = chain_work[k][0].shape[1]
         both = jnp.concatenate([planes[1 + k].value(0), planes[1 + k].value(1)], axis=0)
         for n in range(chips):
             sums[k].own[n] = both[n * count : (n + 1) * count].astype(BF16)
-    for step in range(chips - 1):
+    tick(attn, 0)
+    total(shared)
+    for step in range(1, chips - 1):
         tick(attn, step)
-        if step:
-            step_all(shared, step + 1)
+        step_all(shared, step)
     total(attn)
+    step_all(shared, chips - 1)
     planes[0].second()
     for step in range(1, chips):
         step_all(attn, step)
@@ -1458,10 +1519,10 @@
 
 
 def finish_kernel(*refs, chips, counts):
-    total, results = sum(counts), sum(counts[:2]) + 1
-    inputs, outputs, refs = refs[:total], refs[total : total + results], refs[total + results :]
+    total = sum(counts)
+    inputs, outputs, refs = refs[:total], refs[total : 2 * total], refs[2 * total :]
     held, made, (load_sem, store_sem) = refs[:total], refs[total:-2], refs[-2:]
-    plain, sums = counts[:2]
+    plain, sums = counts
     loads = [pltpu.make_async_copy(a, b, load_sem.at[k]) for k, (a, b) in enumerate(zip(inputs, held))]
     ready = [*held[:plain], *made]
     stores = [
@@ -1475,34 +1536,32 @@
     for k in range(plain, plain + sums):
         loads[k].wait()
         count = held[k].shape[1]
-        if ready[k].shape[0] == count:
-            ready[k][...] = held[k][0].astype(F32)
+        if k == plain:
+            part, shard = ready[k].shape[1], lax.axis_index("shard")
+            rows = held[k][0].astype(F32)
+            ready[k][...] = sum(
+                jnp.where(shard == n, rows[:, n * part : (n + 1) * part], 0.0) for n in range(rows.shape[1] // part)
+            )
         else:
             for n in range(chips):
                 for c in range(2):
                     ready[k][pl.ds((c * chips + n) * count, count), :] = held[k][2 * n + c].astype(F32)
         stores[k].start()
-    for copy in loads[plain + sums :]:
-        copy.wait()
-    ready[-1][...] = sum(v[...] for v in held[plain + sums :])
-    for copy in stores[plain + sums :]:
-        copy.start()
     for copy in stores:
         copy.wait()
 
 
-def finish(plain, sums, summands):
+def finish(plain, sums):
     chips = sums[0].shape[0] // 2
     shape, dma = jax.ShapeDtypeStruct, pltpu.SemaphoreType.DMA
     anywhere = pl.BlockSpec(memory_space=pl.ANY)
-    inputs = [*plain, *sums, *summands]
-    made = [shape(sums[0].shape[1:], F32)]
+    inputs = [*plain, *sums]
+    made = [shape((sums[0].shape[1], sums[0].shape[2] // lax.axis_size("shard")), F32)]
     made += [shape((v.shape[0] * v.shape[1], v.shape[2]), F32) for v in sums[1:]]
-    made.append(shape(summands[0].shape, F32))
     out_shape = [shape(v.shape, F32) for v in plain] + made
     scratch = [pltpu.VMEM(v.shape, v.dtype) for v in inputs] + [pltpu.VMEM(s.shape, F32) for s in made]
     return pl.pallas_call(
-        functools.partial(finish_kernel, chips=chips, counts=(len(plain), len(sums), len(summands))),
+        functools.partial(finish_kernel, chips=chips, counts=(len(plain), len(sums))),
         out_shape=out_shape,
         in_specs=[anywhere] * len(inputs),
         out_specs=[anywhere] * len(out_shape),
@@ -1545,17 +1604,14 @@
         gains,
         qkv_full,
         out_full,
-        gate_blocks,
-        up_blocks,
-        down_full,
     ) = front(
         prefix,
         inputs,
         cotangent,
         route_rows,
         gate_weights.T,
-        [norm_one, norm_two],
-        [qkv_weight, out_weight, shared_gate, shared_up, shared_down],
+        jnp.stack([norm_one, norm_two]),
+        [qkv_weight, out_weight],
         1,
     )
     (
@@ -1567,11 +1623,19 @@
         mix_part,
         back_part,
         weight_back,
-    ) = middle(normed_two, table_all, cot_all, [expert_gate, expert_up, expert_down], 2)
+        *shared_full,
+    ) = middle(
+        normed_two,
+        table_all,
+        cot_all,
+        [expert_gate, expert_up, expert_down],
+        [shared_gate, shared_up, shared_down],
+        2,
+    )
     rows, grad_rows, hidden, gate_pre_grad, up_pre_grad = (
         v.reshape(-1, v.shape[-1]) for v in (rows, grad_rows, hidden, gate_pre_grad, up_pre_grad)
     )
-    down_term, *shared_halves, gate_term, up_term, normed_two_grad, shared_out, gate_weights_grad = weights(
+    down_term, *shared_halves, normed_two_grad, shared_out, gate_weights_grad = weights(
         weight_back,
         route_rows,
         rows,
@@ -1582,16 +1646,18 @@
         gate_pre_grad,
         up_pre_grad,
         back_part,
-        [gate_blocks, up_blocks, down_full],
+        shared_full,
         3,
     )
+    gate_up = shared_halves[6:]
     shared_halves = [shared_halves[k + n] for k in range(3) for n in (0, 3)]
-    mixture, input_grad, qkv_grad, gain_grads, *pieces = rear(
+    output, input_grad, qkv_grad, gain_grads, *pieces = rear(
         prefix,
         inputs,
         cotangent,
         resid,
         normed_two_grad,
+        shared_out,
         gains,
         [turned, attended, normed_one, logsum],
         [qkv_full, out_full],
@@ -1602,8 +1668,9 @@
     qkv_grad = qkv_grad.reshape(shards, width // shards, 3 * width)
     if shards == 4:
         qkv_sum, gain_sums, *pieces, down_term = last(qkv_grad, gain_grads, pieces, down_term, 5)
-        input_grad, gate_term, up_term, down_term, gain_sums, qkv_sum, *shared_sums, out_sum, output = finish(
-            [input_grad, gate_term, up_term, down_term], [gain_sums, qkv_sum, *pieces], [resid, mixture, shared_out]
+        gate_term, up_term = gate_up
+        output, input_grad, gate_term, up_term, down_term, gain_sums, qkv_sum, *shared_sums, out_sum = finish(
+            [output, input_grad, gate_term, up_term, down_term], [gain_sums, qkv_sum, *pieces]
         )
     else:
 
@@ -1613,18 +1680,17 @@
         def over_all(value):
             return lax.psum(over_plane(value), "expert").astype(F32)
 
-        output = resid + mixture + shared_out
         gate_term, up_term, down_term = (
-            over_plane(v).astype(F32) for v in (gate_term, up_term, down_term)
+            over_plane(v).astype(F32) for v in (*gate_up[0], down_term)
         )
         qkv_sum, gain_sums, out_sum = over_all(qkv_grad), over_all(gain_grads), over_all(pieces[0])
+        part = width // shards
+        gain_sums = lax.dynamic_slice(gain_sums, (0, shard * part), (gain_sums.shape[0], part))
         shared_sums = []
         for own, got in zip(shared_halves[::2], shared_halves[1::2]):
             half = (own.astype(F32) + got.astype(F32)).astype(BF16)
             both = jnp.concatenate([jnp.where(me % 2 == c, half, 0) for c in range(2)], axis=1)
             shared_sums.append(over_all(both))
-    part = width // shards
-    gain_sums = lax.dynamic_slice(gain_sums[:2], (0, shard * part), (2, part))
     return (
         output,
         input_grad,

time: 369 us -> 361 us (0.978); the launches traced: 365 us -> 361 us
    pallas_call x1, Pallas kernels: 70.9 us -> 66 us  [front(): pl.pallas_call(functools.partial(front_kernel, plane=plane, chips=chips),...]
where the time goes in v6:
time: 361 us
  Pallas kernels  355 us (98%)
    pallas_call x1, Pallas kernels, middle(): pl.pallas_call(functools.partial(middle_kernel, plane=plane, chips=chips,...  87.4 us
    pallas_call x1, Pallas kernels, front(): pl.pallas_call(functools.partial(front_kernel, plane=plane, chips=chips),...  66 us
    pallas_call x1, Pallas kernels, weights(): pl.pallas_call(functools.partial(weights_kernel, plane=plane, chips=chips...  65.4 us
    pallas_call x1, Pallas kernels, last(): pl.pallas_call(functools.partial(last_kernel, chips=chips, shards=shards)...  65.3 us
    pallas_call x1, Pallas kernels, rear(): pl.pallas_call(functools.partial(rear_kernel, plane=plane, chips=chips, s...  62.4 us
    pallas_call x1, Pallas kernels, finish(): pl.pallas_call(functools.partial(finish_kernel, chips=chips, counts=(len(...  8.97 us

profile of v6, /device:TPU:0, one launch (start us, length us, event | category | flops | bytes accessed | tf_op | source)
XLA Modules:
  0.0 360.7 jit_solution(8035940954622486999)
XLA Ops:
  1.3 0.7 stack.9
  2.0 0.7 stack.10
  2.6 0.6 pad_maximum_fusion.refs_7_
  3.2 66.0 %shard_map.282 = (bf16[8,512,768]{2,1,0:T(8,128)(2,1)}, f32[8,16,512]{2,1,0:T(8,128)}, bf16[512,768]{1,0:T(8,128)(2,1)}, bf16[512,2304]{1,0:T(8,128)(2,1)}, bf16...) custom-call(s32[1]{0:T(128)S(6)} %copy.33.refs_0_, ...), custom_call_target="tpu_custom_call" | custom-call | tf_op jit(solution)/shard_map/pallas_call | solution.py:490
  69.2 87.4 %shard_map.283 = (bf16[4,512,768]{2,1,0:T(8,128)(2,1)}, bf16[4,512,768]{2,1,0:T(8,128)(2,1)}, bf16[4,512,2048]{2,1,0:T(8,128)(2,1)}, bf16[4,512,2048]{2,1,0:T(8,...) custom-call(bf16[512,768]{1,0:T(8,128)(2,1)} %get-tuple-element.75.r, ...), custom_call_target="tpu_custom_call" | custom-call | tf_op jit(solution)/shard_map/pallas_call | solution.py:768
  156.6 65.4 %shard_map.284 = (bf16[4,512,768]{2,1,0:T(8,128)(2,1)}, bf16[4,384,512]{2,1,0:T(8,128)(2,1)}, bf16[4,384,512]{2,1,0:T(8,128)(2,1)}, bf16[4,256,768]{2,1,0:T(8,12...) custom-call(f32[8,1,512]{2,1,0:T(1,128)} %get-tuple-element.80.refs_, ...), custom_call_target="tpu_custom_call" | custom-call | tf_op jit(solution)/shard_map/pallas_call | solution.py:1127
  222.0 62.4 %shard_map.285 = (f32[512,768]{1,0:T(8,128)}, f32[512,768]{1,0:T(8,128)}, bf16[768,2304]{1,0:T(8,128)(2,1)}, bf16[4,64,768]{2,1,0:T(8,128)(2,1)}, bf16[4,96,512]...) custom-call(s32[1]{0:T(128)S(6)} %copy.33.refs_0_, ...), custom_call_target="tpu_custom_call" | custom-call | tf_op jit(solution)/shard_map/pallas_call | solution.py:1373
  284.4 65.3 %shard_map.286 = (bf16[8,24,2304]{2,1,0:T(8,128)(2,1)}, bf16[8,8,768]{2,1,0:T(8,128)(2,1)}, bf16[8,96,512]{2,1,0:T(8,128)(2,1)}, bf16[8,96,512]{2,1,0:T(8,128)(2...) custom-call(bf16[4,192,2304]{2,1,0:T(8,128)(2,1)} %bitcast.17, ...), custom_call_target="tpu_custom_call" | custom-call | tf_op jit(solution)/shard_map/pallas_call | solution.py:1509
  349.7 0.0 copy-start
  349.7 9.0 %shard_map.287 = (f32[512,768]{1,0:T(8,128)}, f32[512,768]{1,0:T(8,128)}, f32[768,512]{1,0:T(8,128)}, f32[768,512]{1,0:T(8,128)}, f32[512,768]{1,0:T(8,128)}, /*...) custom-call(f32[512,768]{1,0:T(8,128)} %get-tuple-element.105.refs_0, ...), custom_call_target="tpu_custom_call" | custom-call | tf_op jit(solution)/shard_map/pallas_call | solution.py:1563
  358.7 1.3 fusion
  360.1 0.0 copy-done
  360.1 0.6 copy.34
Async XLA Ops:
  349.7 10.3 %copy-start = (f32[2,512]{1,0:T(2,128)S(1)}, f32[2,512]{1,0:T(2,128)}, u32[]{:S(2)}) copy-start(f32[2,512]{1,0:T(2,128)} %get-tuple-element.134) | copy-start | bytes 12292
